TPU v7x, 128 devices: a whole 4x4x4 slice. The times are simulated.
128 devices in a mesh: dev: 128 (over z, y, x, core).
Axes of the slice: x: 4, y: 4, z: 4, core: 2. Of those that a mesh axis runs over, the one named last changes fastest.
Arguments:
- tile_lists: int32 [3072, 512], P('dev'), may hold values from -1 to 8191, as said below
- send_rows: int32 [128, 8192], P('dev'), may hold values from -1 to 2047, as said below
- centres: float32 [2, 262144], P(None, 'dev'), may hold values from -12 to 12
- conic: float32 [2, 262144], P(None, 'dev'), may hold values from 0.015625 to 0.25
- rho: float32 [1, 262144], P(None, 'dev'), may hold values from -0.6 to 0.6
- opacity: float32 [1, 262144], P(None, 'dev'), may hold values from 0.002 to 0.03
- colors: float32 [3, 262144], P(None, 'dev'), may hold values from 0 to 1
- target: float32 [3, 2048, 384], P(None, 'dev'), may hold values from 0 to 1
Outputs:
- rendered: float32 [3, 2048, 384], P(None, 'dev')
- grads: float32 [9, 262144], P(None, 'dev')
Inputs may be any that keep to these rules, and one draw needn't show every extreme that they name: `tile_lists`: row t belongs to strip t // 24. An entry is -1 only after all live entries of its row; a live entry s * 64 + m names a slot m that owner s fills for that strip. Some row has no -1. `send_rows`: entry [s, r * 64 + m] is the local index on owner s of the Gaussian in slot m for strip r, or -1 for an unused slot. The used slots of an owner and strip come first, are distinct, and number at least 32; some owner fills all 64 slots for some strip.
All inputs are finite; a program needn't handle non-finite values.
Results may differ from a plain program's by a relative error of at most 0.0003.
Values sent between devices are 32-bit elements; how exact they have to be, the bound alone decides.
A program may use at most 256 MiB of HBM per device.

v0:
```python
import jax
import jax.numpy as jnp
from jax import lax
from jax.sharding import PartitionSpec as P


def with_halo(value, sides, width):
    for axis, dim in sides:
        size, length = (lax.axis_size(axis), value.shape[dim])
        up = [(i, (i + 1) % size) for i in range(size - 1)]
        down = [(j, i) for i, j in up]
        last = lax.slice_in_dim(value, length - width, length, axis=dim)
        first = lax.slice_in_dim(value, 0, width, axis=dim)
        before = lax.ppermute(last, axis, up)
        after = lax.ppermute(first, axis, down)
        value = jnp.concatenate([before, value, after], axis=dim)
    return value


def filter_taps():
    offsets = jnp.arange(11).astype(jnp.float32) - 5.0
    taps = jnp.exp(-offsets * offsets / 4.5)
    return taps / jnp.sum(taps)


def blur_strip(values):
    taps = filter_taps()
    count = values.shape[1] - 10
    width = values.shape[2]
    rows_done = taps[0] * values[:, 0:count]
    for shift in range(1, 11):
        rows_done = rows_done + taps[shift] * values[:, shift : shift + count]
    padded = jnp.pad(rows_done, ((0, 0), (0, 0), (5, 5)))
    result = taps[0] * padded[:, :, 0:width]
    for shift in range(1, 11):
        result = result + taps[shift] * padded[:, :, shift : shift + width]
    return result


def local_loss(render_pad, target_pad):
    mean_r = blur_strip(render_pad)
    mean_t = blur_strip(target_pad)
    var_r = blur_strip(render_pad * render_pad) - mean_r * mean_r
    var_t = blur_strip(target_pad * target_pad) - mean_t * mean_t
    covar = blur_strip(render_pad * target_pad) - mean_r * mean_t
    ssim = (
        (2.0 * mean_r * mean_t + 0.0001)
        * (2.0 * covar + 0.0009)
        / ((mean_r * mean_r + mean_t * mean_t + 0.0001) * (var_r + var_t + 0.0009))
    )
    centre_r = render_pad[:, 5:-5]
    centre_t = target_pad[:, 5:-5]
    diff = centre_r - centre_t
    return jnp.sum(0.8 * diff * diff + 0.2 * (1.0 - ssim))


def composite(params, live, tile, lower):
    count = tile * tile
    pixel = jnp.arange(count)
    vert = (pixel // tile).astype(jnp.float32) - (tile - 1) / 2.0
    horiz = (pixel % tile).astype(jnp.float32) - (tile - 1) / 2.0
    delta_x = horiz[None, :] - params[0][:, None]
    delta_y = vert[None, :] - params[1][:, None]
    cross = params[4] * jnp.sqrt(params[2] * params[3])
    quad = (
        params[2][:, None] * delta_x * delta_x
        + 2.0 * cross[:, None] * delta_x * delta_y
        + params[3][:, None] * delta_y * delta_y
    )
    alpha = jnp.where(live[:, None], params[5][:, None] * jnp.exp(-0.5 * quad), 0.0)
    logs = jnp.log1p(-alpha)
    before = jnp.dot(
        lower, logs, precision=lax.Precision.HIGHEST, preferred_element_type=jnp.float32
    )
    weight = alpha * jnp.exp(before)
    return jnp.dot(
        params[6:9], weight, precision=lax.Precision.HIGHEST, preferred_element_type=jnp.float32
    )


def shards(tile_lists, send_rows, centres, conic, rho, opacity, colors, target):
    devices = lax.axis_size("dev")
    slot_count = send_rows.shape[1]
    capacity = slot_count // devices
    owned_count = centres.shape[1]
    tile = target.shape[1]
    strip_tiles = tile_lists.shape[0]
    list_len = tile_lists.shape[1]
    local_params = jnp.concatenate([centres, conic, rho, opacity, colors], axis=0)
    nine = local_params.shape[0]
    owned = send_rows[0]
    wanted = lax.all_to_all(send_rows, "dev", split_axis=1, concat_axis=1, tiled=True)[0]
    anchor = jnp.arange(slot_count) // capacity
    global_id = anchor * owned_count + wanted
    piece = lax.all_gather(local_params, "dev", axis=1, tiled=True)
    inside = (wanted >= 0) & (global_id >= 0) & (global_id < piece.shape[1])
    taken = jnp.take(piece, jnp.clip(global_id, 0, piece.shape[1] - 1), axis=1)
    received = jnp.where(inside[None, :], taken, 0.0)
    live = tile_lists >= 0
    entry = jnp.maximum(tile_lists, 0)
    gathered = jnp.take(received, entry, axis=1).transpose(1, 0, 2)
    steps_idx = jnp.arange(list_len)
    lower = (steps_idx[:, None] > steps_idx[None, :]).astype(jnp.float32)

    def render_tile(args):
        return composite(args[0], args[1], tile, lower)

    colour_tiles = lax.map(render_tile, (gathered, live))
    image = (
        colour_tiles.reshape(strip_tiles, 3, tile, tile)
        .transpose(1, 2, 0, 3)
        .reshape(3, tile, strip_tiles * tile)
    )
    stacked = jnp.concatenate([image, target], axis=0)
    padded = with_halo(stacked, (("dev", 1),), 5)
    target_pad = padded[3:]
    loss_value, pull = jax.vjp(lambda rend: local_loss(rend, target_pad), padded[:3])
    grad_pad = pull(jnp.ones_like(loss_value))[0]
    rims = jnp.concatenate([grad_pad[:, :5], grad_pad[:, -5:]], axis=1)
    arrived = with_halo(rims, (("dev", 1),), 5)
    pixel_grad = grad_pad[:, 5:-5]
    pixel_grad = pixel_grad + jnp.pad(arrived[:, :5], ((0, 0), (0, tile - 5), (0, 0)))
    pixel_grad = pixel_grad + jnp.pad(arrived[:, -5:], ((0, 0), (tile - 5, 0), (0, 0)))
    cot_tiles = (
        pixel_grad.reshape(3, tile, strip_tiles, tile)
        .transpose(2, 0, 1, 3)
        .reshape(strip_tiles, 3, tile * tile)
    )

    def back_tile(args):
        params_tile, mask, cotangent = args
        _, back = jax.vjp(lambda chosen: composite(chosen, mask, tile, lower), params_tile)
        return jnp.where(mask[None, :], back(cotangent)[0], 0.0)

    entry_grads = lax.map(back_tile, (gathered, live, cot_tiles))
    flat_grads = entry_grads.transpose(1, 0, 2).reshape(nine, strip_tiles * list_len)
    target_slot = jnp.where(live, tile_lists, slot_count).reshape(strip_tiles * list_len)
    slot_grads = (
        jnp.zeros((nine, slot_count), jnp.float32).at[:, target_slot].add(flat_grads, mode="drop")
    )
    returned = lax.all_to_all(slot_grads, "dev", split_axis=1, concat_axis=1, tiled=True)
    home = jnp.where(owned >= 0, owned, owned_count)
    grads = jnp.zeros((nine, owned_count), jnp.float32).at[:, home].add(returned, mode="drop")
    return (image, grads)


def solution(mesh):
    return jax.shard_map(
        shards,
        mesh=mesh,
        in_specs=(
            P("dev", None),
            P("dev", None),
            P(None, "dev"),
            P(None, "dev"),
            P(None, "dev"),
            P(None, "dev"),
            P(None, "dev"),
            P(None, "dev", None),
        ),
        out_specs=(P(None, "dev", None), P(None, "dev")),
        check_vma=False,
    )
```

profile of v0, /device:TPU:1, one launch (start us, length us, event | category | flops | bytes accessed | tf_op | source)
XLA Modules:
  0.0 948.3 jit_solution(15841024074018081677)
XLA Ops:
  7.2 1.7 concatenate.33
  13.1 11.5 %all-to-all-start = ((s32[1,128,64]{2,0,1:T(1,128)}), s32[1,128,64]{2,0,1:T(1,128)S(1)}, u32[]{:S(2)}, u32[]{:S(2)}) async-start(s32[1,128,64]{2,0,1:T(1,128)} %bitcast), calls=%async_computation | async-start | bytes 131072 | tf_op jit(solution)/shard_map/all_to_all | solution.py:92
  27.6 6.6 all-to-all-done
  35.3 262.5 %all-gather.2.cloned.1.call-done = f32[9,262144]{0,1:T(8,128)} async-done(((f32[9,2048]{0,1:T(8,128)}), f32[9,262144]{0,1:T(8,128)}) %all-gather.2.cloned.1.call-update) | async-done | bytes 9437200 | tf_op jit(solution)/shard_map/all_gather | solution.py:95
  297.9 143.7 %gather_fusion = f32[8192,9]{1,0:T(8,128)} fusion(f32[9,262144]{0,1:T(8,128)} %all-gather.2.cloned.1.call-done, s32[8192]{0:T(1024)S(1)} %broadcast_clamp_fusion.1), kind=kCustom, calls=%fused_computation | custom fusion | bytes 622592 | tf_op jit(solution)/shard_map/jit(_take)/gather | solution.py:97
  441.6 7.6 select_bitcast_fusion
  449.2 43.2 %gather_fusion.1 = f32[12288,9]{1,0:T(8,128)} fusion(f32[9,8192]{0,1:T(8,128)} %select_bitcast_fusion, s32[12288]{0:T(1024)S(1)} %broadcast_clamp_fusion), kind=kCustom, calls=%fused_computation.1 | custom fusion | bytes 933888 | tf_op jit(solution)/shard_map/jit(_take)/gather | solution.py:101
  492.4 4.4 copy.45
  497.0 55.9 %while.29 = (s32[]{:T(128)}, f32[24,3,256]{2,0,1:T(8,128)S(1)}, f32[24,9,512]{2,1,0:T(8,128)S(1)}, pred[24,512]{1,0:T(8,128)(4,1)S(1)}, s32[]{:T(128)}, /*index=...) while((s32[]{:T(128)}, f32[24,3,256]{2,0,1:T(8,128)S(1)}, ...), condition=%wide.region_1.2_spmd.clone, body=%wide.region_0.1_spmd.clone.sunk | while | flops 814224896 | bytes 1123045 | solution.py:108
  504.1 1.6 fusion.368
  506.4 1.6 fusion.368
  511.1 1.6 fusion.368
  513.4 1.6 fusion.368
  518.1 1.6 fusion.368
  553.6 4.8 collective-permute-start
  558.4 1.9 collective-permute-start.1
  568.1 7.0 fusion.312
  575.1 7.0 fusion.302
  582.1 7.0 fusion.292
  589.0 7.0 fusion.245
  596.0 7.0 fusion.238
  603.0 7.7 broadcast_multiply_fusion.11
  610.7 7.1 broadcast_multiply_fusion.64
  617.9 5.0 broadcast_multiply_fusion.24
  622.9 2.1 broadcast_multiply_fusion.10
  626.3 6.2 broadcast_multiply_fusion.15
  632.6 6.2 broadcast_multiply_fusion.13
  638.8 6.2 broadcast_multiply_fusion.12
  646.1 6.2 broadcast_multiply_fusion.16
  652.8 3.6 collective-permute-start.2
  656.4 2.1 collective-permute-start.3
  658.6 4.6 collective-permute-done.3
  664.0 122.0 %while.30 = (s32[]{:T(128)}, f32[24,9,512]{2,1,0:T(8,128)S(1)}, pred[24,512]{1,0:T(8,128)(4,1)S(1)}, f32[24,3,256]{2,1,0:T(4,128)S(1)}, f32[24,9,512]{2,1,0:T(8,...) while((s32[]{:T(128)}, f32[24,9,512]{2,1,0:T(8,128)S(1)}, ...), condition=%wide.region_10.11_spmd.clone.clone, body=%wide.region_3.10_spmd.clone.clone.sunk | while | flops 1632681984 | bytes 2828525 | solution.py:135
  666.1 2.1 fusion.377
  671.2 2.1 fusion.377
  676.3 2.1 fusion.377
  681.4 2.1 fusion.377
  686.5 2.1 fusion.377
  691.5 2.1 fusion.377
  696.6 2.1 fusion.377
  701.7 2.1 fusion.377
  706.8 2.1 fusion.377
  711.9 2.1 fusion.377
  717.0 2.1 fusion.377
  722.0 2.1 fusion.377
  727.1 2.1 fusion.377
  732.2 2.1 fusion.377
  737.3 2.1 fusion.377
  742.4 2.1 fusion.377
  747.4 2.1 fusion.377
  752.5 2.1 fusion.377
  757.6 2.1 fusion.377
  762.7 2.1 fusion.377
  767.8 2.1 fusion.377
  772.9 2.1 fusion.377
  777.9 2.1 fusion.377
  783.0 2.1 fusion.377
  786.8 4.0 copy.51
  790.8 68.2 %scatter_custom_fusion = f32[9,8192]{0,1:T(8,128)} fusion(s32[12288]{0:T(1024)S(1)} %bitcast.225, f32[12288,9]{1,0:T(8,128)} %copy.51, f32[]{:T(128)} %constant.261.clone.1), kind=kCustom, calls=%fused_computation.157 | custom fusion | flops 110592 | bytes 295424 | tf_op jit(solution)/shard_map/scatter-add | solution.py:139
  859.0 3.0 copy.52
  863.2 15.9 %all-to-all-start.1 = ((f32[128,1,576]{2,1,0:T(1,128)}), f32[128,1,576]{2,1,0:T(1,128)S(1)}, u32[]{:S(2)}, u32[]{:S(2)}) async-start(f32[128,1,576]{2,1,0:T(1,128)} %reshape.604), calls=%async_computation.1 | async-start | bytes 655360 | tf_op jit(solution)/shard_map/all_to_all | solution.py:141
  879.1 11.7 %all-to-all-done.1 = f32[128,1,576]{2,1,0:T(1,128)S(1)} async-done(((f32[128,1,576]{2,1,0:T(1,128)}), f32[128,1,576]{2,1,0:T(1,128)S(1)}, u32[]{:S(2)}, u32[]{:S(2)}) %all-to-all-start.1) | async-done | bytes 294944 | tf_op jit(solution)/shard_map/all_to_all | solution.py:141
  893.3 2.6 copy.54
  895.9 44.6 %scatter_custom_fusion.1 = f32[9,2048]{0,1:T(8,128)S(1)} fusion(s32[8192]{0:T(1024)S(1)} %bitcast.226, f32[8192,9]{1,0:T(8,128)} %copy.54, f32[]{:T(128)} %constant.261.clone.1), kind=kCustom, calls=%fused_computation.178 | custom fusion | flops 73728 | bytes 74240 | tf_op jit(solution)/shard_map/scatter-add | solution.py:143
  (562 shorter events, 135.6 us)
Async XLA Ops:
  7.2 290.7 %all-gather.2.cloned.1.call-start = ((), (), s32[]{:S(2)}) async-start(), calls=%async_computation.2 | async-start | bytes 135266304 | tf_op jit(solution)/shard_map/all_gather | solution.py:95
  13.1 21.1 %all-to-all-start = ((s32[1,128,64]{2,0,1:T(1,128)}), s32[1,128,64]{2,0,1:T(1,128)S(1)}, u32[]{:S(2)}, u32[]{:S(2)}) async-start(s32[1,128,64]{2,0,1:T(1,128)} %bitcast), calls=%async_computation | async-start | bytes 131072 | tf_op jit(solution)/shard_map/all_to_all | solution.py:92
  497.0 56.6 %copy-start.1 = (f32[3,16,384]{2,1,0:T(8,128)S(1)}, f32[3,16,384]{2,1,0:T(8,128)}, u32[]{:S(2)}) copy-start(f32[3,16,384]{2,1,0:T(8,128)} %param.19) | copy-start | bytes 221188
  553.5 71.4 %copy-start = (f32[3,16,384]{2,1,0:T(8,128)}, f32[3,16,384]{2,1,0:T(8,128)S(1)}, u32[]{:S(2)}) copy-start(f32[3,16,384]{2,1,0:T(8,128)S(1)} %reshape.539) | copy-start | bytes 221188
  553.6 14.4 %collective-permute-start = (f32[6,5,384]{2,1,0:T(8,128)S(1)}, f32[6,5,384]{2,1,0:T(8,128)S(1)}, u32[]{:S(2)}, u32[]{:S(2)}) collective-permute-start(f32[6,5,384]{2,1,0:T(8,128)S(1)} %get-tuple-element.332), channel_id=1, source_target_pairs={{0,1},{1,2},{2,3},{3,4},{4,5},{5,6},{6,7},{7,8},{8,9},{9,10},{10,1... | collective-permute-start | bytes 138248 | tf_op jit(solution)/shard_map/ppermute | solution.py:14
  558.4 9.6 %collective-permute-start.1 = (f32[6,5,384]{2,1,0:T(8,128)S(1)}, f32[6,5,384]{2,1,0:T(8,128)S(1)}, u32[]{:S(2)}, u32[]{:S(2)}) collective-permute-start(f32[6,5,384]{2,1,0:T(8,128)S(1)} %get-tuple-element.333), channel_id=1, source_target_pairs={{1,0},{2,1},{3,2},{4,3},{5,4},{6,5},{7,6},{8,7},{9,8},{10,9},{11,1... | collective-permute-start | bytes 138248 | tf_op jit(solution)/shard_map/ppermute | solution.py:15
  652.8 5.8 collective-permute-start.2
  656.4 6.8 collective-permute-start.3
  859.0 20.1 %copy-start.2 = (s32[1,8192]{1,0:T(1,128)S(1)}, s32[1,8192]{1,0:T(1,128)}, u32[]{:S(2)}) copy-start(s32[1,8192]{1,0:T(1,128)} %param.13) | copy-start | bytes 98308
  863.2 27.6 %all-to-all-start.1 = ((f32[128,1,576]{2,1,0:T(1,128)}), f32[128,1,576]{2,1,0:T(1,128)S(1)}, u32[]{:S(2)}, u32[]{:S(2)}) async-start(f32[128,1,576]{2,1,0:T(1,128)} %reshape.604), calls=%async_computation.1 | async-start | bytes 655360 | tf_op jit(solution)/shard_map/all_to_all | solution.py:141
Sparse Core Ops, SparseCore 0:
  11.0 286.8 all-gather.1
where the time goes:
time: 952 us; the launch traced here: 948 us
  waiting for transfers between devices  285 us (30%)
  local copies, waits for them, and re-layouts  216 us (23%)
  other arithmetic  215 us (23%)
  matrix products  167 us (18%)
  starting transfers between devices  39.9 us (4%)
  between operations  21.4 us (2%)
    all_gather x1, waiting for transfers between devices, shards(): piece = lax.all_gather(local_params, 'dev', axis=1, tiled=True)  263 us
    gather x1, local copies, waits for them, and re-layouts, shards(): taken = jnp.take(piece, jnp.clip(global_id, 0, piece.shape[1] - 1), axis=1)  144 us
    dot_general x72, matrix products, composite(): jnp.dot(lower, logs, precision=lax.Precision.HIGHEST, preferred_element_t...  123 us
    scatter-add x1, other arithmetic, shards(): jnp.zeros((nine, slot_count), jnp.float32).at[:, target_slot]  68.2 us
    gather x2, local copies, waits for them, and re-layouts, shards(): gathered = jnp.take(received, entry, axis=1).transpose(1, 0, 2)  47.6 us
    scatter-add x1, other arithmetic, shards(): jnp.zeros((nine, owned_count), jnp.float32).at[:, home]  44.6 us
    dot_general x72, matrix products, composite(): jnp.dot(params[6:9], weight, precision=lax.Precision.HIGHEST, preferred_e...  44.3 us
    add x5, other arithmetic, blur_strip(): rows_done = rows_done + taps[shift] * values[:, shift:shift + count]  34.9 us
  transfers between devices with their start and end apart: 7, of which 4 were waited for; matrix products, arithmetic and copies ran while one was open for 1% of the time, Pallas kernels for 0%

commit v1 on v0

v1 whole, which is shorter than its diff:
```python
import functools
import math

import jax
import jax.numpy as jnp
import numpy as np
from jax import lax
from jax.experimental import pallas as pl
from jax.experimental.pallas import tpu as pltpu
from jax.sharding import PartitionSpec as P

F32 = jnp.float32
BF16 = jnp.bfloat16
LOG2E = math.log2(math.e)
SUB, LANE = 8, 128
DEAD = -10000.0


def lane_pick(table, lanes):
    return jnp.take_along_axis(table, lanes, axis=1, mode="promise_in_bounds")


def iota(shape, dim):
    return lax.broadcasted_iota(jnp.int32, shape, dim)


def sub_sum(x):
    for d in (4, 2, 1):
        x = x + pltpu.roll(x, d, 0)
    return x


def split2(x):
    one = x.astype(BF16).astype(F32)
    return one, x - one


def coefficient_rows(cx, cy, a, c, rho, op):
    b = rho * jnp.sqrt(a * c)
    bx, by = a * cx + b * cy, c * cy + b * cx
    one = jnp.log(op) - 0.5 * (cx * bx + cy * by)
    return [LOG2E * k for k in (-0.5 * a, -b, -0.5 * c, bx, by, one)]


def owner_kernel(send, centres, conic, rho, opacity, colors, out, table, ninth):
    rows = coefficient_rows(
        centres[0:1, :], centres[1:2, :], conic[0:1, :], conic[1:2, :], rho[...], opacity[...]
    )
    for p, row in enumerate(rows + [colors[0:1, :], colors[1:2, :]]):
        table[p : p + 1, :] = row
    blocks = table.shape[1] // LANE
    for h in range(blocks):
        ninth[h : h + 1, :] = colors[2:3, h * LANE : (h + 1) * LANE]
    lane = iota((SUB, LANE), 1)
    row = iota((SUB, LANE), 0)

    def pair(i, carry):
        start = pl.multiple_of(i * LANE, LANE)
        idx = jnp.broadcast_to(jnp.maximum(send[0:1, pl.ds(start, LANE)], 0), (SUB, LANE))
        hi, lo = lax.shift_right_logical(idx, 7), lax.bitwise_and(idx, 127)
        acc = jnp.zeros((SUB, LANE), F32)
        for h in range(blocks):
            acc = jnp.where(hi == h, lane_pick(table[:, h * LANE : (h + 1) * LANE], lo), acc)
        last = jnp.zeros((SUB, LANE), F32)
        for v in range(blocks // SUB):
            got = lane_pick(ninth[v * SUB : (v + 1) * SUB, :], lo)
            last = jnp.where(hi == row + v * SUB, got, last)
        last = sub_sum(last)
        left = lane < 64
        top = jnp.where(row == 0, 1.0, 0.0)
        out[2 * i] = jnp.where(left, acc, pltpu.roll(last, 64, 1) * top)
        out[2 * i + 1] = jnp.where(left, pltpu.roll(acc, 64, 1), last * top)
        return carry

    lax.fori_loop(0, send.shape[1] // LANE, pair, 0)


def basis_rows(lanes):
    pixel = iota((1, lanes), 1)
    v = lax.shift_right_logical(pixel, 4).astype(F32) - 7.5
    u = lax.bitwise_and(pixel, 15).astype(F32) - 7.5
    return [u * u, u * v, v * v, u, v, jnp.ones_like(u)]


def stack_rows(rows, count):
    shape = (count, next(r for r in rows if r is not None).shape[1])
    at = iota(shape, 0)
    result = jnp.zeros(shape, F32)
    for p, row in enumerate(rows):
        if row is not None:
            result = jnp.where(at == p, jnp.broadcast_to(row, shape), result)
    return result


def scan_sub(x):
    at = iota(x.shape, 0)
    x = jnp.where(at == 0, 1.0, pltpu.roll(x, 1, 0))
    for d in (1, 2, 4):
        x = x * jnp.where(at >= d, pltpu.roll(x, d, 0), 1.0)
    return x


def forward_kernel(lists, recv, rend, chunk_rend, chunk_start, left_out, table, ninth, cols, alphas):
    lane = iota((SUB, LANE), 1)
    row = iota((SUB, LANE), 0)

    @pl.when(pl.program_id(0) == 0)
    def _():
        def pair(h, carry):
            even, odd = recv[2 * h], recv[2 * h + 1]
            left = lane < 64
            table[h] = jnp.where(left, even, pltpu.roll(odd, 64, 1))
            both = jnp.where(left, pltpu.roll(even, 64, 1), odd)
            ninth[pl.ds(h, 1), :] = both[0:1, :]
            return carry

        lax.fori_loop(0, recv.shape[0] // 2, pair, 0)

    blocks = table.shape[0]
    count = lists.shape[2]

    for q in range(count // LANE):
        span = slice(q * LANE, (q + 1) * LANE)
        raw = jnp.broadcast_to(lists[0, 0:1, span], (SUB, LANE))
        idx = jnp.maximum(raw, 0)
        hi, lo = lax.shift_right_logical(idx, 7), lax.bitwise_and(idx, 127)
        acc = jnp.zeros((SUB, LANE), F32)
        for h in range(blocks):
            acc = jnp.where(hi == h, lane_pick(table[h], lo), acc)
        last = jnp.zeros((SUB, LANE), F32)
        for v in range(blocks // SUB):
            got = lane_pick(ninth[v * SUB : (v + 1) * SUB, :], lo)
            last = jnp.where(hi == row + v * SUB, got, last)
        last = sub_sum(last)
        acc = jnp.where((row == 5) & (raw < 0), DEAD, acc)
        one, rest = split2(acc)
        two, three = split2(rest)
        b_one, b_two = split2(last)
        more = jnp.where(row == 1, b_two, jnp.where(row == 7, last, b_one))
        more = jnp.where((row == 3) | (row == 4), pltpu.roll(one, 5, 0), more)
        more = jnp.where((row == 5) | (row == 6), pltpu.roll(acc, 7, 0), more)
        stack = jnp.concatenate([one, two, three, more], axis=0)
        cols[span, :] = jnp.concatenate([stack, jnp.zeros((LANE - 32, LANE), F32)], axis=0).T

    left = cols[:, 0:32].astype(BF16)
    left_out[0] = left
    basis = stack_rows((basis_rows(256) + [None, None]) * 3, 32).astype(BF16)
    alphas[...] = jnp.dot(left, basis, preferred_element_type=F32)

    groups = count // SUB
    step = 8

    def first(j, product):
        for k in range(step):
            at = pl.ds(pl.multiple_of((j * step + k) * SUB, SUB), SUB)
            alpha = jnp.exp2(alphas[at, :])
            alphas[at, :] = alpha
            product = product * (1.0 - alpha)
        return product

    product = lax.fori_loop(0, groups // step, first, jnp.ones((SUB, 256), F32))
    trans = scan_sub(product)
    chunk_start[0] = trans

    def second(j, carry):
        trans, red, green, blue = carry
        for k in range(step):
            at = pl.ds(pl.multiple_of((j * step + k) * SUB, SUB), SUB)
            weight = trans * alphas[at, :]
            trans = trans - weight
            color = cols[at, :]
            red = red + weight * color[:, 29:30]
            green = green + weight * color[:, 30:31]
            blue = blue + weight * color[:, 31:32]
        return trans, red, green, blue

    zero = jnp.zeros((SUB, 256), F32)
    _, *channels = lax.fori_loop(0, groups // step, second, (trans, zero, zero, zero))
    for ch, part in enumerate(channels):
        chunk_rend[0, ch] = part
        rend[0, ch : ch + 1, :] = sub_sum(part)[0:1, :]


def taps_of():
    offsets = np.arange(11, dtype=np.float32) - np.float32(5)
    taps = np.exp(-offsets * offsets / np.float32(4.5)).astype(np.float32)
    return [float(t) for t in taps / taps.sum(dtype=np.float32)]


TAPS = taps_of()


def blur_rows(read, start, count):
    total = TAPS[5] * read(start, count)
    for m in range(1, 6):
        total = total + TAPS[5 + m] * (read(start - m, count) + read(start + m, count))
    return total


def blur_lanes(x):
    rows, width = x.shape
    pad = jnp.zeros((rows, LANE), F32)
    wide = jnp.concatenate([x, pad], axis=1)
    total = TAPS[5] * x
    for m in range(1, 6):
        both = pltpu.roll(wide, m, 1) + pltpu.roll(wide, width + LANE - m, 1)
        total = total + TAPS[5 + m] * both[:, :width]
    return total


def loss_kernel(me, before, centre, after, t_before, t_centre, t_after, grad, pads, maps):
    height = centre.shape[1]
    mine = me[0]
    total_rows = me[1]
    width = centre.shape[2]
    at = iota((2 * height, width), 0) - height // 2 + mine * height
    inside = (at >= 0) & (at < total_rows)
    for ch in range(3):
        for i, (r, t) in enumerate(((before, t_before), (centre, t_centre), (after, t_after))):
            span = slice(i * height, (i + 1) * height)
            rr, tt = r[ch], t[ch]
            pads[0, span, :] = rr
            pads[1, span, :] = tt
            pads[2, span, :] = rr * rr
            pads[3, span, :] = tt * tt
            pads[4, span, :] = rr * tt

        def wide_blur(k):
            vertical = blur_rows(lambda s, n: pads[k, s : s + n, :], height // 2, 2 * height)
            return blur_lanes(vertical)

        mr, mt, rr, tt, rt = (wide_blur(k) for k in range(5))
        cv = rt - mr * mt
        top1 = 2.0 * mr * mt + 0.0001
        top2 = 2.0 * cv + 0.0009
        low1 = mr * mr + mt * mt + 0.0001
        low2 = (rr - mr * mr) + (tt - mt * mt) + 0.0009
        inv1, inv2 = 1.0 / low1, 1.0 / low2
        both = inv1 * inv2
        ssim = top1 * top2 * both
        d_rr = -ssim * inv2
        d_rt = 2.0 * top1 * both
        d_mr = 2.0 * (mt * (top2 - top1) * both + mr * ssim * (inv2 - inv1))
        for k, value in enumerate((d_mr, d_rr, d_rt)):
            maps[k] = jnp.where(inside, value, 0.0)

        def back_blur(k):
            vertical = blur_rows(lambda s, n: maps[k, s : s + n, :], height // 2, height)
            return blur_lanes(vertical)

        g_mr, g_rr, g_rt = (back_blur(k) for k in range(3))
        r, t = centre[ch], t_centre[ch]
        grad[ch] = 1.6 * (r - t) - 0.2 * (g_mr + 2.0 * r * g_rr + t * g_rt)


NT = (((1,), (1,)), ((), ()))


def onehot(lo, rows):
    return jnp.where(iota((rows, lo.shape[1]), 0) == lo, 1.0, 0.0).astype(BF16)


def spread(values, hi, blocks):
    masked = [jnp.where(hi == h, values, 0.0) for h in range(blocks)]
    return jnp.concatenate(masked, axis=0)


def scatter_block(eight, ninth, idx, blocks):
    span = idx.shape[1]
    hi, lo = lax.shift_right_arithmetic(idx, 8), lax.bitwise_and(idx, 255)
    hot = onehot(lo, 256)
    hi8 = jnp.broadcast_to(hi, (SUB, span))
    own = iota((blocks, span), 0) == hi
    total = None
    for values, extra in zip(split2(eight), split2(ninth)):
        left = jnp.concatenate(
            [spread(values, hi8, blocks), jnp.where(own, jnp.broadcast_to(extra, own.shape), 0.0)],
            axis=0,
        ).astype(BF16)
        part = lax.dot_general(left, hot, NT, preferred_element_type=F32)
        total = part if total is None else total + part
    return total


def backward_kernel(lists, left_in, cot, chunk_rend, chunk_start, out, fields, weights, halves, grads, slots):
    tile = pl.program_id(0)
    count = lists.shape[2]
    groups = count // SUB
    step = 8
    rows = [cot[0, ch : ch + 1, :] for ch in range(3)]
    ones, twos = zip(*(split2(r) for r in rows))
    basis = stack_rows((basis_rows(256) + [None, None]) * 3, 32)
    back = stack_rows(
        [None] * 6 + [ones[0], ones[1]] + [None] * 6 + [ones[0], ones[1]] + [None] * 6
        + [ones[0], ones[1], ones[2], ones[2], twos[2], twos[0], twos[1]], 32
    )
    right = jnp.concatenate([basis, back], axis=1).astype(BF16)
    fields[...] = jnp.dot(left_in[0], right, preferred_element_type=F32)
    start = chunk_start[0]

    def first(j, trans):
        for k in range(step):
            at = pl.ds(pl.multiple_of((j * step + k) * SUB, SUB), SUB)
            alpha = jnp.exp2(fields[at, 0:256])
            fields[at, 0:256] = alpha
            weight = trans * alpha
            weights[at, :] = weight
            trans = trans - weight
        return trans

    final = lax.fori_loop(0, groups // step, first, start)
    behind = sum(chunk_rend[0, ch] * rows[ch] for ch in range(3))
    at8 = iota((SUB, 256), 0)
    behind = jnp.where(at8 == SUB - 1, 0.0, pltpu.roll(behind, SUB - 1, 0))
    for d in (1, 2, 4):
        behind = behind + jnp.where(at8 < SUB - d, pltpu.roll(behind, SUB - d, 0), 0.0)
    shade = behind / final

    def second(jj, shade):
        j = groups // step - 1 - jj
        parts = []
        for k in reversed(range(step)):
            at = pl.ds(pl.multiple_of((j * step + k) * SUB, SUB), SUB)
            alpha, weight = fields[at, 0:256], weights[at, :]
            diff = fields[at, 256:512] - shade
            shade = shade + alpha * diff
            parts.append((weight * diff, weight))
        parts = parts[::-1]
        for k in range(0, step, 2):
            at = pl.ds(pl.multiple_of((j * step + k) * SUB, 2 * SUB), 2 * SUB)
            for i in range(2):
                value = jnp.concatenate([parts[k][i], parts[k + 1][i]], axis=0)
                one = value.astype(BF16)
                halves[at, 512 * i : 512 * i + 256] = one
                halves[at, 512 * i + 256 : 512 * i + 512] = (value - one.astype(F32)).astype(BF16)
        return shade

    lax.fori_loop(0, groups // step, second, shade)
    base = stack_rows(basis_rows(256), 16)
    firsts = stack_rows([None] * 6 + list(ones) + list(twos), 16)
    seconds = stack_rows([None] * 6 + list(ones), 16)
    kernel = jnp.concatenate([base, base, firsts, seconds], axis=1).astype(BF16)
    found = lax.dot_general(kernel, halves[...], NT, preferred_element_type=F32)
    low = found[8:16, :]
    at16 = iota(low.shape, 0)
    top = found[0:8, :] + jnp.where(at16 >= 6, pltpu.roll(low, 5, 0), 0.0)
    last = low[0:1, :] + low[3:4, :]
    idx = jnp.maximum(lists[0], 0)
    blocks = slots.shape[0] // (SUB + 1)
    part = scatter_block(top, last, idx, blocks)

    @pl.when(tile == 0)
    def _():
        slots[...] = part

    @pl.when(tile > 0)
    def _():
        slots[...] = slots[...] + part

    @pl.when(tile == pl.num_programs(0) - 1)
    def _():
        lane = iota((SUB, LANE), 1)
        left = lane < 64
        top8 = jnp.where(iota((SUB, LANE), 0) == 0, 1.0, 0.0)

        for h in range(blocks):
            for half in range(2):
                span = slice(half * LANE, (half + 1) * LANE)
                acc = slots[h * SUB : (h + 1) * SUB, span]
                extra = jnp.broadcast_to(slots[blocks * SUB + h : blocks * SUB + h + 1, span], (SUB, LANE))
                owner = 4 * h + 2 * half
                out[owner] = jnp.where(left, acc, pltpu.roll(extra, 64, 1) * top8)
                out[owner + 1] = jnp.where(left, pltpu.roll(acc, 64, 1), extra * top8)


def home_kernel(back, send, centres, conic, rho, opacity, out, total, rows):
    lane = iota((SUB, LANE), 1)
    left = lane < 64
    pairs = back.shape[0] // 2
    per = 8
    blocks = centres.shape[1] // 256
    total[...] = jnp.zeros_like(total)

    def chunk(c, carry):
        eight, ninth = [], []
        for k in range(per):
            i = c * per + k
            even, odd = back[2 * i], back[2 * i + 1]
            eight.append(jnp.where(left, even, pltpu.roll(odd, 64, 1)))
            ninth.append(jnp.where(left, pltpu.roll(even, 64, 1), odd)[0:1, :])
        start = pl.multiple_of(c * per * LANE, per * LANE)
        idx = send[0:1, pl.ds(start, per * LANE)]
        total[...] = total[...] + scatter_block(
            jnp.concatenate(eight, axis=1), jnp.concatenate(ninth, axis=1), idx, blocks
        )
        return carry

    lax.fori_loop(0, pairs // per, chunk, 0)
    for h in range(blocks):
        span = slice(h * 256, (h + 1) * 256)
        rows[0:8, span] = total[h * SUB : (h + 1) * SUB, :]
        rows[8:9, span] = total[blocks * SUB + h : blocks * SUB + h + 1, :]
    m_uu, m_uv, m_vv, m_u, m_v, m_1 = (rows[p : p + 1, :] for p in range(6))
    cx, cy = centres[0:1, :], centres[1:2, :]
    a, c = conic[0:1, :], conic[1:2, :]
    r = rho[...]
    root = jnp.sqrt(a * c)
    b = r * root
    x1, y1 = m_u - cx * m_1, m_v - cy * m_1
    xx = m_uu - cx * (m_u + x1)
    yy = m_vv - cy * (m_v + y1)
    xy = m_uv - cx * m_v - cy * x1
    out[0:1, :] = a * x1 + b * y1
    out[1:2, :] = c * y1 + b * x1
    out[2:3, :] = -0.5 * xx - xy * (0.5 * r * (root / a))
    out[3:4, :] = -0.5 * yy - xy * (0.5 * r * (root / c))
    out[4:5, :] = -xy * root
    out[5:6, :] = m_1 / opacity[...]
    out[6:9, :] = rows[6:9, :]


def struct(*shape, dtype=F32):
    return jax.ShapeDtypeStruct(shape, dtype)


def shards(tile_lists, send_rows, centres, conic, rho, opacity, colors, target):
    devices = lax.axis_size("dev")
    owned = centres.shape[1]
    tiles, count = tile_lists.shape
    height, width = target.shape[1], target.shape[2]
    pixels = height * height
    params = pltpu.CompilerParams(vmem_limit_bytes=48 << 20)
    outgoing = pl.pallas_call(
        owner_kernel,
        out_shape=struct(devices, SUB, LANE),
        scratch_shapes=[pltpu.VMEM((SUB, owned), F32), pltpu.VMEM((owned // LANE, LANE), F32)],
        name="owner_gather",
    )(send_rows, centres, conic, rho, opacity, colors)
    incoming = lax.all_to_all(outgoing, "dev", split_axis=0, concat_axis=0, tiled=True)

    lists = tile_lists.reshape(tiles, SUB, count // SUB).transpose(0, 2, 1).reshape(tiles, 1, count)
    whole = lambda *shape: pl.BlockSpec(shape, lambda t: (0,) * len(shape))
    per_tile = lambda *shape: pl.BlockSpec((1,) + shape, lambda t: (t,) + (0,) * len(shape))
    rend, chunk_rend, chunk_start, left = pl.pallas_call(
        forward_kernel,
        grid=(tiles,),
        in_specs=[per_tile(1, count), whole(devices, SUB, LANE)],
        out_specs=[per_tile(3, pixels), per_tile(3, SUB, pixels), per_tile(SUB, pixels), per_tile(count, 32)],
        out_shape=[
            struct(tiles, 3, pixels),
            struct(tiles, 3, SUB, pixels),
            struct(tiles, SUB, pixels),
            struct(tiles, count, 32, dtype=BF16),
        ],
        scratch_shapes=[
            pltpu.VMEM((devices // 2, SUB, LANE), F32),
            pltpu.VMEM((devices // 2, LANE), F32),
            pltpu.VMEM((count, LANE), F32),
            pltpu.VMEM((count, pixels), F32),
        ],
        compiler_params=params,
        name="tile_forward",
    )(lists, incoming)
    image = rend.reshape(tiles, 3, height, height).transpose(1, 2, 0, 3).reshape(3, height, width)

    up = [(i, i + 1) for i in range(devices - 1)]
    down = [(j, i) for i, j in up]
    me = lax.axis_index("dev")
    where = jnp.stack([me, devices * height]).astype(jnp.int32)
    pixel_grad = pl.pallas_call(
        loss_kernel,
        in_specs=[pl.BlockSpec(memory_space=pltpu.SMEM)] + [pl.BlockSpec(memory_space=pltpu.VMEM)] * 6,
        out_shape=struct(3, height, width),
        scratch_shapes=[pltpu.VMEM((5, 3 * height, width), F32), pltpu.VMEM((3, 2 * height, width), F32)],
        name="loss_gradient",
    )(
        where,
        lax.ppermute(image, "dev", up), image, lax.ppermute(image, "dev", down),
        lax.ppermute(target, "dev", up), target, lax.ppermute(target, "dev", down),
    )
    cot = pixel_grad.reshape(3, height, tiles, height).transpose(2, 0, 1, 3).reshape(tiles, 3, pixels)

    hi_blocks = devices * 64 // 256
    slot_grads = pl.pallas_call(
        backward_kernel,
        grid=(tiles,),
        in_specs=[
            per_tile(1, count), per_tile(count, 32), per_tile(3, pixels),
            per_tile(3, SUB, pixels), per_tile(SUB, pixels),
        ],
        out_specs=whole(devices, SUB, LANE),
        out_shape=struct(devices, SUB, LANE),
        scratch_shapes=[
            pltpu.VMEM((count, 2 * pixels), F32),
            pltpu.VMEM((count, pixels), F32),
            pltpu.VMEM((count, 4 * pixels), BF16),
            pltpu.VMEM((16, count), F32),
            pltpu.VMEM((hi_blocks * (SUB + 1), 256), F32),
        ],
        compiler_params=params,
        name="tile_backward",
    )(lists, left, cot, chunk_rend, chunk_start)
    returned = lax.all_to_all(slot_grads, "dev", split_axis=0, concat_axis=0, tiled=True)
    grads = pl.pallas_call(
        home_kernel,
        out_shape=struct(9, owned),
        scratch_shapes=[
            pltpu.VMEM((owned // 256 * (SUB + 1), 256), F32),
            pltpu.VMEM((16, owned), F32),
        ],
        name="owner_scatter",
    )(returned, send_rows, centres, conic, rho, opacity)
    return image, grads


def solution(mesh):
    return jax.shard_map(
        shards,
        mesh=mesh,
        in_specs=(
            P("dev", None),
            P("dev", None),
            P(None, "dev"),
            P(None, "dev"),
            P(None, "dev"),
            P(None, "dev"),
            P(None, "dev"),
            P(None, "dev", None),
        ),
        out_specs=(P(None, "dev", None), P(None, "dev")),
        check_vma=False,
    )
```

time: 952 us -> 196 us (0.21)
  waiting for transfers between devices: 285 us -> 9.2 us
  other arithmetic: 215 us -> 0.67 us
  local copies, waits for them, and re-layouts: 216 us -> 15.2 us
  matrix products: 167 us -> 0 us
  Pallas kernels: 0 us -> 123 us
  blocking collectives: 0 us -> 25 us
  between operations: 21.4 us -> 0.76 us
  starting transfers between devices: 39.9 us -> 22.2 us
    all_gather x1 -> x0, waiting for transfers between devices: 263 us -> none  [shards(): piece = lax.all_gather(local_params, 'dev', axis=1, tiled=True)]
    gather x3 -> x0, local copies, waits for them, and re-layouts: 191 us -> none  [the longest x1 144 us: shards(): taken = jnp.take(piece, jnp.clip(global_id, 0, piece.shape[1] - 1), axis=1)]
    dot_general x144 -> x0, matrix products: 167 us -> none  [the longest x72 123 us: composite(): jnp.dot(lower, logs, precision=lax.Precision.HIGHEST, preferred_element_t...]
    pallas_call x0 -> x5, Pallas kernels: none -> 123 us  [the longest x1 55 us: shards(): pl.pallas_call(forward_kernel, grid=(tiles,), in_specs=[per_tile(1, count...]
    scatter-add x2 -> x0, other arithmetic: 113 us -> none  [the longest x1 68.2 us: shards(): jnp.zeros((nine, slot_count), jnp.float32).at[:, target_slot]]
    mul x131 -> x0, other arithmetic: 49.8 us -> none  [the longest x5 28.1 us: blur_strip(): result = result + taps[shift] * padded[:, :, shift:shift + width]]
    add x6 -> x0, other arithmetic: 34.9 us -> none  [the longest x5 34.9 us: blur_strip(): rows_done = rows_done + taps[shift] * values[:, shift:shift + count]]
    all_to_all x0 -> x1, blocking collectives: none -> 25 us  [shards(): lax.all_to_all(slot_grads, 'dev', split_axis=0, concat_axis=0, tiled=True)]
  transfers between devices with their start and end apart: 7 -> 5, of which waited for: 4 -> 2; matrix products, arithmetic and copies ran while one was open for 1% -> 3% of each run, Pallas kernels for 0% -> 28%
where the time goes in v1:
time: 196 us
  Pallas kernels  123 us (63%)
  blocking collectives  25 us (13%)
  starting transfers between devices  22.2 us (11%)
  local copies, waits for them, and re-layouts  15.2 us (8%)
  waiting for transfers between devices  9.2 us (5%)
    pallas_call x1, Pallas kernels, shards(): pl.pallas_call(forward_kernel, grid=(tiles,), in_specs=[per_tile(1, count...  55 us
    pallas_call x1, Pallas kernels, shards(): pl.pallas_call(backward_kernel, grid=(tiles,), in_specs=[per_tile(1, coun...  45.1 us
    all_to_all x1, blocking collectives, shards(): lax.all_to_all(slot_grads, 'dev', split_axis=0, concat_axis=0, tiled=True)  25 us
    pallas_call x1, Pallas kernels, shards(): pl.pallas_call(owner_kernel, out_shape=struct(devices, SUB, LANE), scratc...  12 us
    all_to_all x1, starting transfers between devices, shards(): lax.all_to_all(outgoing, 'dev', split_axis=0, concat_axis=0, tiled=True)  11.5 us
    all_to_all x1, waiting for transfers between devices, shards(): lax.all_to_all(outgoing, 'dev', split_axis=0, concat_axis=0, tiled=True)  6.67 us
    pallas_call x1, Pallas kernels, shards(): pl.pallas_call(home_kernel, out_shape=struct(9, owned), scratch_shapes=[p...  5.45 us
    reshape x3, local copies, waits for them, and re-layouts, shards(): pixel_grad.reshape(3, height, tiles, height).transpose(2, 0, 1, 3)  5.3 us
  transfers between devices with their start and end apart: 5, of which 2 were waited for; matrix products, arithmetic and copies ran while one was open for 3% of the time, Pallas kernels for 28%

profile of v1, /device:TPU:1, one launch (start us, length us, event | category | flops | bytes accessed | tf_op | source)
XLA Modules:
  0.0 195.6 jit_solution(8156463655891399111)
XLA Ops:
  0.6 12.0 %owner_gather.1 = f32[128,8,128]{2,1,0:T(8,128)} custom-call(s32[1,8192]{1,0:T(1,128)} %send.3, f32[2,2048]{1,0:T(2,128)} %centres.3, f32[2,2048]{1,0:T(2,128)} %conic.3, f32[1,2048]{1,0:T(1,128)} %rho.3, f32[1,2048]{1,0:T(1,128)} %opacity.3, f32[3,2048]{1,0:T(4,128)} %colors.1), custom_call_target="tpu_custom_call" | custom-call | tf_op jit(solution)/shard_map/owner_gather/pallas_call | solution.py:433
  12.6 11.5 %all-to-all-start = ((f32[128,8,128]{2,1,0:T(8,128)}), f32[128,8,128]{2,1,0:T(8,128)S(1)}, u32[]{:S(2)}, u32[]{:S(2)}) async-start(f32[128,8,128]{2,1,0:T(8,128)} %owner_gather.1), calls=%async_computation | async-start | bytes 1048576 | tf_op jit(solution)/shard_map/all_to_all | solution.py:439
  24.1 3.5 %collective-permute-start.2 = (f32[3,16,384]{2,1,0:T(8,128)}, f32[3,16,384]{2,1,0:T(8,128)S(1)}, u32[]{:S(2)}, u32[]{:S(2)}) collective-permute-start(f32[3,16,384]{2,1,0:T(8,128)} %t_centre.1), channel_id=1, source_target_pairs={{0,1},{1,2},{2,3},{3,4},{4,5},{5,6},{6,7},{7,8},{8,9},{9,10},{10,1... | collective-permute-start | bytes 221192 | tf_op jit(solution)/shard_map/ppermute | solution.py:479
  27.7 1.9 collective-permute-start.3
  29.6 0.9 reshape.22
  30.5 0.2 copy.13
  30.7 0.1 copy.14.lists
  30.8 6.7 %all-to-all-done.recv = f32[128,8,128]{2,1,0:T(8,128)S(1)} async-done(((f32[128,8,128]{2,1,0:T(8,128)}), f32[128,8,128]{2,1,0:T(8,128)S(1)}, u32[]{:S(2)}, u32[]{:S(2)}) %all-to-all-start) | async-done | bytes 524320 | tf_op jit(solution)/shard_map/all_to_all | solution.py:439
  37.4 0.0 copy-start
  37.4 0.8 copy-done
  38.2 0.0 copy-start.1
  38.2 1.0 copy-done.1
  39.3 55.0 %tile_forward.1 = (f32[24,3,256]{2,1,0:T(4,128)S(1)}, f32[24,3,8,256]{3,2,1,0:T(8,128)S(1)}, f32[24,8,256]{2,1,0:T(8,128)S(1)}, bf16[24,512,32]{2,1,0:T(8,128)(2,1)S(1)}) custom-call(s32[24,1,512]{2,1,0:T(1,128)S(1)} %copy.14.lists, f32[128,8,128]{2,1,0:T(8,128)S(1)} %copy-done.1), custom_call_target="tpu_custom_call" | custom-call | tf_op jit(solution)/shard_map/tile_forward/pallas_call | solution.py:444
  94.3 0.0 copy-start.2
  94.3 0.8 copy-done.2
  95.1 1.0 reshape.24
  96.2 2.1 %copy.16 = f32[3,16,24,16]{3,2,1,0:T(8,128)} copy(f32[3,16,24,16]{3,1,2,0:T(8,128)} %bitcast.12) | data formatting | bytes 147456 | tf_op jit(solution)/shard_map/transpose | solution.py:464
  98.2 1.3 reshape.25.centre
  99.5 0.0 copy-start.4
  99.5 3.4 %collective-permute-start = (f32[3,16,384]{2,1,0:T(8,128)S(1)}, f32[3,16,384]{2,1,0:T(8,128)S(1)}, u32[]{:S(2)}, u32[]{:S(2)}) collective-permute-start(f32[3,16,384]{2,1,0:T(8,128)S(1)} %reshape.25.centre), channel_id=1, source_target_pairs={{0,1},{1,2},{2,3},{3,4},{4,5},{5,6},{6,7},{7,8},{8,9},{9,10},{10,1... | collective-permute-start | bytes 221192 | tf_op jit(solution)/shard_map/ppermute | solution.py:478
  102.9 1.9 collective-permute-start.1
  104.8 0.7 pad_add_fusion.me
  105.5 0.0 collective-permute-done.2.t_before
  105.5 0.0 copy-start.5
  105.5 0.0 collective-permute-done.3.t_after
  105.5 0.0 collective-permute-done.before
  105.5 0.0 copy-start.6
  105.5 0.6 copy-done.6
  106.1 2.5 %collective-permute-done.1.after = f32[3,16,384]{2,1,0:T(8,128)} collective-permute-done((f32[3,16,384]{2,1,0:T(8,128)S(1)}, f32[3,16,384]{2,1,0:T(8,128)}, u32[]{:S(2)}, u32[]{:S(2)}) %collective-permute-start.1) | collective-permute-done | bytes 73760 | tf_op jit(solution)/shard_map/ppermute | solution.py:478
  108.7 0.0 copy-done.4
  108.7 0.0 copy-done.5
  108.7 5.0 %loss_gradient.1 = f32[3,16,384]{2,1,0:T(8,128)} custom-call(s32[2]{0:T(128)} %pad_add_fusion.me, f32[3,16,384]{2,1,0:T(8,128)} %copy-done.6, f32[3,16,384]{2,1,0:T(8,128)} %copy-done.4, f32[3,16,384]{2,1,0:T(8,128)} %collective-permute-done.1.after, f32[3,16,384]{2,1,0:T(8,128)} %copy-done.5, f32[3,16,384]{2,1,0:T(8,128)} %t_centre.1, ...), custom_call_target="tpu_custom_call" | custom-call | tf_op jit(solution)/shard_map/loss_gradient/pallas_call | solution.py:470
  113.7 1.9 reshape.26
  115.6 2.0 %copy.20 = f32[24,3,16,16]{3,2,1,0:T(8,128)} copy(f32[24,3,16,16]{3,0,2,1:T(8,128)} %bitcast.13) | data formatting | bytes 147456 | tf_op jit(solution)/shard_map/reshape | solution.py:481
  117.6 1.4 reshape.28.cot
  119.0 0.0 copy-start.3
  119.0 1.1 copy-done.3
  120.1 45.1 %tile_backward.1 = f32[128,8,128]{2,1,0:T(8,128)S(1)} custom-call(s32[24,1,512]{2,1,0:T(1,128)S(1)} %copy.14.lists, bf16[24,512,32]{2,1,0:T(8,128)(2,1)S(1)} %get-tuple-element.7.left_in, f32[24,3,256]{2,1,0:T(4,128)S(1)} %reshape.28.cot, f32[24,3,8,256]{3,2,1,0:T(8,128)S(1)} %copy-done.3, f32[24,8,256]{2,1,0:T(8,128)S(1)} %get-tuple-element.9.chunk_start), custom_call_target="tpu_custom_call" | custom-call | tf_op jit(solution)/shard_map/tile_backward/pallas_call | solution.py:484
  165.1 25.0 %all_to_all.10.back = f32[128,8,128]{2,1,0:T(8,128)} all-to-all(f32[128,8,128]{2,1,0:T(8,128)S(1)} %tile_backward.1), channel_id=1, replica_groups=mesh['dev'=128] {'dev'}, dimensions={0} | all-to-all | bytes 1048576 | tf_op jit(solution)/shard_map/all_to_all | solution.py:503
  190.2 5.4 %owner_scatter.1 = f32[9,2048]{1,0:T(8,128)} custom-call(f32[128,8,128]{2,1,0:T(8,128)} %all_to_all.10.back, s32[1,8192]{1,0:T(1,128)} %send.3, f32[2,2048]{1,0:T(2,128)} %centres.3, f32[2,2048]{1,0:T(2,128)} %conic.3, f32[1,2048]{1,0:T(1,128)} %rho.3, f32[1,2048]{1,0:T(1,128)} %opacity.3), custom_call_target="tpu_custom_call" | custom-call | tf_op jit(solution)/shard_map/owner_scatter/pallas_call | solution.py:504
  (1 shorter events, 0.0 us)
Async XLA Ops:
  12.6 24.8 %all-to-all-start = ((f32[128,8,128]{2,1,0:T(8,128)}), f32[128,8,128]{2,1,0:T(8,128)S(1)}, u32[]{:S(2)}, u32[]{:S(2)}) async-start(f32[128,8,128]{2,1,0:T(8,128)} %owner_gather.1), calls=%async_computation | async-start | bytes 1048576 | tf_op jit(solution)/shard_map/all_to_all | solution.py:439
  24.1 81.4 %collective-permute-start.2 = (f32[3,16,384]{2,1,0:T(8,128)}, f32[3,16,384]{2,1,0:T(8,128)S(1)}, u32[]{:S(2)}, u32[]{:S(2)}) collective-permute-start(f32[3,16,384]{2,1,0:T(8,128)} %t_centre.1), channel_id=1, source_target_pairs={{0,1},{1,2},{2,3},{3,4},{4,5},{5,6},{6,7},{7,8},{8,9},{9,10},{10,1... | collective-permute-start | bytes 221192 | tf_op jit(solution)/shard_map/ppermute | solution.py:479
  27.7 77.8 %collective-permute-start.3 = (f32[3,16,384]{2,1,0:T(8,128)}, f32[3,16,384]{2,1,0:T(8,128)}, u32[]{:S(2)}, u32[]{:S(2)}) collective-permute-start(f32[3,16,384]{2,1,0:T(8,128)} %t_centre.1), channel_id=1, source_target_pairs={{1,0},{2,1},{3,2},{4,3},{5,4},{6,5},{7,6},{8,7},{9,8},{10,9},{11,1... | collective-permute-start | bytes 221192 | tf_op jit(solution)/shard_map/ppermute | solution.py:479
  37.4 0.8 copy-start
  38.2 1.0 copy-start.1
  94.3 0.8 copy-start.2
  99.5 9.2 %copy-start.4 = (f32[3,16,384]{2,1,0:T(8,128)}, f32[3,16,384]{2,1,0:T(8,128)S(1)}, u32[]{:S(2)}) copy-start(f32[3,16,384]{2,1,0:T(8,128)S(1)} %reshape.25.centre) | copy-start | bytes 221188
  99.5 6.0 %collective-permute-start = (f32[3,16,384]{2,1,0:T(8,128)S(1)}, f32[3,16,384]{2,1,0:T(8,128)S(1)}, u32[]{:S(2)}, u32[]{:S(2)}) collective-permute-start(f32[3,16,384]{2,1,0:T(8,128)S(1)} %reshape.25.centre), channel_id=1, source_target_pairs={{0,1},{1,2},{2,3},{3,4},{4,5},{5,6},{6,7},{7,8},{8,9},{9,10},{10,1... | collective-permute-start | bytes 221192 | tf_op jit(solution)/shard_map/ppermute | solution.py:478
  102.9 5.8 %collective-permute-start.1 = (f32[3,16,384]{2,1,0:T(8,128)S(1)}, f32[3,16,384]{2,1,0:T(8,128)}, u32[]{:S(2)}, u32[]{:S(2)}) collective-permute-start(f32[3,16,384]{2,1,0:T(8,128)S(1)} %reshape.25.centre), channel_id=1, source_target_pairs={{1,0},{2,1},{3,2},{4,3},{5,4},{6,5},{7,6},{8,7},{9,8},{10,9},{11,1... | collective-permute-start | bytes 221192 | tf_op jit(solution)/shard_map/ppermute | solution.py:478
  105.5 3.2 %copy-start.5 = (f32[3,16,384]{2,1,0:T(8,128)}, f32[3,16,384]{2,1,0:T(8,128)S(1)}, u32[]{:S(2)}) copy-start(f32[3,16,384]{2,1,0:T(8,128)S(1)} %collective-permute-done.2.t_before) | copy-start | bytes 221188
  105.5 0.6 copy-start.6
  119.0 1.1 copy-start.3

commit v2 on v1

--- a/solution.py
+++ b/solution.py
@@ -40,6 +40,24 @@
     bx, by = a * cx + b * cy, c * cy + b * cx
     one = jnp.log(op) - 0.5 * (cx * bx + cy * by)
     return [LOG2E * k for k in (-0.5 * a, -b, -0.5 * c, bx, by, one)]
+
+
+def pick_tree(parts, bits):
+    if len(parts) == 1:
+        return parts[0]()
+    half = len(parts) // 2
+    return jnp.where(bits[half], pick_tree(parts[half:], bits), pick_tree(parts[:half], bits))
+
+
+def pick_nine(table, ninth, idx, row, blocks):
+    hi, lo = lax.shift_right_logical(idx, 7), lax.bitwise_and(idx, 127)
+    bits = {1 << k: lax.bitwise_and(hi, 1 << k) != 0 for k in range(blocks.bit_length() - 1)}
+    eight = pick_tree([lambda h=h: lane_pick(table(h), lo) for h in range(blocks)], bits)
+    coarse = {k // SUB: v for k, v in bits.items() if k >= SUB}
+    last = pick_tree(
+        [lambda v=v: lane_pick(ninth[v * SUB : (v + 1) * SUB, :], lo) for v in range(blocks // SUB)], coarse
+    )
+    return eight, sub_sum(jnp.where(lax.bitwise_and(hi, 7) == row, last, 0.0))
 
 
 def owner_kernel(send, centres, conic, rho, opacity, colors, out, table, ninth):
@@ -51,28 +69,79 @@
     blocks = table.shape[1] // LANE
     for h in range(blocks):
         ninth[h : h + 1, :] = colors[2:3, h * LANE : (h + 1) * LANE]
-    lane = iota((SUB, LANE), 1)
+    left = iota((SUB, LANE), 1) < 64
     row = iota((SUB, LANE), 0)
-
-    def pair(i, carry):
-        start = pl.multiple_of(i * LANE, LANE)
-        idx = jnp.broadcast_to(jnp.maximum(send[0:1, pl.ds(start, LANE)], 0), (SUB, LANE))
-        hi, lo = lax.shift_right_logical(idx, 7), lax.bitwise_and(idx, 127)
-        acc = jnp.zeros((SUB, LANE), F32)
-        for h in range(blocks):
-            acc = jnp.where(hi == h, lane_pick(table[:, h * LANE : (h + 1) * LANE], lo), acc)
-        last = jnp.zeros((SUB, LANE), F32)
-        for v in range(blocks // SUB):
-            got = lane_pick(ninth[v * SUB : (v + 1) * SUB, :], lo)
-            last = jnp.where(hi == row + v * SUB, got, last)
-        last = sub_sum(last)
-        left = lane < 64
-        top = jnp.where(row == 0, 1.0, 0.0)
-        out[2 * i] = jnp.where(left, acc, pltpu.roll(last, 64, 1) * top)
-        out[2 * i + 1] = jnp.where(left, pltpu.roll(acc, 64, 1), last * top)
+    top = jnp.where(row == 0, 1.0, 0.0)
+    step = 4
+
+    def pairs(ii, carry):
+        for k in range(step):
+            i = ii * step + k
+            start = pl.multiple_of(i * LANE, LANE)
+            idx = jnp.broadcast_to(jnp.maximum(send[0:1, pl.ds(start, LANE)], 0), (SUB, LANE))
+            eight, last = pick_nine(lambda h: table[:, h * LANE : (h + 1) * LANE], ninth, idx, row, blocks)
+            out[2 * i] = jnp.where(left, eight, pltpu.roll(last, 64, 1) * top)
+            out[2 * i + 1] = jnp.where(left, pltpu.roll(eight, 64, 1), last * top)
         return carry
 
-    lax.fori_loop(0, send.shape[1] // LANE, pair, 0)
+    lax.fori_loop(0, send.shape[1] // LANE // step, pairs, 0)
+
+
+MESH = pl.DeviceIdType.MESH
+
+
+def exchange_kernel(x, out, local_sem, send_sem, recv_sem):
+    me = lax.axis_index("dev")
+    n = lax.axis_size("dev")
+    barrier = pltpu.get_barrier_semaphore()
+
+    def greet(k, carry):
+        peer = lax.rem(me + k, n)
+        pl.semaphore_signal(barrier, inc=1, device_id=(peer,), device_id_type=MESH)
+        return carry
+
+    lax.fori_loop(1, n, greet, 0)
+    own = pltpu.make_async_copy(x.at[me], out.at[me], local_sem)
+    own.start()
+    pl.semaphore_wait(barrier, n - 1)
+
+    def start(k, carry):
+        peer = lax.rem(me + k, n)
+        pltpu.make_async_remote_copy(
+            src_ref=x.at[peer], dst_ref=out.at[me], send_sem=send_sem, recv_sem=recv_sem,
+            device_id=(peer,), device_id_type=MESH,
+        ).start()
+        return carry
+
+    lax.fori_loop(1, n, start, 0)
+    own.wait()
+    rest = pl.ds(0, n - 1)
+    pltpu.make_async_copy(x.at[rest], x.at[rest], send_sem).wait()
+    pltpu.make_async_copy(out.at[rest], out.at[rest], recv_sem).wait()
+
+
+def exchange(x, number):
+    return pl.pallas_call(
+        exchange_kernel,
+        out_shape=jax.ShapeDtypeStruct(x.shape, x.dtype),
+        in_specs=[pl.BlockSpec(memory_space=pltpu.VMEM)],
+        out_specs=pl.BlockSpec(memory_space=pltpu.VMEM),
+        scratch_shapes=[pltpu.SemaphoreType.DMA] * 3,
+        compiler_params=pltpu.CompilerParams(collective_id=number, has_side_effects=True),
+        name="exchange",
+    )(x)
+
+
+def block_transpose(x):
+    row = iota(x.shape, 0)
+    block = lax.shift_right_logical(iota(x.shape, 1), 4)
+    for d in (1, 2, 4):
+        low_row = lax.bitwise_and(row, d) == 0
+        low_block = lax.bitwise_and(block, d) == 0
+        down = pltpu.roll(pltpu.roll(x, SUB - d, 0), 16 * d, 1)
+        back = pltpu.roll(pltpu.roll(x, d, 0), LANE - 16 * d, 1)
+        x = jnp.where(low_row == low_block, x, jnp.where(low_row, down, back))
+    return x
 
 
 def basis_rows(lanes):
@@ -100,15 +169,20 @@
     return x
 
 
-def forward_kernel(lists, recv, rend, chunk_rend, chunk_start, left_out, table, ninth, cols, alphas):
-    lane = iota((SUB, LANE), 1)
+def segments(count):
+    groups = count // SUB // 2
+    return [(seg, j, (seg * groups + j) * SUB) for j in range(groups) for seg in range(2)]
+
+
+def forward_kernel(lists, recv, image, chunk_rend, chunk_start, left_out, table, ninth, cols, alphas, rends):
+    tile = pl.program_id(0)
     row = iota((SUB, LANE), 0)
 
-    @pl.when(pl.program_id(0) == 0)
+    @pl.when(tile == 0)
     def _():
         def pair(h, carry):
             even, odd = recv[2 * h], recv[2 * h + 1]
-            left = lane < 64
+            left = iota((SUB, LANE), 1) < 64
             table[h] = jnp.where(left, even, pltpu.roll(odd, 64, 1))
             both = jnp.where(left, pltpu.roll(even, 64, 1), odd)
             ninth[pl.ds(h, 1), :] = both[0:1, :]
@@ -118,20 +192,10 @@
 
     blocks = table.shape[0]
     count = lists.shape[2]
-
     for q in range(count // LANE):
         span = slice(q * LANE, (q + 1) * LANE)
         raw = jnp.broadcast_to(lists[0, 0:1, span], (SUB, LANE))
-        idx = jnp.maximum(raw, 0)
-        hi, lo = lax.shift_right_logical(idx, 7), lax.bitwise_and(idx, 127)
-        acc = jnp.zeros((SUB, LANE), F32)
-        for h in range(blocks):
-            acc = jnp.where(hi == h, lane_pick(table[h], lo), acc)
-        last = jnp.zeros((SUB, LANE), F32)
-        for v in range(blocks // SUB):
-            got = lane_pick(ninth[v * SUB : (v + 1) * SUB, :], lo)
-            last = jnp.where(hi == row + v * SUB, got, last)
-        last = sub_sum(last)
+        acc, last = pick_nine(lambda h: table[h], ninth, jnp.maximum(raw, 0), row, blocks)
         acc = jnp.where((row == 5) & (raw < 0), DEAD, acc)
         one, rest = split2(acc)
         two, three = split2(rest)
@@ -142,43 +206,47 @@
         stack = jnp.concatenate([one, two, three, more], axis=0)
         cols[span, :] = jnp.concatenate([stack, jnp.zeros((LANE - 32, LANE), F32)], axis=0).T
 
-    left = cols[:, 0:32].astype(BF16)
-    left_out[0] = left
     basis = stack_rows((basis_rows(256) + [None, None]) * 3, 32).astype(BF16)
-    alphas[...] = jnp.dot(left, basis, preferred_element_type=F32)
-
-    groups = count // SUB
-    step = 8
-
-    def first(j, product):
-        for k in range(step):
-            at = pl.ds(pl.multiple_of((j * step + k) * SUB, SUB), SUB)
-            alpha = jnp.exp2(alphas[at, :])
-            alphas[at, :] = alpha
-            product = product * (1.0 - alpha)
-        return product
-
-    product = lax.fori_loop(0, groups // step, first, jnp.ones((SUB, 256), F32))
-    trans = scan_sub(product)
-    chunk_start[0] = trans
-
-    def second(j, carry):
-        trans, red, green, blue = carry
-        for k in range(step):
-            at = pl.ds(pl.multiple_of((j * step + k) * SUB, SUB), SUB)
-            weight = trans * alphas[at, :]
-            trans = trans - weight
-            color = cols[at, :]
-            red = red + weight * color[:, 29:30]
-            green = green + weight * color[:, 30:31]
-            blue = blue + weight * color[:, 31:32]
-        return trans, red, green, blue
-
+    ones = jnp.ones((SUB, 256), F32)
+    product = [ones, ones]
+    piece = 64
+    for c in range(count // piece):
+        span = slice(c * piece, (c + 1) * piece)
+        left = cols[span, 0:32].astype(BF16)
+        left_out[0, span, :] = left
+        alpha = jnp.exp2(jnp.dot(left, basis, preferred_element_type=F32))
+        alphas[span, :] = alpha
+        rest = 1.0 - alpha
+        parts = [rest[k * SUB : (k + 1) * SUB, :] for k in range(piece // SUB)]
+        while len(parts) > 1:
+            parts = [parts[k] * parts[k + 1] for k in range(0, len(parts), 2)]
+        seg = 2 * c * piece // count
+        product[seg] = product[seg] * parts[0]
+
+    begin = scan_sub(product[0] * product[1])
+    trans = [begin, begin * product[0]]
     zero = jnp.zeros((SUB, 256), F32)
-    _, *channels = lax.fori_loop(0, groups // step, second, (trans, zero, zero, zero))
-    for ch, part in enumerate(channels):
-        chunk_rend[0, ch] = part
-        rend[0, ch : ch + 1, :] = sub_sum(part)[0:1, :]
+    sums = [[zero] * 3, [zero] * 3]
+    for seg in range(2):
+        chunk_start[0, seg] = trans[seg]
+    for seg, j, at in segments(count):
+        weight = trans[seg] * alphas[at : at + SUB, :]
+        trans[seg] = trans[seg] - weight
+        color = cols[at : at + SUB, :]
+        sums[seg] = [t + weight * color[:, 29 + ch : 30 + ch] for ch, t in enumerate(sums[seg])]
+    for ch in range(3):
+        for seg in range(2):
+            chunk_rend[0, ch, seg] = sums[seg][ch]
+        rends[ch, pl.ds(tile, 1), :] = sub_sum(sums[0][ch] + sums[1][ch])[0:1, :]
+
+    @pl.when(tile == pl.num_programs(0) - 1)
+    def _():
+        for ch in range(3):
+            for g in range(rends.shape[1] // SUB):
+                for h in range(2):
+                    image[ch, h * SUB : (h + 1) * SUB, g * LANE : (g + 1) * LANE] = block_transpose(
+                        rends[ch, g * SUB : (g + 1) * SUB, h * LANE : (h + 1) * LANE]
+                    )
 
 
 def taps_of():
@@ -271,23 +339,31 @@
     hot = onehot(lo, 256)
     hi8 = jnp.broadcast_to(hi, (SUB, span))
     own = iota((blocks, span), 0) == hi
-    total = None
+    left = []
     for values, extra in zip(split2(eight), split2(ninth)):
-        left = jnp.concatenate(
-            [spread(values, hi8, blocks), jnp.where(own, jnp.broadcast_to(extra, own.shape), 0.0)],
-            axis=0,
-        ).astype(BF16)
-        part = lax.dot_general(left, hot, NT, preferred_element_type=F32)
-        total = part if total is None else total + part
-    return total
-
-
-def backward_kernel(lists, left_in, cot, chunk_rend, chunk_start, out, fields, weights, halves, grads, slots):
+        left.append(spread(values, hi8, blocks))
+        left.append(jnp.where(own, jnp.broadcast_to(extra, own.shape), 0.0))
+    left = jnp.concatenate(left, axis=0).astype(BF16)
+    both = lax.dot_general(left, hot, NT, preferred_element_type=F32)
+    return both[: blocks * (SUB + 1), :] + both[blocks * (SUB + 1) :, :]
+
+
+def backward_kernel(lists, left_in, grad, chunk_rend, chunk_start, out, cots, halves, grads, slots):
     tile = pl.program_id(0)
-    count = lists.shape[2]
-    groups = count // SUB
-    step = 8
-    rows = [cot[0, ch : ch + 1, :] for ch in range(3)]
+    tiles = pl.num_programs(0)
+    count = left_in.shape[1]
+
+    @pl.when(tile == 0)
+    def _():
+        for ch in range(3):
+            for g in range(cots.shape[0] // SUB):
+                for h in range(2):
+                    span = slice(h * LANE, (h + 1) * LANE)
+                    block = block_transpose(grad[ch, h * SUB : (h + 1) * SUB, g * LANE : (g + 1) * LANE])
+                    for t in range(SUB):
+                        cots[g * SUB + t, ch : ch + 1, span] = block[t : t + 1, :]
+
+    rows = [cots[tile, ch : ch + 1, :] for ch in range(3)]
     ones, twos = zip(*(split2(r) for r in rows))
     basis = stack_rows((basis_rows(256) + [None, None]) * 3, 32)
     back = stack_rows(
@@ -295,74 +371,65 @@
         + [ones[0], ones[1], ones[2], ones[2], twos[2], twos[0], twos[1]], 32
     )
     right = jnp.concatenate([basis, back], axis=1).astype(BF16)
-    fields[...] = jnp.dot(left_in[0], right, preferred_element_type=F32)
-    start = chunk_start[0]
-
-    def first(j, trans):
-        for k in range(step):
-            at = pl.ds(pl.multiple_of((j * step + k) * SUB, SUB), SUB)
-            alpha = jnp.exp2(fields[at, 0:256])
-            fields[at, 0:256] = alpha
-            weight = trans * alpha
-            weights[at, :] = weight
-            trans = trans - weight
-        return trans
-
-    final = lax.fori_loop(0, groups // step, first, start)
-    behind = sum(chunk_rend[0, ch] * rows[ch] for ch in range(3))
+
+    inside = [sum(chunk_rend[0, ch, seg] * rows[ch] for ch in range(3)) for seg in range(2)]
     at8 = iota((SUB, 256), 0)
-    behind = jnp.where(at8 == SUB - 1, 0.0, pltpu.roll(behind, SUB - 1, 0))
+    later = inside[0] + inside[1]
+    later = jnp.where(at8 == SUB - 1, 0.0, pltpu.roll(later, SUB - 1, 0))
     for d in (1, 2, 4):
-        behind = behind + jnp.where(at8 < SUB - d, pltpu.roll(behind, SUB - d, 0), 0.0)
-    shade = behind / final
-
-    def second(jj, shade):
-        j = groups // step - 1 - jj
+        later = later + jnp.where(at8 < SUB - d, pltpu.roll(later, SUB - d, 0), 0.0)
+    behind = [later + inside[1] + inside[0], later + inside[1]]
+    trans = [chunk_start[0, seg] for seg in range(2)]
+
+    piece = 32
+    order = [c // 2 + (c % 2) * (count // piece // 2) for c in range(count // piece)]
+    for c in order:
+        seg = 2 * c * piece // count
+        field = jnp.dot(left_in[0, c * piece : (c + 1) * piece, :], right, preferred_element_type=F32)
+        alpha = jnp.exp2(field[:, 0:256])
+        ratio = alpha / (1.0 - alpha)
         parts = []
-        for k in reversed(range(step)):
-            at = pl.ds(pl.multiple_of((j * step + k) * SUB, SUB), SUB)
-            alpha, weight = fields[at, 0:256], weights[at, :]
-            diff = fields[at, 256:512] - shade
-            shade = shade + alpha * diff
-            parts.append((weight * diff, weight))
-        parts = parts[::-1]
-        for k in range(0, step, 2):
-            at = pl.ds(pl.multiple_of((j * step + k) * SUB, 2 * SUB), 2 * SUB)
-            for i in range(2):
-                value = jnp.concatenate([parts[k][i], parts[k + 1][i]], axis=0)
-                one = value.astype(BF16)
-                halves[at, 512 * i : 512 * i + 256] = one
-                halves[at, 512 * i + 256 : 512 * i + 512] = (value - one.astype(F32)).astype(BF16)
-        return shade
-
-    lax.fori_loop(0, groups // step, second, shade)
+        for k in range(piece // SUB):
+            span = slice(k * SUB, (k + 1) * SUB)
+            weight = trans[seg] * alpha[span]
+            trans[seg] = trans[seg] - weight
+            shown = weight * field[span, 256:512]
+            behind[seg] = behind[seg] - shown
+            parts.append((shown - ratio[span] * behind[seg], weight))
+        at = slice(c * piece, (c + 1) * piece)
+        value = jnp.concatenate([p[0] for p in parts], axis=0)
+        one = value.astype(BF16)
+        halves[at, 0:256] = one
+        halves[at, 256:512] = (value - one.astype(F32)).astype(BF16)
+        halves[at, 512:768] = jnp.concatenate([p[1] for p in parts], axis=0).astype(BF16)
+
     base = stack_rows(basis_rows(256), 16)
-    firsts = stack_rows([None] * 6 + list(ones) + list(twos), 16)
-    seconds = stack_rows([None] * 6 + list(ones), 16)
-    kernel = jnp.concatenate([base, base, firsts, seconds], axis=1).astype(BF16)
+    colours = stack_rows([None] * 6 + list(ones) + list(twos), 16)
+    kernel = jnp.concatenate([base, base, colours], axis=1).astype(BF16)
     found = lax.dot_general(kernel, halves[...], NT, preferred_element_type=F32)
     low = found[8:16, :]
     at16 = iota(low.shape, 0)
     top = found[0:8, :] + jnp.where(at16 >= 6, pltpu.roll(low, 5, 0), 0.0)
-    last = low[0:1, :] + low[3:4, :]
-    idx = jnp.maximum(lists[0], 0)
-    blocks = slots.shape[0] // (SUB + 1)
-    part = scatter_block(top, last, idx, blocks)
-
-    @pl.when(tile == 0)
+    grads[tile, 0:8, :] = top
+    grads[tile, 8:9, :] = low[0:1, :] + low[3:4, :]
+
+    @pl.when(tile == tiles - 1)
     def _():
-        slots[...] = part
-
-    @pl.when(tile > 0)
-    def _():
-        slots[...] = slots[...] + part
-
-    @pl.when(tile == pl.num_programs(0) - 1)
-    def _():
-        lane = iota((SUB, LANE), 1)
-        left = lane < 64
+        slots[...] = jnp.zeros_like(slots)
+        blocks = slots.shape[0] // (SUB + 1)
+        per = 2
+
+        def chunk(c, carry):
+            each = [c * per + k for k in range(per)]
+            idx = jnp.concatenate([jnp.maximum(lists[t], 0) for t in each], axis=1)
+            eight = jnp.concatenate([grads[t, 0:8, :] for t in each], axis=1)
+            ninth = jnp.concatenate([grads[t, 8:9, :] for t in each], axis=1)
+            slots[...] = slots[...] + scatter_block(eight, ninth, idx, blocks)
+            return carry
+
+        lax.fori_loop(0, cots.shape[0] // per, chunk, 0)
+        left = iota((SUB, LANE), 1) < 64
         top8 = jnp.where(iota((SUB, LANE), 0) == 0, 1.0, 0.0)
-
         for h in range(blocks):
             for half in range(2):
                 span = slice(half * LANE, (half + 1) * LANE)
@@ -436,20 +503,21 @@
         scratch_shapes=[pltpu.VMEM((SUB, owned), F32), pltpu.VMEM((owned // LANE, LANE), F32)],
         name="owner_gather",
     )(send_rows, centres, conic, rho, opacity, colors)
-    incoming = lax.all_to_all(outgoing, "dev", split_axis=0, concat_axis=0, tiled=True)
-
     lists = tile_lists.reshape(tiles, SUB, count // SUB).transpose(0, 2, 1).reshape(tiles, 1, count)
+    incoming = exchange(outgoing, 0)
     whole = lambda *shape: pl.BlockSpec(shape, lambda t: (0,) * len(shape))
     per_tile = lambda *shape: pl.BlockSpec((1,) + shape, lambda t: (t,) + (0,) * len(shape))
-    rend, chunk_rend, chunk_start, left = pl.pallas_call(
+    image, chunk_rend, chunk_start, left = pl.pallas_call(
         forward_kernel,
         grid=(tiles,),
         in_specs=[per_tile(1, count), whole(devices, SUB, LANE)],
-        out_specs=[per_tile(3, pixels), per_tile(3, SUB, pixels), per_tile(SUB, pixels), per_tile(count, 32)],
+        out_specs=[
+            whole(3, height, width), per_tile(3, 2, SUB, pixels), per_tile(2, SUB, pixels), per_tile(count, 32)
+        ],
         out_shape=[
-            struct(tiles, 3, pixels),
-            struct(tiles, 3, SUB, pixels),
-            struct(tiles, SUB, pixels),
+            struct(3, height, width),
+            struct(tiles, 3, 2, SUB, pixels),
+            struct(tiles, 2, SUB, pixels),
             struct(tiles, count, 32, dtype=BF16),
         ],
         scratch_shapes=[
@@ -457,11 +525,11 @@
             pltpu.VMEM((devices // 2, LANE), F32),
             pltpu.VMEM((count, LANE), F32),
             pltpu.VMEM((count, pixels), F32),
+            pltpu.VMEM((3, tiles, pixels), F32),
         ],
         compiler_params=params,
         name="tile_forward",
     )(lists, incoming)
-    image = rend.reshape(tiles, 3, height, height).transpose(1, 2, 0, 3).reshape(3, height, width)
 
     up = [(i, i + 1) for i in range(devices - 1)]
     down = [(j, i) for i, j in up]
@@ -478,29 +546,26 @@
         lax.ppermute(image, "dev", up), image, lax.ppermute(image, "dev", down),
         lax.ppermute(target, "dev", up), target, lax.ppermute(target, "dev", down),
     )
-    cot = pixel_grad.reshape(3, height, tiles, height).transpose(2, 0, 1, 3).reshape(tiles, 3, pixels)
-
     hi_blocks = devices * 64 // 256
     slot_grads = pl.pallas_call(
         backward_kernel,
         grid=(tiles,),
         in_specs=[
-            per_tile(1, count), per_tile(count, 32), per_tile(3, pixels),
-            per_tile(3, SUB, pixels), per_tile(SUB, pixels),
+            whole(tiles, 1, count), per_tile(count, 32), whole(3, height, width),
+            per_tile(3, 2, SUB, pixels), per_tile(2, SUB, pixels),
         ],
         out_specs=whole(devices, SUB, LANE),
         out_shape=struct(devices, SUB, LANE),
         scratch_shapes=[
-            pltpu.VMEM((count, 2 * pixels), F32),
-            pltpu.VMEM((count, pixels), F32),
-            pltpu.VMEM((count, 4 * pixels), BF16),
-            pltpu.VMEM((16, count), F32),
+            pltpu.VMEM((tiles, 3, pixels), F32),
+            pltpu.VMEM((count, 3 * pixels), BF16),
+            pltpu.VMEM((tiles, 16, count), F32),
             pltpu.VMEM((hi_blocks * (SUB + 1), 256), F32),
         ],
         compiler_params=params,
         name="tile_backward",
-    )(lists, left, cot, chunk_rend, chunk_start)
-    returned = lax.all_to_all(slot_grads, "dev", split_axis=0, concat_axis=0, tiled=True)
+    )(lists, left, pixel_grad, chunk_rend, chunk_start)
+    returned = exchange(slot_grads, 1)
     grads = pl.pallas_call(
         home_kernel,
         out_shape=struct(9, owned),

time: 196 us -> 136 us (0.69)
  blocking collectives: 25 us -> 0 us
  starting transfers between devices: 22.2 us -> 9.87 us
  Pallas kernels: 123 us -> 113 us
  local copies, waits for them, and re-layouts: 15.2 us -> 8.54 us
  waiting for transfers between devices: 9.2 us -> 3.28 us
    pallas_call x1, Pallas kernels: 55 us -> 27.9 us  [shards(): pl.pallas_call(forward_kernel, grid=(tiles,), in_specs=[per_tile(1, count...]
    all_to_all x1 -> x0, blocking collectives: 25 us -> none  [shards(): lax.all_to_all(slot_grads, 'dev', split_axis=0, concat_axis=0, tiled=True)]
    pallas_call x1 -> x3, Pallas kernels: 45.1 us -> 69.5 us  [the longest x2 47.8 us: exchange(): pl.pallas_call(exchange_kernel, out_shape=jax.ShapeDtypeStruct(x.shape, x...]
    all_to_all x1 -> x0, starting transfers between devices: 11.5 us -> none  [shards(): lax.all_to_all(outgoing, 'dev', split_axis=0, concat_axis=0, tiled=True)]
    reshape x5 -> x0, local copies, waits for them, and re-layouts: 7.58 us -> none  [the longest x3 5.3 us: shards(): pixel_grad.reshape(3, height, tiles, height).transpose(2, 0, 1, 3)]
    all_to_all x1 -> x0, waiting for transfers between devices: 6.67 us -> none  [shards(): lax.all_to_all(outgoing, 'dev', split_axis=0, concat_axis=0, tiled=True)]
    pallas_call x1, Pallas kernels: 12 us -> 5.72 us  [shards(): pl.pallas_call(owner_kernel, out_shape=struct(devices, SUB, LANE), scratc...]
    ppermute x1, waiting for transfers between devices: 0.01 us -> 3.27 us  [shards(): lax.ppermute(target, 'dev', down)]
  transfers between devices with their start and end apart: 5 -> 4, of which waited for: 2 -> 1; matrix products, arithmetic and copies ran while one was open for 3% -> 0% of each run, Pallas kernels for 28% -> 0%
where the time goes in v2:
time: 136 us
  Pallas kernels  113 us (83%)
  starting transfers between devices  9.87 us (7%)
  local copies, waits for them, and re-layouts  8.54 us (6%)
  waiting for transfers between devices  3.28 us (2%)
    pallas_call x2, Pallas kernels, exchange(): pl.pallas_call(exchange_kernel, out_shape=jax.ShapeDtypeStruct(x.shape, x...  47.8 us
    pallas_call x1, Pallas kernels, shards(): pl.pallas_call(forward_kernel, grid=(tiles,), in_specs=[per_tile(1, count...  27.9 us
    pallas_call x1, Pallas kernels, shards(): pl.pallas_call(backward_kernel, grid=(tiles,), in_specs=[whole(tiles, 1,...  21.7 us
    unnamed x22, local copies, waits for them, and re-layouts  7.39 us
    pallas_call x1, Pallas kernels, shards(): pl.pallas_call(owner_kernel, out_shape=struct(devices, SUB, LANE), scratc...  5.72 us
    pallas_call x1, Pallas kernels, shards(): pl.pallas_call(loss_kernel, in_specs=[pl.BlockSpec(memory_space=pltpu.SME...  5.03 us
    pallas_call x1, Pallas kernels, shards(): pl.pallas_call(home_kernel, out_shape=struct(9, owned), scratch_shapes=[p...  4.58 us
    ppermute x1, starting transfers between devices, shards(): lax.ppermute(target, 'dev', up)  3.63 us
  transfers between devices with their start and end apart: 4, of which 1 were waited for; matrix products, arithmetic and copies ran while one was open for 0% of the time, Pallas kernels for 0%

profile of v2, /device:TPU:1, one launch (start us, length us, event | category | flops | bytes accessed | tf_op | source)
XLA Modules:
  0.0 135.8 jit_solution(7395249036436314123)
XLA Ops:
  0.6 0.9 reshape.10
  1.5 0.2 copy.11
  1.7 0.1 copy.12.lists
  1.8 5.7 %owner_gather.1.x = f32[128,8,128]{2,1,0:T(8,128)} custom-call(s32[1,8192]{1,0:T(1,128)} %send.3, f32[2,2048]{1,0:T(2,128)} %centres.3, f32[2,2048]{1,0:T(2,128)} %conic.3, f32[1,2048]{1,0:T(1,128)} %rho.3, f32[1,2048]{1,0:T(1,128)} %opacity.3, f32[3,2048]{1,0:T(4,128)} %colors.1), custom_call_target="tpu_custom_call" | custom-call | tf_op jit(solution)/shard_map/owner_gather/pallas_call | solution.py:500
  7.5 21.1 %exchange.2.recv = f32[128,8,128]{2,1,0:T(8,128)} custom-call(f32[128,8,128]{2,1,0:T(8,128)} %owner_gather.1.x), custom_call_target="tpu_custom_call" | custom-call | tf_op jit(solution)/shard_map/exchange/pallas_call | solution.py:124
  28.6 0.0 copy-start
  28.6 1.0 copy-done
  29.7 27.9 %tile_forward.1 = (f32[3,16,384]{2,1,0:T(8,128)}, f32[24,3,2,8,256]{4,3,2,1,0:T(8,128)S(1)}, f32[24,2,8,256]{3,2,1,0:T(8,128)S(1)}, bf16[24,512,32]{2,1,0:T(8,128)(2,1)S(1)}) custom-call(s32[24,1,512]{2,1,0:T(1,128)S(1)} %copy.12.lists, f32[128,8,128]{2,1,0:T(8,128)S(1)} %copy-done), custom_call_target="tpu_custom_call" | custom-call | tf_op jit(solution)/shard_map/tile_forward/pallas_call | solution.py:510
  57.6 0.0 copy-start.2
  57.6 1.0 copy-done.2
  58.6 0.0 copy-start.4
  58.6 0.8 copy-done.4
  59.4 2.4 %collective-permute-start = (f32[3,16,384]{2,1,0:T(8,128)}, f32[3,16,384]{2,1,0:T(8,128)S(1)}, u32[]{:S(2)}, u32[]{:S(2)}) collective-permute-start(f32[3,16,384]{2,1,0:T(8,128)} %get-tuple-element.4.centre), channel_id=1, source_target_pairs={{0,1},{1,2},{2,3},{3,4},{4,5},{5,6},{6,7},{7,8},{8,9},{9,10},{10,1... | collective-permute-start | bytes 221192 | tf_op jit(solution)/shard_map/ppermute | solution.py:546
  61.7 1.9 %collective-permute-start.1 = (f32[3,16,384]{2,1,0:T(8,128)}, f32[3,16,384]{2,1,0:T(8,128)S(1)}, u32[]{:S(2)}, u32[]{:S(2)}) collective-permute-start(f32[3,16,384]{2,1,0:T(8,128)} %get-tuple-element.4.centre), channel_id=1, source_target_pairs={{1,0},{2,1},{3,2},{4,3},{5,4},{6,5},{7,6},{8,7},{9,8},{10,9},{11,1... | collective-permute-start | bytes 221192 | tf_op jit(solution)/shard_map/ppermute | solution.py:546
  63.7 3.6 %collective-permute-start.2 = (f32[3,16,384]{2,1,0:T(8,128)}, f32[3,16,384]{2,1,0:T(8,128)S(1)}, u32[]{:S(2)}, u32[]{:S(2)}) collective-permute-start(f32[3,16,384]{2,1,0:T(8,128)} %t_centre.1), channel_id=1, source_target_pairs={{0,1},{1,2},{2,3},{3,4},{4,5},{5,6},{6,7},{7,8},{8,9},{9,10},{10,1... | collective-permute-start | bytes 221192 | tf_op jit(solution)/shard_map/ppermute | solution.py:547
  67.3 1.9 %collective-permute-start.3 = (f32[3,16,384]{2,1,0:T(8,128)}, f32[3,16,384]{2,1,0:T(8,128)S(1)}, u32[]{:S(2)}, u32[]{:S(2)}) collective-permute-start(f32[3,16,384]{2,1,0:T(8,128)} %t_centre.1), channel_id=1, source_target_pairs={{1,0},{2,1},{3,2},{4,3},{5,4},{6,5},{7,6},{8,7},{9,8},{10,9},{11,1... | collective-permute-start | bytes 221192 | tf_op jit(solution)/shard_map/ppermute | solution.py:547
  69.3 0.6 pad_add_fusion.me
  69.9 0.0 collective-permute-done.before
  69.9 0.0 copy-start.7
  69.9 0.0 collective-permute-done.1.after
  69.9 0.0 copy-start.8
  69.9 0.0 collective-permute-done.2.t_before
  69.9 0.0 copy-start.9
  69.9 3.3 %collective-permute-done.3.t_after = f32[3,16,384]{2,1,0:T(8,128)S(1)} collective-permute-done((f32[3,16,384]{2,1,0:T(8,128)}, f32[3,16,384]{2,1,0:T(8,128)S(1)}, u32[]{:S(2)}, u32[]{:S(2)}) %collective-permute-start.3) | collective-permute-done | bytes 73760 | tf_op jit(solution)/shard_map/ppermute | solution.py:547
  73.2 0.0 copy-done.7
  73.2 0.0 copy-done.8
  73.2 0.0 copy-done.9
  73.2 0.0 copy-start.10
  73.2 0.6 copy-done.10
  73.8 5.0 %loss_gradient.1.grad = f32[3,16,384]{2,1,0:T(8,128)} custom-call(s32[2]{0:T(128)} %pad_add_fusion.me, f32[3,16,384]{2,1,0:T(8,128)} %copy-done.7, f32[3,16,384]{2,1,0:T(8,128)} %get-tuple-element.4.centre, f32[3,16,384]{2,1,0:T(8,128)} %copy-done.8, f32[3,16,384]{2,1,0:T(8,128)} %copy-done.9, f32[3,16,384]{2,1,0:T(8,128)} %t_centre.1, f32[3,16,384]{2,1,0:T(8,128)} %copy-done.10), custom_call_target="tpu_custom_call" | custom-call | tf_op jit(solution)/shard_map/loss_gradient/pallas_call | solution.py:538
  78.9 0.0 copy-start.3
  78.9 1.3 copy-done.3
  80.1 0.0 copy-start.5
  80.1 1.0 copy-done.5
  81.1 0.0 copy-start.6
  81.1 0.9 copy-done.6
  82.0 21.7 %tile_backward.1.x = f32[128,8,128]{2,1,0:T(8,128)S(1)} custom-call(s32[24,1,512]{2,1,0:T(1,128)S(1)} %copy.12.lists, bf16[24,512,32]{2,1,0:T(8,128)(2,1)S(1)} %get-tuple-element.7.left_in, f32[3,16,384]{2,1,0:T(8,128)S(1)} %copy-done.6, f32[24,3,2,8,256]{4,3,2,1,0:T(8,128)S(1)} %copy-done.3, f32[24,2,8,256]{3,2,1,0:T(8,128)S(1)} %copy-done.5), custom_call_target="tpu_custom_call" | custom-call | tf_op jit(solution)/shard_map/tile_backward/pallas_call | solution.py:550
  103.7 0.0 copy-start.1
  103.7 0.8 copy-done.1
  104.5 26.7 %exchange.3.back = f32[128,8,128]{2,1,0:T(8,128)} custom-call(f32[128,8,128]{2,1,0:T(8,128)} %copy-done.1), custom_call_target="tpu_custom_call" | custom-call | tf_op jit(solution)/shard_map/exchange/pallas_call | solution.py:124
  131.2 4.6 %owner_scatter.1 = f32[9,2048]{1,0:T(8,128)} custom-call(f32[128,8,128]{2,1,0:T(8,128)} %exchange.3.back, s32[1,8192]{1,0:T(1,128)} %send.3, f32[2,2048]{1,0:T(2,128)} %centres.3, f32[2,2048]{1,0:T(2,128)} %conic.3, f32[1,2048]{1,0:T(1,128)} %rho.3, f32[1,2048]{1,0:T(1,128)} %opacity.3), custom_call_target="tpu_custom_call" | custom-call | tf_op jit(solution)/shard_map/owner_scatter/pallas_call | solution.py:569
Async XLA Ops:
  28.6 1.0 copy-start
  57.6 1.0 copy-start.2
  58.6 0.8 copy-start.4
  59.4 10.5 %collective-permute-start = (f32[3,16,384]{2,1,0:T(8,128)}, f32[3,16,384]{2,1,0:T(8,128)S(1)}, u32[]{:S(2)}, u32[]{:S(2)}) collective-permute-start(f32[3,16,384]{2,1,0:T(8,128)} %get-tuple-element.4.centre), channel_id=1, source_target_pairs={{0,1},{1,2},{2,3},{3,4},{4,5},{5,6},{6,7},{7,8},{8,9},{9,10},{10,1... | collective-permute-start | bytes 221192 | tf_op jit(solution)/shard_map/ppermute | solution.py:546
  61.7 8.2 %collective-permute-start.1 = (f32[3,16,384]{2,1,0:T(8,128)}, f32[3,16,384]{2,1,0:T(8,128)S(1)}, u32[]{:S(2)}, u32[]{:S(2)}) collective-permute-start(f32[3,16,384]{2,1,0:T(8,128)} %get-tuple-element.4.centre), channel_id=1, source_target_pairs={{1,0},{2,1},{3,2},{4,3},{5,4},{6,5},{7,6},{8,7},{9,8},{10,9},{11,1... | collective-permute-start | bytes 221192 | tf_op jit(solution)/shard_map/ppermute | solution.py:546
  63.7 6.2 %collective-permute-start.2 = (f32[3,16,384]{2,1,0:T(8,128)}, f32[3,16,384]{2,1,0:T(8,128)S(1)}, u32[]{:S(2)}, u32[]{:S(2)}) collective-permute-start(f32[3,16,384]{2,1,0:T(8,128)} %t_centre.1), channel_id=1, source_target_pairs={{0,1},{1,2},{2,3},{3,4},{4,5},{5,6},{6,7},{7,8},{8,9},{9,10},{10,1... | collective-permute-start | bytes 221192 | tf_op jit(solution)/shard_map/ppermute | solution.py:547
  67.3 5.9 %collective-permute-start.3 = (f32[3,16,384]{2,1,0:T(8,128)}, f32[3,16,384]{2,1,0:T(8,128)S(1)}, u32[]{:S(2)}, u32[]{:S(2)}) collective-permute-start(f32[3,16,384]{2,1,0:T(8,128)} %t_centre.1), channel_id=1, source_target_pairs={{1,0},{2,1},{3,2},{4,3},{5,4},{6,5},{7,6},{8,7},{9,8},{10,9},{11,1... | collective-permute-start | bytes 221192 | tf_op jit(solution)/shard_map/ppermute | solution.py:547
  69.9 3.3 %copy-start.7 = (f32[3,16,384]{2,1,0:T(8,128)}, f32[3,16,384]{2,1,0:T(8,128)S(1)}, u32[]{:S(2)}) copy-start(f32[3,16,384]{2,1,0:T(8,128)S(1)} %collective-permute-done.before) | copy-start | bytes 221188
  69.9 3.3 %copy-start.8 = (f32[3,16,384]{2,1,0:T(8,128)}, f32[3,16,384]{2,1,0:T(8,128)S(1)}, u32[]{:S(2)}) copy-start(f32[3,16,384]{2,1,0:T(8,128)S(1)} %collective-permute-done.1.after) | copy-start | bytes 221188
  69.9 3.3 %copy-start.9 = (f32[3,16,384]{2,1,0:T(8,128)}, f32[3,16,384]{2,1,0:T(8,128)S(1)}, u32[]{:S(2)}) copy-start(f32[3,16,384]{2,1,0:T(8,128)S(1)} %collective-permute-done.2.t_before) | copy-start | bytes 221188
  73.2 0.6 copy-start.10
  78.9 1.3 copy-start.3
  80.1 1.0 copy-start.5
  81.1 0.9 copy-start.6
  103.7 0.8 copy-start.1

commit v3 on v2

--- a/solution.py
+++ b/solution.py
@@ -71,7 +71,6 @@
         ninth[h : h + 1, :] = colors[2:3, h * LANE : (h + 1) * LANE]
     left = iota((SUB, LANE), 1) < 64
     row = iota((SUB, LANE), 0)
-    top = jnp.where(row == 0, 1.0, 0.0)
     step = 4
 
     def pairs(ii, carry):
@@ -80,56 +79,127 @@
             start = pl.multiple_of(i * LANE, LANE)
             idx = jnp.broadcast_to(jnp.maximum(send[0:1, pl.ds(start, LANE)], 0), (SUB, LANE))
             eight, last = pick_nine(lambda h: table[:, h * LANE : (h + 1) * LANE], ninth, idx, row, blocks)
-            out[2 * i] = jnp.where(left, eight, pltpu.roll(last, 64, 1) * top)
-            out[2 * i + 1] = jnp.where(left, pltpu.roll(eight, 64, 1), last * top)
+            out[2 * i], out[2 * i + 1] = pack_pair(eight, last, left, row)
         return carry
 
     lax.fori_loop(0, send.shape[1] // LANE // step, pairs, 0)
 
 
 MESH = pl.DeviceIdType.MESH
-
-
-def exchange_kernel(x, out, local_sem, send_sem, recv_sem):
+USED = 5
+
+
+def pack_pair(eight, last, left, row):
+    low = pltpu.roll(eight, 4, 0)
+    even = jnp.where(left, eight, pltpu.roll(low, 64, 1))
+    odd = jnp.where(left, pltpu.roll(eight, 64, 1), low)
+    return jnp.where(row < 4, even, last), jnp.where(row < 4, odd, pltpu.roll(last, 64, 1))
+
+
+def unpack_pair(even, odd, left, row):
+    high = jnp.where(left, even, pltpu.roll(odd, 64, 1))
+    low = jnp.where(left, pltpu.roll(even, 64, 1), odd)
+    return jnp.where(row < 4, high, pltpu.roll(low, 4, 0)), high[4:5, :]
+
+
+def greet_all(n, me):
+    barrier = pltpu.get_barrier_semaphore()
+
+    def greet(k, carry):
+        pl.semaphore_signal(barrier, inc=1, device_id=(lax.rem(me + k, n),), device_id_type=MESH)
+        return carry
+
+    lax.fori_loop(1, n, greet, 0)
+    return barrier
+
+
+def halo_copies(n, me, strip, before, after, send_sem, recv_sem):
+    return [
+        pltpu.make_async_remote_copy(
+            src_ref=strip, dst_ref=to, send_sem=send_sem.at[k], recv_sem=recv_sem.at[k],
+            device_id=(lax.rem(me + hop, n),), device_id_type=MESH,
+        )
+        for k, (hop, to) in enumerate(((1, before), (n - 1, after)))
+    ]
+
+
+def exchange_kernel(halo, *refs):
+    if halo:
+        x, strip, out, before, after, local_sem, send_sem, recv_sem, halo_send, halo_recv = refs
+    else:
+        x, out, local_sem, send_sem, recv_sem = refs
+    me = lax.axis_index("dev")
+    n = lax.axis_size("dev")
+    rows = pl.ds(0, USED)
+    barrier = greet_all(n, me)
+    own = pltpu.make_async_copy(x.at[me, rows], out.at[me, rows], local_sem)
+    own.start()
+    pl.semaphore_wait(barrier, n - 1)
+
+    def start(k, carry):
+        peer = lax.rem(me + k, n)
+        pltpu.make_async_remote_copy(
+            src_ref=x.at[peer, rows], dst_ref=out.at[me, rows], send_sem=send_sem, recv_sem=recv_sem,
+            device_id=(peer,), device_id_type=MESH,
+        ).start()
+        return carry
+
+    lax.fori_loop(1, n, start, 0)
+    copies = halo_copies(n, me, strip, before, after, halo_send, halo_recv) if halo else []
+    for copy in copies:
+        copy.start()
+    own.wait()
+    rest = pl.ds(0, n - 1)
+    pltpu.make_async_copy(x.at[rest, rows], x.at[rest, rows], send_sem).wait()
+    pltpu.make_async_copy(out.at[rest, rows], out.at[rest, rows], recv_sem).wait()
+    for copy in copies:
+        copy.wait()
+
+
+def comm_params(number):
+    return pltpu.CompilerParams(collective_id=number, has_side_effects=True, vmem_limit_bytes=4 << 20)
+
+
+def exchange(x, number, strip=None):
+    vmem = pl.BlockSpec(memory_space=pltpu.VMEM)
+    halo = strip is not None
+    like = lambda v: jax.ShapeDtypeStruct(v.shape, v.dtype)
+    return pl.pallas_call(
+        functools.partial(exchange_kernel, halo),
+        out_shape=[like(x)] + [like(strip)] * 2 if halo else like(x),
+        in_specs=[vmem] * (2 if halo else 1),
+        out_specs=[vmem] * 3 if halo else vmem,
+        scratch_shapes=[pltpu.SemaphoreType.DMA] * 3 + [pltpu.SemaphoreType.DMA((2,))] * (2 if halo else 0),
+        compiler_params=comm_params(number),
+        name="exchange",
+    )(*([x, strip] if halo else [x]))
+
+
+def halo_kernel(strip, before, after, send_sem, recv_sem):
     me = lax.axis_index("dev")
     n = lax.axis_size("dev")
     barrier = pltpu.get_barrier_semaphore()
-
-    def greet(k, carry):
-        peer = lax.rem(me + k, n)
-        pl.semaphore_signal(barrier, inc=1, device_id=(peer,), device_id_type=MESH)
-        return carry
-
-    lax.fori_loop(1, n, greet, 0)
-    own = pltpu.make_async_copy(x.at[me], out.at[me], local_sem)
-    own.start()
-    pl.semaphore_wait(barrier, n - 1)
-
-    def start(k, carry):
-        peer = lax.rem(me + k, n)
-        pltpu.make_async_remote_copy(
-            src_ref=x.at[peer], dst_ref=out.at[me], send_sem=send_sem, recv_sem=recv_sem,
-            device_id=(peer,), device_id_type=MESH,
-        ).start()
-        return carry
-
-    lax.fori_loop(1, n, start, 0)
-    own.wait()
-    rest = pl.ds(0, n - 1)
-    pltpu.make_async_copy(x.at[rest], x.at[rest], send_sem).wait()
-    pltpu.make_async_copy(out.at[rest], out.at[rest], recv_sem).wait()
-
-
-def exchange(x, number):
+    for hop in (1, n - 1):
+        pl.semaphore_signal(barrier, inc=1, device_id=(lax.rem(me + hop, n),), device_id_type=MESH)
+    pl.semaphore_wait(barrier, 2)
+    copies = halo_copies(n, me, strip, before, after, send_sem, recv_sem)
+    for copy in copies:
+        copy.start()
+    for copy in copies:
+        copy.wait()
+
+
+def halo_strips(strip, number):
+    vmem = pl.BlockSpec(memory_space=pltpu.VMEM)
     return pl.pallas_call(
-        exchange_kernel,
-        out_shape=jax.ShapeDtypeStruct(x.shape, x.dtype),
-        in_specs=[pl.BlockSpec(memory_space=pltpu.VMEM)],
-        out_specs=pl.BlockSpec(memory_space=pltpu.VMEM),
-        scratch_shapes=[pltpu.SemaphoreType.DMA] * 3,
-        compiler_params=pltpu.CompilerParams(collective_id=number, has_side_effects=True),
-        name="exchange",
-    )(x)
+        halo_kernel,
+        out_shape=[jax.ShapeDtypeStruct(strip.shape, strip.dtype)] * 2,
+        in_specs=[vmem],
+        out_specs=[vmem] * 2,
+        scratch_shapes=[pltpu.SemaphoreType.DMA((2,))] * 2,
+        compiler_params=comm_params(number),
+        name="halo",
+    )(strip)
 
 
 def block_transpose(x):
@@ -181,11 +251,8 @@
     @pl.when(tile == 0)
     def _():
         def pair(h, carry):
-            even, odd = recv[2 * h], recv[2 * h + 1]
             left = iota((SUB, LANE), 1) < 64
-            table[h] = jnp.where(left, even, pltpu.roll(odd, 64, 1))
-            both = jnp.where(left, pltpu.roll(even, 64, 1), odd)
-            ninth[pl.ds(h, 1), :] = both[0:1, :]
+            table[h], ninth[pl.ds(h, 1), :] = unpack_pair(recv[2 * h], recv[2 * h + 1], left, row)
             return carry
 
         lax.fori_loop(0, recv.shape[0] // 2, pair, 0)
@@ -276,10 +343,10 @@
     return total
 
 
-def loss_kernel(me, before, centre, after, t_before, t_centre, t_after, grad, pads, maps):
+def loss_kernel(before, centre, after, t_before, t_centre, t_after, grad, pads, maps):
     height = centre.shape[1]
-    mine = me[0]
-    total_rows = me[1]
+    mine = lax.axis_index("dev")
+    total_rows = lax.axis_size("dev") * height
     width = centre.shape[2]
     at = iota((2 * height, width), 0) - height // 2 + mine * height
     inside = (at >= 0) & (at < total_rows)
@@ -287,6 +354,9 @@
         for i, (r, t) in enumerate(((before, t_before), (centre, t_centre), (after, t_after))):
             span = slice(i * height, (i + 1) * height)
             rr, tt = r[ch], t[ch]
+            if i != 1:
+                keep = mine > 0 if i == 0 else mine < total_rows // height - 1
+                rr, tt = jnp.where(keep, rr, 0.0), jnp.where(keep, tt, 0.0)
             pads[0, span, :] = rr
             pads[1, span, :] = tt
             pads[2, span, :] = rr * rr
@@ -429,20 +499,20 @@
 
         lax.fori_loop(0, cots.shape[0] // per, chunk, 0)
         left = iota((SUB, LANE), 1) < 64
-        top8 = jnp.where(iota((SUB, LANE), 0) == 0, 1.0, 0.0)
+        row = iota((SUB, LANE), 0)
         for h in range(blocks):
             for half in range(2):
                 span = slice(half * LANE, (half + 1) * LANE)
                 acc = slots[h * SUB : (h + 1) * SUB, span]
                 extra = jnp.broadcast_to(slots[blocks * SUB + h : blocks * SUB + h + 1, span], (SUB, LANE))
                 owner = 4 * h + 2 * half
-                out[owner] = jnp.where(left, acc, pltpu.roll(extra, 64, 1) * top8)
-                out[owner + 1] = jnp.where(left, pltpu.roll(acc, 64, 1), extra * top8)
+                out[owner], out[owner + 1] = pack_pair(acc, extra, left, row)
 
 
 def home_kernel(back, send, centres, conic, rho, opacity, out, total, rows):
     lane = iota((SUB, LANE), 1)
     left = lane < 64
+    row = iota((SUB, LANE), 0)
     pairs = back.shape[0] // 2
     per = 8
     blocks = centres.shape[1] // 256
@@ -452,9 +522,9 @@
         eight, ninth = [], []
         for k in range(per):
             i = c * per + k
-            even, odd = back[2 * i], back[2 * i + 1]
-            eight.append(jnp.where(left, even, pltpu.roll(odd, 64, 1)))
-            ninth.append(jnp.where(left, pltpu.roll(even, 64, 1), odd)[0:1, :])
+            values, last = unpack_pair(back[2 * i], back[2 * i + 1], left, row)
+            eight.append(values)
+            ninth.append(last)
         start = pl.multiple_of(c * per * LANE, per * LANE)
         idx = send[0:1, pl.ds(start, per * LANE)]
         total[...] = total[...] + scatter_block(
@@ -496,15 +566,16 @@
     tiles, count = tile_lists.shape
     height, width = target.shape[1], target.shape[2]
     pixels = height * height
-    params = pltpu.CompilerParams(vmem_limit_bytes=48 << 20)
+    params = lambda mib: pltpu.CompilerParams(vmem_limit_bytes=mib << 20)
     outgoing = pl.pallas_call(
         owner_kernel,
         out_shape=struct(devices, SUB, LANE),
         scratch_shapes=[pltpu.VMEM((SUB, owned), F32), pltpu.VMEM((owned // LANE, LANE), F32)],
+        compiler_params=params(8),
         name="owner_gather",
     )(send_rows, centres, conic, rho, opacity, colors)
     lists = tile_lists.reshape(tiles, SUB, count // SUB).transpose(0, 2, 1).reshape(tiles, 1, count)
-    incoming = exchange(outgoing, 0)
+    incoming, t_before, t_after = exchange(outgoing, 0, target)
     whole = lambda *shape: pl.BlockSpec(shape, lambda t: (0,) * len(shape))
     per_tile = lambda *shape: pl.BlockSpec((1,) + shape, lambda t: (t,) + (0,) * len(shape))
     image, chunk_rend, chunk_start, left = pl.pallas_call(
@@ -527,25 +598,19 @@
             pltpu.VMEM((count, pixels), F32),
             pltpu.VMEM((3, tiles, pixels), F32),
         ],
-        compiler_params=params,
+        compiler_params=params(16),
         name="tile_forward",
     )(lists, incoming)
 
-    up = [(i, i + 1) for i in range(devices - 1)]
-    down = [(j, i) for i, j in up]
-    me = lax.axis_index("dev")
-    where = jnp.stack([me, devices * height]).astype(jnp.int32)
+    before, after = halo_strips(image, 1)
     pixel_grad = pl.pallas_call(
         loss_kernel,
-        in_specs=[pl.BlockSpec(memory_space=pltpu.SMEM)] + [pl.BlockSpec(memory_space=pltpu.VMEM)] * 6,
         out_shape=struct(3, height, width),
         scratch_shapes=[pltpu.VMEM((5, 3 * height, width), F32), pltpu.VMEM((3, 2 * height, width), F32)],
+        compiler_params=params(8),
         name="loss_gradient",
-    )(
-        where,
-        lax.ppermute(image, "dev", up), image, lax.ppermute(image, "dev", down),
-        lax.ppermute(target, "dev", up), target, lax.ppermute(target, "dev", down),
-    )
+    )(before, image, after, t_before, target, t_after)
+
     hi_blocks = devices * 64 // 256
     slot_grads = pl.pallas_call(
         backward_kernel,
@@ -562,10 +627,10 @@
             pltpu.VMEM((tiles, 16, count), F32),
             pltpu.VMEM((hi_blocks * (SUB + 1), 256), F32),
         ],
-        compiler_params=params,
+        compiler_params=params(20),
         name="tile_backward",
     )(lists, left, pixel_grad, chunk_rend, chunk_start)
-    returned = exchange(slot_grads, 1)
+    returned = exchange(slot_grads, 2)
     grads = pl.pallas_call(
         home_kernel,
         out_shape=struct(9, owned),
@@ -573,6 +638,7 @@
             pltpu.VMEM((owned // 256 * (SUB + 1), 256), F32),
             pltpu.VMEM((16, owned), F32),
         ],
+        compiler_params=params(16),
         name="owner_scatter",
     )(returned, send_rows, centres, conic, rho, opacity)
     return image, grads

time: 136 us -> 111 us (0.82)
  Pallas kernels: 113 us -> 100 us
  starting transfers between devices: 9.87 us -> 0 us
  waiting for transfers between devices: 3.28 us -> 0 us
    pallas_call x3 -> x4, Pallas kernels: 52.8 us -> 42.9 us  [the longest x2 32.9 us: exchange(): pl.pallas_call(functools.partial(exchange_kernel, halo), out_shape=[like(...]
    ppermute x4 -> x0, starting transfers between devices: 9.87 us -> none  [the longest x1 3.63 us: shards(): lax.ppermute(target, 'dev', up)]
    ppermute x4 -> x0, waiting for transfers between devices: 3.28 us -> none  [the longest x1 3.27 us: shards(): lax.ppermute(target, 'dev', down)]
    pallas_call x1, Pallas kernels: 5.72 us -> 4.28 us  [shards(): pl.pallas_call(owner_kernel, out_shape=struct(devices, SUB, LANE), scratc...]
    unnamed x22 -> x30, local copies, waits for them, and re-layouts: 7.39 us -> 7.91 us
  transfers between devices with their start and end apart: 4 -> 0, of which waited for: 1 -> 0; matrix products, arithmetic and copies ran while one was open for 0% -> 0% of each run, Pallas kernels for 0% -> 0%
where the time goes in v3:
time: 111 us; the launch traced here: 110 us
  Pallas kernels  100 us (90%)
  local copies, waits for them, and re-layouts  9.06 us (8%)
    pallas_call x2, Pallas kernels, exchange(): pl.pallas_call(functools.partial(exchange_kernel, halo), out_shape=[like(...  32.9 us
    pallas_call x1, Pallas kernels, shards(): pl.pallas_call(forward_kernel, grid=(tiles,), in_specs=[per_tile(1, count...  27.9 us
    pallas_call x1, Pallas kernels, shards(): pl.pallas_call(backward_kernel, grid=(tiles,), in_specs=[whole(tiles, 1,...  21.8 us
    unnamed x30, local copies, waits for them, and re-layouts  7.91 us
    pallas_call x1, Pallas kernels, halo_strips(): pl.pallas_call(halo_kernel, out_shape=[jax.ShapeDtypeStruct(strip.shape,...  6.7 us
    pallas_call x1, Pallas kernels, shards(): pl.pallas_call(owner_kernel, out_shape=struct(devices, SUB, LANE), scratc...  4.28 us
    pallas_call x1, Pallas kernels, shards(): pl.pallas_call(home_kernel, out_shape=struct(9, owned), scratch_shapes=[p...  3.52 us
    pallas_call x1, Pallas kernels, shards(): pl.pallas_call(loss_kernel, out_shape=struct(3, height, width), scratch_s...  3.35 us

profile of v3, /device:TPU:1, one launch (start us, length us, event | category | flops | bytes accessed | tf_op | source)
XLA Modules:
  0.0 110.3 jit_solution(3621950800898235636)
XLA Ops:
  0.6 0.9 reshape.10
  1.5 0.2 copy.11
  1.7 0.1 copy.12.lists
  1.8 0.0 copy-start.4
  1.8 0.8 copy-done.4
  2.6 0.0 copy-start.6
  2.6 0.7 copy-done.6
  3.3 0.0 copy-start.8
  3.3 0.7 copy-done.8
  4.0 0.0 copy-start.10
  4.0 0.7 copy-done.10
  4.7 0.0 copy-start.12
  4.7 0.7 copy-done.12
  5.4 0.0 copy-start.14
  5.4 0.8 copy-done.14
  6.1 4.3 %owner_gather.1.refs_0_ = f32[128,8,128]{2,1,0:T(8,128)S(1)} custom-call(s32[1,8192]{1,0:T(1,128)S(1)} %copy-done.4, f32[2,2048]{1,0:T(2,128)S(1)} %copy-done.6, f32[2,2048]{1,0:T(2,128)S(1)} %copy-done.8, f32[1,2048]{1,0:T(1,128)S(1)} %copy-done.10, f32[1,2048]{1,0:T(1,128)S(1)} %copy-done.12, f32[3,2048]{1,0:T(4,128)S(1)} %copy-done.14), custom_call_target="tpu_custom_call" | custom-call | tf_op jit(solution)/shard_map/owner_gather/pallas_call | solution.py:570
  10.4 0.0 copy-start
  10.4 0.9 copy-done
  11.3 17.4 %exchange.2 = (f32[128,8,128]{2,1,0:T(8,128)S(1)}, f32[3,16,384]{2,1,0:T(8,128)S(1)}, f32[3,16,384]{2,1,0:T(8,128)S(1)}) custom-call(f32[128,8,128]{2,1,0:T(8,128)S(1)} %owner_gather.1.refs_0_, f32[3,16,384]{2,1,0:T(8,128)S(1)} %copy-done), custom_call_target="tpu_custom_call" | custom-call | tf_op jit(solution)/shard_map/exchange/pallas_call | solution.py:167
  28.7 27.9 %tile_forward.1 = (f32[3,16,384]{2,1,0:T(8,128)}, f32[24,3,2,8,256]{4,3,2,1,0:T(8,128)S(1)}, f32[24,2,8,256]{3,2,1,0:T(8,128)S(1)}, bf16[24,512,32]{2,1,0:T(8,128)(2,1)S(1)}) custom-call(s32[24,1,512]{2,1,0:T(1,128)S(1)} %copy.12.lists, f32[128,8,128]{2,1,0:T(8,128)S(1)} %get-tuple-element.11.recv), custom_call_target="tpu_custom_call" | custom-call | tf_op jit(solution)/shard_map/tile_forward/pallas_call | solution.py:581
  56.7 0.0 copy-start.2
  56.7 0.9 copy-done.2
  57.6 6.7 %halo.1 = (f32[3,16,384]{2,1,0:T(8,128)S(1)}, f32[3,16,384]{2,1,0:T(8,128)S(1)}) custom-call(f32[3,16,384]{2,1,0:T(8,128)S(1)} %copy-done.2), custom_call_target="tpu_custom_call" | custom-call | tf_op jit(solution)/shard_map/halo/pallas_call | solution.py:194
  64.3 0.0 copy-start.1
  64.3 0.9 copy-done.1
  65.2 0.0 copy-start.3
  65.2 0.9 copy-done.3
  66.0 3.4 %loss_gradient.1.grad = f32[3,16,384]{2,1,0:T(8,128)S(1)} custom-call(f32[3,16,384]{2,1,0:T(8,128)S(1)} %get-tuple-element.14.before, f32[3,16,384]{2,1,0:T(8,128)S(1)} %copy-done.3, f32[3,16,384]{2,1,0:T(8,128)S(1)} %get-tuple-element.15.after, f32[3,16,384]{2,1,0:T(8,128)S(1)} %get-tuple-element.16.t_before, f32[3,16,384]{2,1,0:T(8,128)S(1)} %copy-done.1, ...), custom_call_target="tpu_custom_call" | custom-call | tf_op jit(solution)/shard_map/loss_gradient/pallas_call | solution.py:606
  69.4 0.0 copy-start.5
  69.4 0.0 copy-start.7
  69.4 0.0 copy-start.9
  69.4 0.0 copy-start.11
  69.4 0.0 copy-start.13
  69.5 21.8 %tile_backward.1.refs_0_ = f32[128,8,128]{2,1,0:T(8,128)S(1)} custom-call(s32[24,1,512]{2,1,0:T(1,128)S(1)} %copy.12.lists, bf16[24,512,32]{2,1,0:T(8,128)(2,1)S(1)} %get-tuple-element.13.left_in, f32[3,16,384]{2,1,0:T(8,128)S(1)} %loss_gradient.1.grad, f32[24,3,2,8,256]{4,3,2,1,0:T(8,128)S(1)} %get-tuple-element.18.chunk_rend, ...), custom_call_target="tpu_custom_call" | custom-call | tf_op jit(solution)/shard_map/tile_backward/pallas_call | solution.py:615
  91.2 15.5 %exchange.3.back = f32[128,8,128]{2,1,0:T(8,128)S(1)} custom-call(f32[128,8,128]{2,1,0:T(8,128)S(1)} %tile_backward.1.refs_0_), custom_call_target="tpu_custom_call" | custom-call | tf_op jit(solution)/shard_map/exchange/pallas_call | solution.py:167
  106.7 0.0 copy-done.5
  106.7 0.0 copy-done.7
  106.7 0.0 copy-done.9
  106.7 0.0 copy-done.11
  106.7 0.0 copy-done.13
  106.7 3.5 %owner_scatter.1 = f32[9,2048]{1,0:T(8,128)} custom-call(f32[128,8,128]{2,1,0:T(8,128)S(1)} %exchange.3.back, s32[1,8192]{1,0:T(1,128)S(1)} %copy-done.5, f32[2,2048]{1,0:T(2,128)S(1)} %copy-done.7, f32[2,2048]{1,0:T(2,128)S(1)} %copy-done.9, f32[1,2048]{1,0:T(1,128)S(1)} %copy-done.11, f32[1,2048]{1,0:T(1,128)S(1)} %copy-done.13), custom_call_target="tpu_custom_call" | custom-call | tf_op jit(solution)/shard_map/owner_scatter/pallas_call | solution.py:634
Async XLA Ops:
  1.8 0.8 copy-start.4
  2.6 0.7 copy-start.6
  3.3 0.7 copy-start.8
  4.0 0.7 copy-start.10
  4.7 0.7 copy-start.12
  5.4 0.8 copy-start.14
  10.4 0.9 copy-start
  56.7 0.9 copy-start.2
  64.3 0.9 copy-start.1
  65.2 0.9 copy-start.3
  69.4 37.3 %copy-start.5 = (s32[1,8192]{1,0:T(1,128)S(1)}, s32[1,8192]{1,0:T(1,128)}, u32[]{:S(2)}) copy-start(s32[1,8192]{1,0:T(1,128)} %send.3) | copy-start | bytes 98308
  69.4 37.3 %copy-start.7 = (f32[2,2048]{1,0:T(2,128)S(1)}, f32[2,2048]{1,0:T(2,128)}, u32[]{:S(2)}) copy-start(f32[2,2048]{1,0:T(2,128)} %centres.3) | copy-start | bytes 49156
  69.4 37.3 %copy-start.9 = (f32[2,2048]{1,0:T(2,128)S(1)}, f32[2,2048]{1,0:T(2,128)}, u32[]{:S(2)}) copy-start(f32[2,2048]{1,0:T(2,128)} %conic.3) | copy-start | bytes 49156
  69.4 37.3 %copy-start.11 = (f32[1,2048]{1,0:T(1,128)S(1)}, f32[1,2048]{1,0:T(1,128)}, u32[]{:S(2)}) copy-start(f32[1,2048]{1,0:T(1,128)} %rho.3) | copy-start | bytes 24580
  69.4 37.3 %copy-start.13 = (f32[1,2048]{1,0:T(1,128)S(1)}, f32[1,2048]{1,0:T(1,128)}, u32[]{:S(2)}) copy-start(f32[1,2048]{1,0:T(1,128)} %opacity.3) | copy-start | bytes 24580

commit v4 on v3

--- a/solution.py
+++ b/solution.py
@@ -60,7 +60,14 @@
     return eight, sub_sum(jnp.where(lax.bitwise_and(hi, 7) == row, last, 0.0))
 
 
-def owner_kernel(send, centres, conic, rho, opacity, colors, out, table, ninth):
+def owner_kernel(*refs):
+    sources, (out, table, ninth), places, sems = refs[:6], refs[6:9], refs[9:15], refs[15]
+    copies = [pltpu.make_async_copy(a, b, sems.at[k]) for k, (a, b) in enumerate(zip(sources, places))]
+    for copy in copies:
+        copy.start()
+    for copy in copies:
+        copy.wait()
+    send, centres, conic, rho, opacity, colors = places
     rows = coefficient_rows(
         centres[0:1, :], centres[1:2, :], conic[0:1, :], conic[1:2, :], rho[...], opacity[...]
     )
@@ -125,7 +132,7 @@
 
 def exchange_kernel(halo, *refs):
     if halo:
-        x, strip, out, before, after, local_sem, send_sem, recv_sem, halo_send, halo_recv = refs
+        x, strip, out, before, centre, after, local_sem, send_sem, recv_sem, halo_send, halo_recv = refs
     else:
         x, out, local_sem, send_sem, recv_sem = refs
     me = lax.axis_index("dev")
@@ -145,7 +152,10 @@
         return carry
 
     lax.fori_loop(1, n, start, 0)
-    copies = halo_copies(n, me, strip, before, after, halo_send, halo_recv) if halo else []
+    copies = []
+    if halo:
+        copies = halo_copies(n, me, strip, before, after, halo_send, halo_recv)
+        copies.append(pltpu.make_async_copy(strip, centre, halo_recv.at[2]))
     for copy in copies:
         copy.start()
     own.wait()
@@ -166,10 +176,10 @@
     like = lambda v: jax.ShapeDtypeStruct(v.shape, v.dtype)
     return pl.pallas_call(
         functools.partial(exchange_kernel, halo),
-        out_shape=[like(x)] + [like(strip)] * 2 if halo else like(x),
-        in_specs=[vmem] * (2 if halo else 1),
-        out_specs=[vmem] * 3 if halo else vmem,
-        scratch_shapes=[pltpu.SemaphoreType.DMA] * 3 + [pltpu.SemaphoreType.DMA((2,))] * (2 if halo else 0),
+        out_shape=[like(x)] + [like(strip)] * 3 if halo else like(x),
+        in_specs=[vmem] + [pl.BlockSpec(memory_space=pltpu.HBM)] * halo,
+        out_specs=[vmem] * 4 if halo else vmem,
+        scratch_shapes=[pltpu.SemaphoreType.DMA] * 3 + [pltpu.SemaphoreType.DMA((3,))] * (2 if halo else 0),
         compiler_params=comm_params(number),
         name="exchange",
     )(*([x, strip] if halo else [x]))
@@ -244,45 +254,53 @@
     return [(seg, j, (seg * groups + j) * SUB) for j in range(groups) for seg in range(2)]
 
 
-def forward_kernel(lists, recv, image, chunk_rend, chunk_start, left_out, table, ninth, cols, alphas, rends):
-    tile = pl.program_id(0)
+def split3(x):
+    one, rest = split2(x)
+    two, three = split2(rest)
+    return one, two, three
+
+
+def gather_columns(lists, flat, cols, slot):
+    count = lists.shape[2]
+    raw = lists[slot, 0:1, :]
+    idx = jnp.maximum(raw, 0)
+    hi, lo = lax.shift_right_logical(idx, 8), lax.bitwise_and(idx, 255)
+    blocks = flat.shape[0] // (SUB + 1)
+    hot = onehot(lo, 256)
+    found = jnp.dot(flat[...], jnp.concatenate([hot] * 3, axis=0), preferred_element_type=F32)
     row = iota((SUB, LANE), 0)
-
-    @pl.when(tile == 0)
-    def _():
-        def pair(h, carry):
-            left = iota((SUB, LANE), 1) < 64
-            table[h], ninth[pl.ds(h, 1), :] = unpack_pair(recv[2 * h], recv[2 * h + 1], left, row)
-            return carry
-
-        lax.fori_loop(0, recv.shape[0] // 2, pair, 0)
-
-    blocks = table.shape[0]
-    count = lists.shape[2]
     for q in range(count // LANE):
         span = slice(q * LANE, (q + 1) * LANE)
-        raw = jnp.broadcast_to(lists[0, 0:1, span], (SUB, LANE))
-        acc, last = pick_nine(lambda h: table[h], ninth, jnp.maximum(raw, 0), row, blocks)
-        acc = jnp.where((row == 5) & (raw < 0), DEAD, acc)
-        one, rest = split2(acc)
-        two, three = split2(rest)
+        hq = jnp.broadcast_to(hi[:, span], (SUB, LANE))
+        bits = {1 << k: lax.bitwise_and(hq, 1 << k) != 0 for k in range(blocks.bit_length() - 1)}
+        acc = pick_tree([lambda h=h: found[h * SUB : (h + 1) * SUB, span] for h in range(blocks)], bits)
+        coarse = {k // SUB: v for k, v in bits.items() if k >= SUB}
+        base = blocks * SUB
+        last = pick_tree(
+            [lambda v=v: found[base + v * SUB : base + (v + 1) * SUB, span] for v in range(blocks // SUB)], coarse
+        )
+        last = sub_sum(jnp.where(lax.bitwise_and(hq, 7) == row, last, 0.0))
+        acc = jnp.where((row == 5) & (jnp.broadcast_to(raw[:, span], (SUB, LANE)) < 0), DEAD, acc)
+        one, two, three = split3(acc)
         b_one, b_two = split2(last)
         more = jnp.where(row == 1, b_two, jnp.where(row == 7, last, b_one))
         more = jnp.where((row == 3) | (row == 4), pltpu.roll(one, 5, 0), more)
         more = jnp.where((row == 5) | (row == 6), pltpu.roll(acc, 7, 0), more)
         stack = jnp.concatenate([one, two, three, more], axis=0)
-        cols[span, :] = jnp.concatenate([stack, jnp.zeros((LANE - 32, LANE), F32)], axis=0).T
-
-    basis = stack_rows((basis_rows(256) + [None, None]) * 3, 32).astype(BF16)
+        cols[slot, span, :] = jnp.concatenate([stack, jnp.zeros((LANE - 32, LANE), F32)], axis=0).T
+
+
+def draw_tile(slot, tile, basis, chunk_rend, chunk_start, left_out, cols, alphas, rends):
+    count = cols.shape[1]
     ones = jnp.ones((SUB, 256), F32)
     product = [ones, ones]
     piece = 64
     for c in range(count // piece):
         span = slice(c * piece, (c + 1) * piece)
-        left = cols[span, 0:32].astype(BF16)
-        left_out[0, span, :] = left
+        left = cols[slot, span, 0:32].astype(BF16)
+        left_out[slot, span, :] = left
         alpha = jnp.exp2(jnp.dot(left, basis, preferred_element_type=F32))
-        alphas[span, :] = alpha
+        alphas[slot, span, :] = alpha
         rest = 1.0 - alpha
         parts = [rest[k * SUB : (k + 1) * SUB, :] for k in range(piece // SUB)]
         while len(parts) > 1:
@@ -295,25 +313,59 @@
     zero = jnp.zeros((SUB, 256), F32)
     sums = [[zero] * 3, [zero] * 3]
     for seg in range(2):
-        chunk_start[0, seg] = trans[seg]
+        chunk_start[slot, seg] = trans[seg]
     for seg, j, at in segments(count):
-        weight = trans[seg] * alphas[at : at + SUB, :]
+        weight = trans[seg] * alphas[slot, at : at + SUB, :]
         trans[seg] = trans[seg] - weight
-        color = cols[at : at + SUB, :]
+        color = cols[slot, at : at + SUB, :]
         sums[seg] = [t + weight * color[:, 29 + ch : 30 + ch] for ch, t in enumerate(sums[seg])]
     for ch in range(3):
         for seg in range(2):
-            chunk_rend[0, ch, seg] = sums[seg][ch]
+            chunk_rend[slot, ch, seg] = sums[seg][ch]
         rends[ch, pl.ds(tile, 1), :] = sub_sum(sums[0][ch] + sums[1][ch])[0:1, :]
 
-    @pl.when(tile == pl.num_programs(0) - 1)
+
+def forward_kernel(
+    lists, recv, image, image_too, chunk_rend, chunk_start, left_out, pieces, ninth, flat, cols, alphas, rends
+):
+    step = pl.program_id(0)
+    per = lists.shape[0]
+    row = iota((SUB, LANE), 0)
+
+    @pl.when(step == 0)
+    def _():
+        blocks = pieces.shape[0] // SUB
+        left = iota((SUB, LANE), 1) < 64
+
+        def block(h, carry):
+            lasts = []
+            for half in range(2):
+                owner = 4 * h + 2 * half
+                eight, last = unpack_pair(recv[owner], recv[owner + 1], left, row)
+                pieces[pl.ds(pl.multiple_of(h * SUB, SUB), SUB), half * LANE : (half + 1) * LANE] = eight
+                lasts.append(last)
+            ninth[pl.ds(h, 1), :] = jnp.concatenate(lasts, axis=1)
+            return carry
+
+        lax.fori_loop(0, blocks, block, 0)
+        for rows, source in ((slice(0, blocks * SUB), pieces), (slice(blocks * SUB, None), ninth)):
+            for k, part in enumerate(split3(source[...])):
+                flat[rows, k * 256 : (k + 1) * 256] = part.astype(BF16)
+
+    basis = stack_rows((basis_rows(256) + [None, None]) * 3, 32).astype(BF16)
+    for slot in range(per):
+        gather_columns(lists, flat, cols, slot)
+    for slot in range(per):
+        draw_tile(slot, step * per + slot, basis, chunk_rend, chunk_start, left_out, cols, alphas, rends)
+
+    @pl.when(step == pl.num_programs(0) - 1)
     def _():
         for ch in range(3):
             for g in range(rends.shape[1] // SUB):
                 for h in range(2):
-                    image[ch, h * SUB : (h + 1) * SUB, g * LANE : (g + 1) * LANE] = block_transpose(
-                        rends[ch, g * SUB : (g + 1) * SUB, h * LANE : (h + 1) * LANE]
-                    )
+                    block = block_transpose(rends[ch, g * SUB : (g + 1) * SUB, h * LANE : (h + 1) * LANE])
+                    for to in (image, image_too):
+                        to[ch, h * SUB : (h + 1) * SUB, g * LANE : (g + 1) * LANE] = block
 
 
 def taps_of():
@@ -418,21 +470,8 @@
     return both[: blocks * (SUB + 1), :] + both[blocks * (SUB + 1) :, :]
 
 
-def backward_kernel(lists, left_in, grad, chunk_rend, chunk_start, out, cots, halves, grads, slots):
-    tile = pl.program_id(0)
-    tiles = pl.num_programs(0)
+def shade_tile(slot, tile, left_in, chunk_rend, chunk_start, cots, halves, grads):
     count = left_in.shape[1]
-
-    @pl.when(tile == 0)
-    def _():
-        for ch in range(3):
-            for g in range(cots.shape[0] // SUB):
-                for h in range(2):
-                    span = slice(h * LANE, (h + 1) * LANE)
-                    block = block_transpose(grad[ch, h * SUB : (h + 1) * SUB, g * LANE : (g + 1) * LANE])
-                    for t in range(SUB):
-                        cots[g * SUB + t, ch : ch + 1, span] = block[t : t + 1, :]
-
     rows = [cots[tile, ch : ch + 1, :] for ch in range(3)]
     ones, twos = zip(*(split2(r) for r in rows))
     basis = stack_rows((basis_rows(256) + [None, None]) * 3, 32)
@@ -442,20 +481,20 @@
     )
     right = jnp.concatenate([basis, back], axis=1).astype(BF16)
 
-    inside = [sum(chunk_rend[0, ch, seg] * rows[ch] for ch in range(3)) for seg in range(2)]
+    inside = [sum(chunk_rend[slot, ch, seg] * rows[ch] for ch in range(3)) for seg in range(2)]
     at8 = iota((SUB, 256), 0)
     later = inside[0] + inside[1]
     later = jnp.where(at8 == SUB - 1, 0.0, pltpu.roll(later, SUB - 1, 0))
     for d in (1, 2, 4):
         later = later + jnp.where(at8 < SUB - d, pltpu.roll(later, SUB - d, 0), 0.0)
     behind = [later + inside[1] + inside[0], later + inside[1]]
-    trans = [chunk_start[0, seg] for seg in range(2)]
+    trans = [chunk_start[slot, seg] for seg in range(2)]
 
     piece = 32
     order = [c // 2 + (c % 2) * (count // piece // 2) for c in range(count // piece)]
     for c in order:
         seg = 2 * c * piece // count
-        field = jnp.dot(left_in[0, c * piece : (c + 1) * piece, :], right, preferred_element_type=F32)
+        field = jnp.dot(left_in[slot, c * piece : (c + 1) * piece, :], right, preferred_element_type=F32)
         alpha = jnp.exp2(field[:, 0:256])
         ratio = alpha / (1.0 - alpha)
         parts = []
@@ -469,35 +508,54 @@
         at = slice(c * piece, (c + 1) * piece)
         value = jnp.concatenate([p[0] for p in parts], axis=0)
         one = value.astype(BF16)
-        halves[at, 0:256] = one
-        halves[at, 256:512] = (value - one.astype(F32)).astype(BF16)
-        halves[at, 512:768] = jnp.concatenate([p[1] for p in parts], axis=0).astype(BF16)
+        halves[slot, at, 0:256] = one
+        halves[slot, at, 256:512] = (value - one.astype(F32)).astype(BF16)
+        halves[slot, at, 512:768] = jnp.concatenate([p[1] for p in parts], axis=0).astype(BF16)
 
     base = stack_rows(basis_rows(256), 16)
     colours = stack_rows([None] * 6 + list(ones) + list(twos), 16)
     kernel = jnp.concatenate([base, base, colours], axis=1).astype(BF16)
-    found = lax.dot_general(kernel, halves[...], NT, preferred_element_type=F32)
+    found = lax.dot_general(kernel, halves[slot], NT, preferred_element_type=F32)
     low = found[8:16, :]
     at16 = iota(low.shape, 0)
     top = found[0:8, :] + jnp.where(at16 >= 6, pltpu.roll(low, 5, 0), 0.0)
     grads[tile, 0:8, :] = top
     grads[tile, 8:9, :] = low[0:1, :] + low[3:4, :]
 
-    @pl.when(tile == tiles - 1)
+
+def backward_kernel(lists, left_in, grad, chunk_rend, chunk_start, out, cots, halves, grads, slots):
+    step = pl.program_id(0)
+    steps = pl.num_programs(0)
+
+    @pl.when(step == 0)
+    def _():
+        for ch in range(3):
+            for g in range(cots.shape[0] // SUB):
+                for h in range(2):
+                    span = slice(h * LANE, (h + 1) * LANE)
+                    block = block_transpose(grad[ch, h * SUB : (h + 1) * SUB, g * LANE : (g + 1) * LANE])
+                    for t in range(SUB):
+                        cots[g * SUB + t, ch : ch + 1, span] = block[t : t + 1, :]
+
+    per = left_in.shape[0]
+    for slot in range(per):
+        shade_tile(slot, step * per + slot, left_in, chunk_rend, chunk_start, cots, halves, grads)
+
+    @pl.when(step == steps - 1)
     def _():
         slots[...] = jnp.zeros_like(slots)
         blocks = slots.shape[0] // (SUB + 1)
-        per = 2
+        group = 2
 
         def chunk(c, carry):
-            each = [c * per + k for k in range(per)]
+            each = [c * group + k for k in range(group)]
             idx = jnp.concatenate([jnp.maximum(lists[t], 0) for t in each], axis=1)
             eight = jnp.concatenate([grads[t, 0:8, :] for t in each], axis=1)
             ninth = jnp.concatenate([grads[t, 8:9, :] for t in each], axis=1)
             slots[...] = slots[...] + scatter_block(eight, ninth, idx, blocks)
             return carry
 
-        lax.fori_loop(0, cots.shape[0] // per, chunk, 0)
+        lax.fori_loop(0, cots.shape[0] // group, chunk, 0)
         left = iota((SUB, LANE), 1) < 64
         row = iota((SUB, LANE), 0)
         for h in range(blocks):
@@ -567,54 +625,63 @@
     height, width = target.shape[1], target.shape[2]
     pixels = height * height
     params = lambda mib: pltpu.CompilerParams(vmem_limit_bytes=mib << 20)
+    sources = (send_rows, centres, conic, rho, opacity, colors)
     outgoing = pl.pallas_call(
         owner_kernel,
+        in_specs=[pl.BlockSpec(memory_space=pltpu.HBM)] * 6,
         out_shape=struct(devices, SUB, LANE),
-        scratch_shapes=[pltpu.VMEM((SUB, owned), F32), pltpu.VMEM((owned // LANE, LANE), F32)],
+        scratch_shapes=[pltpu.VMEM((SUB, owned), F32), pltpu.VMEM((owned // LANE, LANE), F32)]
+        + [pltpu.VMEM(v.shape, v.dtype) for v in sources]
+        + [pltpu.SemaphoreType.DMA((6,))],
         compiler_params=params(8),
         name="owner_gather",
-    )(send_rows, centres, conic, rho, opacity, colors)
+    )(*sources)
+
     lists = tile_lists.reshape(tiles, SUB, count // SUB).transpose(0, 2, 1).reshape(tiles, 1, count)
-    incoming, t_before, t_after = exchange(outgoing, 0, target)
+    incoming, t_before, t_centre, t_after = exchange(outgoing, 0, target)
     whole = lambda *shape: pl.BlockSpec(shape, lambda t: (0,) * len(shape))
-    per_tile = lambda *shape: pl.BlockSpec((1,) + shape, lambda t: (t,) + (0,) * len(shape))
-    image, chunk_rend, chunk_start, left = pl.pallas_call(
+    per = 2
+    per_tile = lambda *shape: pl.BlockSpec((per,) + shape, lambda t: (t,) + (0,) * len(shape))
+    hi_blocks = devices * 64 // 256
+    image, image_too, chunk_rend, chunk_start, left = pl.pallas_call(
         forward_kernel,
-        grid=(tiles,),
+        grid=(tiles // per,),
         in_specs=[per_tile(1, count), whole(devices, SUB, LANE)],
         out_specs=[
-            whole(3, height, width), per_tile(3, 2, SUB, pixels), per_tile(2, SUB, pixels), per_tile(count, 32)
+            whole(3, height, width), whole(3, height, width),
+            per_tile(3, 2, SUB, pixels), per_tile(2, SUB, pixels), per_tile(count, 32),
         ],
         out_shape=[
+            struct(3, height, width),
             struct(3, height, width),
             struct(tiles, 3, 2, SUB, pixels),
             struct(tiles, 2, SUB, pixels),
             struct(tiles, count, 32, dtype=BF16),
         ],
         scratch_shapes=[
-            pltpu.VMEM((devices // 2, SUB, LANE), F32),
-            pltpu.VMEM((devices // 2, LANE), F32),
-            pltpu.VMEM((count, LANE), F32),
-            pltpu.VMEM((count, pixels), F32),
+            pltpu.VMEM((hi_blocks * SUB, 256), F32),
+            pltpu.VMEM((hi_blocks, 256), F32),
+            pltpu.VMEM((hi_blocks * (SUB + 1), 3 * 256), BF16),
+            pltpu.VMEM((per, count, LANE), F32),
+            pltpu.VMEM((per, count, pixels), F32),
             pltpu.VMEM((3, tiles, pixels), F32),
         ],
         compiler_params=params(16),
         name="tile_forward",
     )(lists, incoming)
 
-    before, after = halo_strips(image, 1)
+    before, after = halo_strips(image_too, 1)
     pixel_grad = pl.pallas_call(
         loss_kernel,
         out_shape=struct(3, height, width),
         scratch_shapes=[pltpu.VMEM((5, 3 * height, width), F32), pltpu.VMEM((3, 2 * height, width), F32)],
         compiler_params=params(8),
         name="loss_gradient",
-    )(before, image, after, t_before, target, t_after)
-
-    hi_blocks = devices * 64 // 256
+    )(before, image_too, after, t_before, t_centre, t_after)
+
     slot_grads = pl.pallas_call(
         backward_kernel,
-        grid=(tiles,),
+        grid=(tiles // per,),
         in_specs=[
             whole(tiles, 1, count), per_tile(count, 32), whole(3, height, width),
             per_tile(3, 2, SUB, pixels), per_tile(2, SUB, pixels),
@@ -623,7 +690,7 @@
         out_shape=struct(devices, SUB, LANE),
         scratch_shapes=[
             pltpu.VMEM((tiles, 3, pixels), F32),
-            pltpu.VMEM((count, 3 * pixels), BF16),
+            pltpu.VMEM((per, count, 3 * pixels), BF16),
             pltpu.VMEM((tiles, 16, count), F32),
             pltpu.VMEM((hi_blocks * (SUB + 1), 256), F32),
         ],

time: 111 us -> 99.8 us (0.90)
  Pallas kernels: 100 us -> 92 us
  local copies, waits for them, and re-layouts: 9.06 us -> 6.4 us
    pallas_call x3, Pallas kernels: 54 us -> 45.5 us  [the longest x1 21 us: shards(): pl.pallas_call(forward_kernel, grid=(tiles // per,), in_specs=[per_tile(1...]
    unnamed x30 -> x24, local copies, waits for them, and re-layouts: 7.91 us -> 5.26 us
where the time goes in v4:
time: 99.8 us; the launch traced here: 99.2 us
  Pallas kernels  92 us (92%)
  local copies, waits for them, and re-layouts  6.4 us (6%)
    pallas_call x2, Pallas kernels, exchange(): pl.pallas_call(functools.partial(exchange_kernel, halo), out_shape=[like(...  32.9 us
    pallas_call x1, Pallas kernels, shards(): pl.pallas_call(forward_kernel, grid=(tiles // per,), in_specs=[per_tile(1...  21 us
    pallas_call x1, Pallas kernels, shards(): pl.pallas_call(backward_kernel, grid=(tiles // per,), in_specs=[whole(til...  20 us
    pallas_call x1, Pallas kernels, halo_strips(): pl.pallas_call(halo_kernel, out_shape=[jax.ShapeDtypeStruct(strip.shape,...  6.76 us
    unnamed x24, local copies, waits for them, and re-layouts  5.26 us
    pallas_call x1, Pallas kernels, shards(): pl.pallas_call(owner_kernel, in_specs=[pl.BlockSpec(memory_space=pltpu.HB...  4.46 us
    pallas_call x1, Pallas kernels, shards(): pl.pallas_call(home_kernel, out_shape=struct(9, owned), scratch_shapes=[p...  3.52 us
    pallas_call x1, Pallas kernels, shards(): pl.pallas_call(loss_kernel, out_shape=struct(3, height, width), scratch_s...  3.36 us

profile of v4, /device:TPU:1, one launch (start us, length us, event | category | flops | bytes accessed | tf_op | source)
XLA Modules:
  0.0 99.2 jit_solution(15179738998287806736)
XLA Ops:
  0.6 0.9 reshape.10
  1.5 0.2 copy.11
  1.7 0.1 copy.12.lists
  1.8 0.0 copy-start
  1.8 0.8 copy-done
  2.6 0.0 copy-start.3
  2.6 0.7 copy-done.3
  3.3 0.0 copy-start.5
  3.3 0.7 copy-done.5
  4.0 0.0 copy-start.7
  4.0 0.7 copy-done.7
  4.7 0.0 copy-start.9
  4.7 0.7 copy-done.9
  5.4 0.0 copy-start.11
  5.4 0.8 copy-done.11
  6.1 4.5 %owner_gather.1.refs_0_ = f32[128,8,128]{2,1,0:T(8,128)S(1)} custom-call(s32[1,8192]{1,0:T(1,128)S(1)} %copy-done, f32[2,2048]{1,0:T(2,128)S(1)} %copy-done.3, f32[2,2048]{1,0:T(2,128)S(1)} %copy-done.5, f32[1,2048]{1,0:T(1,128)S(1)} %copy-done.7, f32[1,2048]{1,0:T(1,128)S(1)} %copy-done.9, f32[3,2048]{1,0:T(4,128)S(1)} %copy-done.11), custom_call_target="tpu_custom_call" | custom-call | tf_op jit(solution)/shard_map/owner_gather/pallas_call | solution.py:629
  10.6 0.0 copy-start.2
  10.6 0.9 copy-done.2
  11.5 17.4 %exchange.2 = (f32[128,8,128]{2,1,0:T(8,128)S(1)}, f32[3,16,384]{2,1,0:T(8,128)S(1)}, f32[3,16,384]{2,1,0:T(8,128)S(1)}, f32[3,16,384]{2,1,0:T(8,128)S(1)}) custom-call(f32[128,8,128]{2,1,0:T(8,128)S(1)} %owner_gather.1.refs_0_, f32[3,16,384]{2,1,0:T(8,128)S(1)} %copy-done.2), custom_call_target="tpu_custom_call" | custom-call | tf_op jit(solution)/shard_map/exchange/pallas_call | solution.py:177
  28.9 21.0 %tile_forward.1 = (f32[3,16,384]{2,1,0:T(8,128)}, f32[3,16,384]{2,1,0:T(8,128)S(1)}, f32[24,3,2,8,256]{4,3,2,1,0:T(8,128)S(1)}, f32[24,2,8,256]{3,2,1,0:T(8,128)S(1)}, bf16[24,512,32]{2,1,0:T(8,128)(2,1)S(1)}) custom-call(s32[24,1,512]{2,1,0:T(1,128)S(1)} %copy.12.lists, f32[128,8,128]{2,1,0:T(8,128)S(1)} %get-tuple-element.13.recv), custom_call_target="tpu_custom_call" | custom-call | tf_op jit(solution)/shard_map/tile_forward/pallas_call | solution.py:646
  49.9 6.8 %halo.1 = (f32[3,16,384]{2,1,0:T(8,128)S(1)}, f32[3,16,384]{2,1,0:T(8,128)S(1)}) custom-call(f32[3,16,384]{2,1,0:T(8,128)S(1)} %get-tuple-element.16.strip.centre), custom_call_target="tpu_custom_call" | custom-call | tf_op jit(solution)/shard_map/halo/pallas_call | solution.py:204
  56.7 3.4 %loss_gradient.1.grad = f32[3,16,384]{2,1,0:T(8,128)S(1)} custom-call(f32[3,16,384]{2,1,0:T(8,128)S(1)} %get-tuple-element.17.before, f32[3,16,384]{2,1,0:T(8,128)S(1)} %get-tuple-element.16.strip.centre, f32[3,16,384]{2,1,0:T(8,128)S(1)} %get-tuple-element.18.after, f32[3,16,384]{2,1,0:T(8,128)S(1)} %get-tuple-element.19.t_before, ...), custom_call_target="tpu_custom_call" | custom-call | tf_op jit(solution)/shard_map/loss_gradient/pallas_call | solution.py:674
  60.1 0.0 copy-start.1
  60.1 0.0 copy-start.4
  60.1 0.0 copy-start.6
  60.1 0.0 copy-start.8
  60.1 0.0 copy-start.10
  60.1 20.0 %tile_backward.1.refs_0_ = f32[128,8,128]{2,1,0:T(8,128)S(1)} custom-call(s32[24,1,512]{2,1,0:T(1,128)S(1)} %copy.12.lists, bf16[24,512,32]{2,1,0:T(8,128)(2,1)S(1)} %get-tuple-element.15.left_in, f32[3,16,384]{2,1,0:T(8,128)S(1)} %loss_gradient.1.grad, f32[24,3,2,8,256]{4,3,2,1,0:T(8,128)S(1)} %get-tuple-element.22.chunk_rend, ...), custom_call_target="tpu_custom_call" | custom-call | tf_op jit(solution)/shard_map/tile_backward/pallas_call | solution.py:682
  80.2 15.5 %exchange.3.back = f32[128,8,128]{2,1,0:T(8,128)S(1)} custom-call(f32[128,8,128]{2,1,0:T(8,128)S(1)} %tile_backward.1.refs_0_), custom_call_target="tpu_custom_call" | custom-call | tf_op jit(solution)/shard_map/exchange/pallas_call | solution.py:177
  95.6 0.0 copy-done.1
  95.7 0.0 copy-done.4
  95.7 0.0 copy-done.6
  95.7 0.0 copy-done.8
  95.7 0.0 copy-done.10
  95.7 3.5 %owner_scatter.1 = f32[9,2048]{1,0:T(8,128)} custom-call(f32[128,8,128]{2,1,0:T(8,128)S(1)} %exchange.3.back, s32[1,8192]{1,0:T(1,128)S(1)} %copy-done.1, f32[2,2048]{1,0:T(2,128)S(1)} %copy-done.4, f32[2,2048]{1,0:T(2,128)S(1)} %copy-done.6, f32[1,2048]{1,0:T(1,128)S(1)} %copy-done.8, f32[1,2048]{1,0:T(1,128)S(1)} %copy-done.10), custom_call_target="tpu_custom_call" | custom-call | tf_op jit(solution)/shard_map/owner_scatter/pallas_call | solution.py:701
Async XLA Ops:
  1.8 0.8 copy-start
  2.6 0.7 copy-start.3
  3.3 0.7 copy-start.5
  4.0 0.7 copy-start.7
  4.7 0.7 copy-start.9
  5.4 0.8 copy-start.11
  10.6 0.9 copy-start.2
  60.1 35.6 %copy-start.1 = (s32[1,8192]{1,0:T(1,128)S(1)}, s32[1,8192]{1,0:T(1,128)}, u32[]{:S(2)}) copy-start(s32[1,8192]{1,0:T(1,128)} %send.1) | copy-start | bytes 98308
  60.1 35.6 %copy-start.4 = (f32[2,2048]{1,0:T(2,128)S(1)}, f32[2,2048]{1,0:T(2,128)}, u32[]{:S(2)}) copy-start(f32[2,2048]{1,0:T(2,128)} %centres.1) | copy-start | bytes 49156
  60.1 35.6 %copy-start.6 = (f32[2,2048]{1,0:T(2,128)S(1)}, f32[2,2048]{1,0:T(2,128)}, u32[]{:S(2)}) copy-start(f32[2,2048]{1,0:T(2,128)} %conic.1) | copy-start | bytes 49156
  60.1 35.6 %copy-start.8 = (f32[1,2048]{1,0:T(1,128)S(1)}, f32[1,2048]{1,0:T(1,128)}, u32[]{:S(2)}) copy-start(f32[1,2048]{1,0:T(1,128)} %rho.1) | copy-start | bytes 24580
  60.1 35.6 %copy-start.10 = (f32[1,2048]{1,0:T(1,128)S(1)}, f32[1,2048]{1,0:T(1,128)}, u32[]{:S(2)}) copy-start(f32[1,2048]{1,0:T(1,128)} %opacity.1) | copy-start | bytes 24580

commit v5 on v4

--- a/solution.py
+++ b/solution.py
@@ -249,6 +249,14 @@
     return x
 
 
+def take_turns(order, **workers):
+    for name in order:
+        next(workers[name], None)
+    for worker in workers.values():
+        for _ in worker:
+            pass
+
+
 def segments(count):
     groups = count // SUB // 2
     return [(seg, j, (seg * groups + j) * SUB) for j in range(groups) for seg in range(2)]
@@ -260,17 +268,23 @@
     return one, two, three
 
 
-def gather_columns(lists, flat, cols, slot):
-    count = lists.shape[2]
-    raw = lists[slot, 0:1, :]
-    idx = jnp.maximum(raw, 0)
-    hi, lo = lax.shift_right_logical(idx, 8), lax.bitwise_and(idx, 255)
+def gather_columns(raw, flat, cols, slot):
+    count = raw.shape[1]
     blocks = flat.shape[0] // (SUB + 1)
-    hot = onehot(lo, 256)
-    found = jnp.dot(flat[...], jnp.concatenate([hot] * 3, axis=0), preferred_element_type=F32)
     row = iota((SUB, LANE), 0)
+    wide = 2 * LANE
+    founds = []
+    for n in range(count // wide):
+        idx = jnp.maximum(raw[:, n * wide : (n + 1) * wide], 0)
+        hi, lo = lax.shift_right_logical(idx, 8), lax.bitwise_and(idx, 255)
+        hot = onehot(lo, 256)
+        found = jnp.dot(flat[...], jnp.concatenate([hot] * 2, axis=0), preferred_element_type=F32)
+        founds.append((hi, found))
+        yield
     for q in range(count // LANE):
-        span = slice(q * LANE, (q + 1) * LANE)
+        hi, found = founds[q // 2]
+        span = slice((q % 2) * LANE, (q % 2 + 1) * LANE)
+        out = slice(q * LANE, (q + 1) * LANE)
         hq = jnp.broadcast_to(hi[:, span], (SUB, LANE))
         bits = {1 << k: lax.bitwise_and(hq, 1 << k) != 0 for k in range(blocks.bit_length() - 1)}
         acc = pick_tree([lambda h=h: found[h * SUB : (h + 1) * SUB, span] for h in range(blocks)], bits)
@@ -280,14 +294,19 @@
             [lambda v=v: found[base + v * SUB : base + (v + 1) * SUB, span] for v in range(blocks // SUB)], coarse
         )
         last = sub_sum(jnp.where(lax.bitwise_and(hq, 7) == row, last, 0.0))
-        acc = jnp.where((row == 5) & (jnp.broadcast_to(raw[:, span], (SUB, LANE)) < 0), DEAD, acc)
+        yield
+        acc = jnp.where((row == 5) & (jnp.broadcast_to(raw[:, out], (SUB, LANE)) < 0), DEAD, acc)
         one, two, three = split3(acc)
         b_one, b_two = split2(last)
         more = jnp.where(row == 1, b_two, jnp.where(row == 7, last, b_one))
         more = jnp.where((row == 3) | (row == 4), pltpu.roll(one, 5, 0), more)
         more = jnp.where((row == 5) | (row == 6), pltpu.roll(acc, 7, 0), more)
         stack = jnp.concatenate([one, two, three, more], axis=0)
-        cols[slot, span, :] = jnp.concatenate([stack, jnp.zeros((LANE - 32, LANE), F32)], axis=0).T
+        cols[slot, out, :] = jnp.concatenate([stack, jnp.zeros((LANE - 32, LANE), F32)], axis=0).T
+        yield
+
+
+TURNS = "d" * 8 + "g" + "d" * 6 + "g" + "d" * 2 + "gg" + "d" * 2 + "gg" + "d" * 2 + "gg" + "d" * 4 + "gg"
 
 
 def draw_tile(slot, tile, basis, chunk_rend, chunk_start, left_out, cols, alphas, rends):
@@ -307,6 +326,7 @@
             parts = [parts[k] * parts[k + 1] for k in range(0, len(parts), 2)]
         seg = 2 * c * piece // count
         product[seg] = product[seg] * parts[0]
+        yield
 
     begin = scan_sub(product[0] * product[1])
     trans = [begin, begin * product[0]]
@@ -319,6 +339,8 @@
         trans[seg] = trans[seg] - weight
         color = cols[slot, at : at + SUB, :]
         sums[seg] = [t + weight * color[:, 29 + ch : 30 + ch] for ch, t in enumerate(sums[seg])]
+        if seg == 1 and j % 2 == 1:
+            yield
     for ch in range(3):
         for seg in range(2):
             chunk_rend[slot, ch, seg] = sums[seg][ch]
@@ -329,7 +351,6 @@
     lists, recv, image, image_too, chunk_rend, chunk_start, left_out, pieces, ninth, flat, cols, alphas, rends
 ):
     step = pl.program_id(0)
-    per = lists.shape[0]
     row = iota((SUB, LANE), 0)
 
     @pl.when(step == 0)
@@ -349,14 +370,20 @@
 
         lax.fori_loop(0, blocks, block, 0)
         for rows, source in ((slice(0, blocks * SUB), pieces), (slice(blocks * SUB, None), ninth)):
-            for k, part in enumerate(split3(source[...])):
+            for k, part in enumerate(split2(source[...])):
                 flat[rows, k * 256 : (k + 1) * 256] = part.astype(BF16)
+        for _ in gather_columns(lists[0], flat, cols, 0):
+            pass
 
     basis = stack_rows((basis_rows(256) + [None, None]) * 3, 32).astype(BF16)
-    for slot in range(per):
-        gather_columns(lists, flat, cols, slot)
-    for slot in range(per):
-        draw_tile(slot, step * per + slot, basis, chunk_rend, chunk_start, left_out, cols, alphas, rends)
+    for slot in range(2):
+        tile = 2 * step + slot
+        later = jnp.minimum(tile + 1, lists.shape[0] - 1)
+        take_turns(
+            TURNS,
+            g=gather_columns(lists[later], flat, cols, 1 - slot),
+            d=draw_tile(slot, tile, basis, chunk_rend, chunk_start, left_out, cols, alphas, rends),
+        )
 
     @pl.when(step == pl.num_programs(0) - 1)
     def _():
@@ -470,7 +497,7 @@
     return both[: blocks * (SUB + 1), :] + both[blocks * (SUB + 1) :, :]
 
 
-def shade_tile(slot, tile, left_in, chunk_rend, chunk_start, cots, halves, grads):
+def shade_tile(slot, tile, left_in, chunk_rend, chunk_start, cots, halves):
     count = left_in.shape[1]
     rows = [cots[tile, ch : ch + 1, :] for ch in range(3)]
     ones, twos = zip(*(split2(r) for r in rows))
@@ -490,11 +517,19 @@
     behind = [later + inside[1] + inside[0], later + inside[1]]
     trans = [chunk_start[slot, seg] for seg in range(2)]
 
-    piece = 32
+    piece = 64
     order = [c // 2 + (c % 2) * (count // piece // 2) for c in range(count // piece)]
-    for c in order:
+
+    def field_of(c):
+        return jnp.dot(left_in[slot, c * piece : (c + 1) * piece, :], right, preferred_element_type=F32)
+
+    ahead = 1
+    fields = [field_of(c) for c in order[:ahead]]
+    for n, c in enumerate(order):
+        if n + ahead < len(order):
+            fields.append(field_of(order[n + ahead]))
         seg = 2 * c * piece // count
-        field = jnp.dot(left_in[slot, c * piece : (c + 1) * piece, :], right, preferred_element_type=F32)
+        field = fields[n]
         alpha = jnp.exp2(field[:, 0:256])
         ratio = alpha / (1.0 - alpha)
         parts = []
@@ -511,16 +546,28 @@
         halves[slot, at, 0:256] = one
         halves[slot, at, 256:512] = (value - one.astype(F32)).astype(BF16)
         halves[slot, at, 512:768] = jnp.concatenate([p[1] for p in parts], axis=0).astype(BF16)
-
+        yield
+
+
+BACK_TURNS = "fss" * 4
+
+
+def find_moments(slot, tile, cots, halves, grads):
+    rows = [cots[tile, ch : ch + 1, :] for ch in range(3)]
+    ones, twos = zip(*(split2(r) for r in rows))
     base = stack_rows(basis_rows(256), 16)
     colours = stack_rows([None] * 6 + list(ones) + list(twos), 16)
     kernel = jnp.concatenate([base, base, colours], axis=1).astype(BF16)
-    found = lax.dot_general(kernel, halves[slot], NT, preferred_element_type=F32)
-    low = found[8:16, :]
-    at16 = iota(low.shape, 0)
-    top = found[0:8, :] + jnp.where(at16 >= 6, pltpu.roll(low, 5, 0), 0.0)
-    grads[tile, 0:8, :] = top
-    grads[tile, 8:9, :] = low[0:1, :] + low[3:4, :]
+    wide = 128
+    for n in range(halves.shape[1] // wide):
+        at = slice(n * wide, (n + 1) * wide)
+        found = lax.dot_general(kernel, halves[slot, at, :], NT, preferred_element_type=F32)
+        low = found[8:16, :]
+        at16 = iota(low.shape, 0)
+        top = found[0:8, :] + jnp.where(at16 >= 6, pltpu.roll(low, 5, 0), 0.0)
+        grads[tile, 0:8, at] = top
+        grads[tile, 8:9, at] = low[0:1, :] + low[3:4, :]
+        yield
 
 
 def backward_kernel(lists, left_in, grad, chunk_rend, chunk_start, out, cots, halves, grads, slots):
@@ -537,12 +584,19 @@
                     for t in range(SUB):
                         cots[g * SUB + t, ch : ch + 1, span] = block[t : t + 1, :]
 
-    per = left_in.shape[0]
-    for slot in range(per):
-        shade_tile(slot, step * per + slot, left_in, chunk_rend, chunk_start, cots, halves, grads)
+    for slot in range(2):
+        tile = 2 * step + slot
+        past = jnp.maximum(tile - 1, 0)
+        take_turns(
+            BACK_TURNS,
+            f=find_moments(1 - slot, past, cots, halves, grads),
+            s=shade_tile(slot, tile, left_in, chunk_rend, chunk_start, cots, halves),
+        )
 
     @pl.when(step == steps - 1)
     def _():
+        for _ in find_moments(1, 2 * step + 1, cots, halves, grads):
+            pass
         slots[...] = jnp.zeros_like(slots)
         blocks = slots.shape[0] // (SUB + 1)
         group = 2
@@ -646,7 +700,7 @@
     image, image_too, chunk_rend, chunk_start, left = pl.pallas_call(
         forward_kernel,
         grid=(tiles // per,),
-        in_specs=[per_tile(1, count), whole(devices, SUB, LANE)],
+        in_specs=[whole(tiles, 1, count), whole(devices, SUB, LANE)],
         out_specs=[
             whole(3, height, width), whole(3, height, width),
             per_tile(3, 2, SUB, pixels), per_tile(2, SUB, pixels), per_tile(count, 32),
@@ -661,7 +715,7 @@
         scratch_shapes=[
             pltpu.VMEM((hi_blocks * SUB, 256), F32),
             pltpu.VMEM((hi_blocks, 256), F32),
-            pltpu.VMEM((hi_blocks * (SUB + 1), 3 * 256), BF16),
+            pltpu.VMEM((hi_blocks * (SUB + 1), 2 * 256), BF16),
             pltpu.VMEM((per, count, LANE), F32),
             pltpu.VMEM((per, count, pixels), F32),
             pltpu.VMEM((3, tiles, pixels), F32),

time: 99.8 us -> 94.5 us (0.947)
  Pallas kernels: 92 us -> 86.8 us
    pallas_call x1, Pallas kernels: 20 us -> 16.6 us  [shards(): pl.pallas_call(backward_kernel, grid=(tiles // per,), in_specs=[whole(til...]
    pallas_call x1, Pallas kernels: 21 us -> 19.3 us  [shards(): pl.pallas_call(forward_kernel, grid=(tiles // per,), in_specs=[whole(tile...]
where the time goes in v5:
time: 94.5 us; the launch traced here: 94 us
  Pallas kernels  86.8 us (92%)
  local copies, waits for them, and re-layouts  6.4 us (7%)
    pallas_call x2, Pallas kernels, exchange(): pl.pallas_call(functools.partial(exchange_kernel, halo), out_shape=[like(...  32.8 us
    pallas_call x1, Pallas kernels, shards(): pl.pallas_call(forward_kernel, grid=(tiles // per,), in_specs=[whole(tile...  19.3 us
    pallas_call x1, Pallas kernels, shards(): pl.pallas_call(backward_kernel, grid=(tiles // per,), in_specs=[whole(til...  16.6 us
    pallas_call x1, Pallas kernels, halo_strips(): pl.pallas_call(halo_kernel, out_shape=[jax.ShapeDtypeStruct(strip.shape,...  6.69 us
    unnamed x24, local copies, waits for them, and re-layouts  5.26 us
    pallas_call x1, Pallas kernels, shards(): pl.pallas_call(owner_kernel, in_specs=[pl.BlockSpec(memory_space=pltpu.HB...  4.46 us
    pallas_call x1, Pallas kernels, shards(): pl.pallas_call(home_kernel, out_shape=struct(9, owned), scratch_shapes=[p...  3.52 us
    pallas_call x1, Pallas kernels, shards(): pl.pallas_call(loss_kernel, out_shape=struct(3, height, width), scratch_s...  3.36 us

profile of v5, /device:TPU:1, one launch (start us, length us, event | category | flops | bytes accessed | tf_op | source)
XLA Modules:
  0.0 94.0 jit_solution(12928955346950128946)
XLA Ops:
  0.6 0.9 reshape.10
  1.5 0.2 copy.11
  1.7 0.1 copy.12.lists
  1.8 0.0 copy-start
  1.8 0.8 copy-done
  2.6 0.0 copy-start.3
  2.6 0.7 copy-done.3
  3.3 0.0 copy-start.5
  3.3 0.7 copy-done.5
  4.0 0.0 copy-start.7
  4.0 0.7 copy-done.7
  4.7 0.0 copy-start.9
  4.7 0.7 copy-done.9
  5.4 0.0 copy-start.11
  5.4 0.8 copy-done.11
  6.1 4.5 %owner_gather.1.refs_0_ = f32[128,8,128]{2,1,0:T(8,128)S(1)} custom-call(s32[1,8192]{1,0:T(1,128)S(1)} %copy-done, f32[2,2048]{1,0:T(2,128)S(1)} %copy-done.3, f32[2,2048]{1,0:T(2,128)S(1)} %copy-done.5, f32[1,2048]{1,0:T(1,128)S(1)} %copy-done.7, f32[1,2048]{1,0:T(1,128)S(1)} %copy-done.9, f32[3,2048]{1,0:T(4,128)S(1)} %copy-done.11), custom_call_target="tpu_custom_call" | custom-call | tf_op jit(solution)/shard_map/owner_gather/pallas_call | solution.py:683
  10.6 0.0 copy-start.2
  10.6 0.9 copy-done.2
  11.5 17.4 %exchange.2 = (f32[128,8,128]{2,1,0:T(8,128)S(1)}, f32[3,16,384]{2,1,0:T(8,128)S(1)}, f32[3,16,384]{2,1,0:T(8,128)S(1)}, f32[3,16,384]{2,1,0:T(8,128)S(1)}) custom-call(f32[128,8,128]{2,1,0:T(8,128)S(1)} %owner_gather.1.refs_0_, f32[3,16,384]{2,1,0:T(8,128)S(1)} %copy-done.2), custom_call_target="tpu_custom_call" | custom-call | tf_op jit(solution)/shard_map/exchange/pallas_call | solution.py:177
  28.9 19.3 %tile_forward.1 = (f32[3,16,384]{2,1,0:T(8,128)}, f32[3,16,384]{2,1,0:T(8,128)S(1)}, f32[24,3,2,8,256]{4,3,2,1,0:T(8,128)S(1)}, f32[24,2,8,256]{3,2,1,0:T(8,128)S(1)}, bf16[24,512,32]{2,1,0:T(8,128)(2,1)S(1)}) custom-call(s32[24,1,512]{2,1,0:T(1,128)S(1)} %copy.12.lists, f32[128,8,128]{2,1,0:T(8,128)S(1)} %get-tuple-element.13.recv), custom_call_target="tpu_custom_call" | custom-call | tf_op jit(solution)/shard_map/tile_forward/pallas_call | solution.py:700
  48.3 6.7 %halo.1 = (f32[3,16,384]{2,1,0:T(8,128)S(1)}, f32[3,16,384]{2,1,0:T(8,128)S(1)}) custom-call(f32[3,16,384]{2,1,0:T(8,128)S(1)} %get-tuple-element.16.strip.centre), custom_call_target="tpu_custom_call" | custom-call | tf_op jit(solution)/shard_map/halo/pallas_call | solution.py:204
  55.0 3.4 %loss_gradient.1.grad = f32[3,16,384]{2,1,0:T(8,128)S(1)} custom-call(f32[3,16,384]{2,1,0:T(8,128)S(1)} %get-tuple-element.17.before, f32[3,16,384]{2,1,0:T(8,128)S(1)} %get-tuple-element.16.strip.centre, f32[3,16,384]{2,1,0:T(8,128)S(1)} %get-tuple-element.18.after, f32[3,16,384]{2,1,0:T(8,128)S(1)} %get-tuple-element.19.t_before, ...), custom_call_target="tpu_custom_call" | custom-call | tf_op jit(solution)/shard_map/loss_gradient/pallas_call | solution.py:728
  58.4 0.0 copy-start.1
  58.4 0.0 copy-start.4
  58.4 0.0 copy-start.6
  58.4 0.0 copy-start.8
  58.4 0.0 copy-start.10
  58.4 16.6 %tile_backward.1.refs_0_ = f32[128,8,128]{2,1,0:T(8,128)S(1)} custom-call(s32[24,1,512]{2,1,0:T(1,128)S(1)} %copy.12.lists, bf16[24,512,32]{2,1,0:T(8,128)(2,1)S(1)} %get-tuple-element.15.left_in, f32[3,16,384]{2,1,0:T(8,128)S(1)} %loss_gradient.1.grad, f32[24,3,2,8,256]{4,3,2,1,0:T(8,128)S(1)} %get-tuple-element.22.chunk_rend, ...), custom_call_target="tpu_custom_call" | custom-call | tf_op jit(solution)/shard_map/tile_backward/pallas_call | solution.py:736
  75.0 15.4 %exchange.3.back = f32[128,8,128]{2,1,0:T(8,128)S(1)} custom-call(f32[128,8,128]{2,1,0:T(8,128)S(1)} %tile_backward.1.refs_0_), custom_call_target="tpu_custom_call" | custom-call | tf_op jit(solution)/shard_map/exchange/pallas_call | solution.py:177
  90.4 0.0 copy-done.1
  90.4 0.0 copy-done.4
  90.5 0.0 copy-done.6
  90.5 0.0 copy-done.8
  90.5 0.0 copy-done.10
  90.5 3.5 %owner_scatter.1 = f32[9,2048]{1,0:T(8,128)} custom-call(f32[128,8,128]{2,1,0:T(8,128)S(1)} %exchange.3.back, s32[1,8192]{1,0:T(1,128)S(1)} %copy-done.1, f32[2,2048]{1,0:T(2,128)S(1)} %copy-done.4, f32[2,2048]{1,0:T(2,128)S(1)} %copy-done.6, f32[1,2048]{1,0:T(1,128)S(1)} %copy-done.8, f32[1,2048]{1,0:T(1,128)S(1)} %copy-done.10), custom_call_target="tpu_custom_call" | custom-call | tf_op jit(solution)/shard_map/owner_scatter/pallas_call | solution.py:755
Async XLA Ops:
  1.8 0.8 copy-start
  2.6 0.7 copy-start.3
  3.3 0.7 copy-start.5
  4.0 0.7 copy-start.7
  4.7 0.7 copy-start.9
  5.4 0.8 copy-start.11
  10.6 0.9 copy-start.2
  58.4 32.1 %copy-start.1 = (s32[1,8192]{1,0:T(1,128)S(1)}, s32[1,8192]{1,0:T(1,128)}, u32[]{:S(2)}) copy-start(s32[1,8192]{1,0:T(1,128)} %send.1) | copy-start | bytes 98308
  58.4 32.1 %copy-start.4 = (f32[2,2048]{1,0:T(2,128)S(1)}, f32[2,2048]{1,0:T(2,128)}, u32[]{:S(2)}) copy-start(f32[2,2048]{1,0:T(2,128)} %centres.1) | copy-start | bytes 49156
  58.4 32.1 %copy-start.6 = (f32[2,2048]{1,0:T(2,128)S(1)}, f32[2,2048]{1,0:T(2,128)}, u32[]{:S(2)}) copy-start(f32[2,2048]{1,0:T(2,128)} %conic.1) | copy-start | bytes 49156
  58.4 32.1 %copy-start.8 = (f32[1,2048]{1,0:T(1,128)S(1)}, f32[1,2048]{1,0:T(1,128)}, u32[]{:S(2)}) copy-start(f32[1,2048]{1,0:T(1,128)} %rho.1) | copy-start | bytes 24580
  58.4 32.1 %copy-start.10 = (f32[1,2048]{1,0:T(1,128)S(1)}, f32[1,2048]{1,0:T(1,128)}, u32[]{:S(2)}) copy-start(f32[1,2048]{1,0:T(1,128)} %opacity.1) | copy-start | bytes 24580

commit v6 on v5

--- a/solution.py
+++ b/solution.py
@@ -60,38 +60,6 @@
     return eight, sub_sum(jnp.where(lax.bitwise_and(hi, 7) == row, last, 0.0))
 
 
-def owner_kernel(*refs):
-    sources, (out, table, ninth), places, sems = refs[:6], refs[6:9], refs[9:15], refs[15]
-    copies = [pltpu.make_async_copy(a, b, sems.at[k]) for k, (a, b) in enumerate(zip(sources, places))]
-    for copy in copies:
-        copy.start()
-    for copy in copies:
-        copy.wait()
-    send, centres, conic, rho, opacity, colors = places
-    rows = coefficient_rows(
-        centres[0:1, :], centres[1:2, :], conic[0:1, :], conic[1:2, :], rho[...], opacity[...]
-    )
-    for p, row in enumerate(rows + [colors[0:1, :], colors[1:2, :]]):
-        table[p : p + 1, :] = row
-    blocks = table.shape[1] // LANE
-    for h in range(blocks):
-        ninth[h : h + 1, :] = colors[2:3, h * LANE : (h + 1) * LANE]
-    left = iota((SUB, LANE), 1) < 64
-    row = iota((SUB, LANE), 0)
-    step = 4
-
-    def pairs(ii, carry):
-        for k in range(step):
-            i = ii * step + k
-            start = pl.multiple_of(i * LANE, LANE)
-            idx = jnp.broadcast_to(jnp.maximum(send[0:1, pl.ds(start, LANE)], 0), (SUB, LANE))
-            eight, last = pick_nine(lambda h: table[:, h * LANE : (h + 1) * LANE], ninth, idx, row, blocks)
-            out[2 * i], out[2 * i + 1] = pack_pair(eight, last, left, row)
-        return carry
-
-    lax.fori_loop(0, send.shape[1] // LANE // step, pairs, 0)
-
-
 MESH = pl.DeviceIdType.MESH
 USED = 5
 
@@ -130,11 +98,116 @@
     ]
 
 
-def exchange_kernel(halo, *refs):
-    if halo:
-        x, strip, out, before, centre, after, local_sem, send_sem, recv_sem, halo_send, halo_recv = refs
-    else:
-        x, out, local_sem, send_sem, recv_sem = refs
+def send_owned_kernel(*refs):
+    sources, strip, (out, before, centre, after), x, table, ninth = refs[:6], refs[6], refs[7:11], *refs[11:14]
+    places, (local_sem, send_sem, recv_sem, halo_send, halo_recv) = refs[14:20], refs[20:25]
+    me = lax.axis_index("dev")
+    n = lax.axis_size("dev")
+    fetched = [pltpu.make_async_copy(a, b, local_sem.at[k]) for k, (a, b) in enumerate(zip(sources, places))]
+    for copy in fetched:
+        copy.start()
+    barrier = greet_all(n, me)
+    for copy in fetched:
+        copy.wait()
+    send, centres, conic, rho, opacity, colors = places
+    rows = coefficient_rows(
+        centres[0:1, :], centres[1:2, :], conic[0:1, :], conic[1:2, :], rho[...], opacity[...]
+    )
+    for p, value in enumerate(rows + [colors[0:1, :], colors[1:2, :]]):
+        table[p : p + 1, :] = value
+    blocks = table.shape[1] // LANE
+    for h in range(blocks):
+        ninth[h : h + 1, :] = colors[2:3, h * LANE : (h + 1) * LANE]
+    left = iota((SUB, LANE), 1) < 64
+    row = iota((SUB, LANE), 0)
+    pairs = n // 2
+    mine = me // 2
+    used = pl.ds(0, USED)
+    step = 4
+
+    def fill(group):
+        for k in range(step):
+            i = lax.rem(mine + group * step + k, pairs)
+            start = pl.multiple_of(i * LANE, LANE)
+            idx = jnp.broadcast_to(jnp.maximum(send[0:1, pl.ds(start, LANE)], 0), (SUB, LANE))
+            eight, last = pick_nine(lambda h: table[:, h * LANE : (h + 1) * LANE], ninth, idx, row, blocks)
+            x[2 * i], x[2 * i + 1] = pack_pair(eight, last, left, row)
+
+    def ship(k):
+        for core in range(2):
+            peer = 2 * lax.rem(mine + k, pairs) + core
+            pltpu.make_async_remote_copy(
+                src_ref=x.at[peer, used], dst_ref=out.at[me, used], send_sem=send_sem, recv_sem=recv_sem,
+                device_id=(peer,), device_id_type=MESH,
+            ).start()
+
+    copies = halo_copies(n, me, strip, before, after, halo_send, halo_recv)
+    copies.append(pltpu.make_async_copy(strip, centre, halo_recv.at[2]))
+    early = 5
+
+    def first(group, carry):
+        fill(group)
+        return carry
+
+    lax.fori_loop(0, early, first, 0)
+    pl.semaphore_wait(barrier, n - 1)
+    for copy in copies:
+        copy.start()
+    partner = me + 1 - 2 * lax.rem(me, 2)
+    own = pltpu.make_async_copy(x.at[me, used], out.at[me, used], local_sem.at[6])
+    own.start()
+    pltpu.make_async_remote_copy(
+        src_ref=x.at[partner, used], dst_ref=out.at[me, used], send_sem=send_sem, recv_sem=recv_sem,
+        device_id=(partner,), device_id_type=MESH,
+    ).start()
+
+    def ship_one(k, carry):
+        ship(k)
+        return carry
+
+    lax.fori_loop(1, (early - 1) * step, ship_one, 0)
+
+    def both(group, carry):
+        for k in range(step):
+            ship((group - 1) * step + k)
+        fill(group)
+        return carry
+
+    lax.fori_loop(early, pairs // step, both, 0)
+    lax.fori_loop(pairs - step, pairs, ship_one, 0)
+    own.wait()
+    rest = pl.ds(0, n - 1)
+    pltpu.make_async_copy(x.at[rest, used], x.at[rest, used], send_sem).wait()
+    pltpu.make_async_copy(out.at[rest, used], out.at[rest, used], recv_sem).wait()
+    for copy in copies:
+        copy.wait()
+
+
+def send_owned(sources, strip, number):
+    devices, owned = lax.axis_size("dev"), sources[1].shape[1]
+    vmem, hbm = pl.BlockSpec(memory_space=pltpu.VMEM), pl.BlockSpec(memory_space=pltpu.HBM)
+    return pl.pallas_call(
+        send_owned_kernel,
+        out_shape=[struct(devices, SUB, LANE)] + [struct(*strip.shape)] * 3,
+        in_specs=[hbm] * 7,
+        out_specs=[hbm] * 4,
+        scratch_shapes=[
+            pltpu.VMEM((devices, SUB, LANE), F32),
+            pltpu.VMEM((SUB, owned), F32),
+            pltpu.VMEM((owned // LANE, LANE), F32),
+        ]
+        + [pltpu.VMEM(v.shape, v.dtype) for v in sources]
+        + [pltpu.SemaphoreType.DMA((7,))]
+        + [pltpu.SemaphoreType.DMA] * 2
+        + [pltpu.SemaphoreType.DMA((3,))] * 2,
+        compiler_params=pltpu.CompilerParams(
+            collective_id=number, has_side_effects=True, vmem_limit_bytes=60 * 1024 * 1024
+        ),
+        name="owner_send",
+    )(*sources, strip)
+
+
+def exchange_kernel(x, out, local_sem, send_sem, recv_sem):
     me = lax.axis_index("dev")
     n = lax.axis_size("dev")
     rows = pl.ds(0, USED)
@@ -152,37 +225,27 @@
         return carry
 
     lax.fori_loop(1, n, start, 0)
-    copies = []
-    if halo:
-        copies = halo_copies(n, me, strip, before, after, halo_send, halo_recv)
-        copies.append(pltpu.make_async_copy(strip, centre, halo_recv.at[2]))
-    for copy in copies:
-        copy.start()
     own.wait()
     rest = pl.ds(0, n - 1)
     pltpu.make_async_copy(x.at[rest, rows], x.at[rest, rows], send_sem).wait()
     pltpu.make_async_copy(out.at[rest, rows], out.at[rest, rows], recv_sem).wait()
-    for copy in copies:
-        copy.wait()
 
 
 def comm_params(number):
     return pltpu.CompilerParams(collective_id=number, has_side_effects=True, vmem_limit_bytes=4 << 20)
 
 
-def exchange(x, number, strip=None):
+def exchange(x, number):
     vmem = pl.BlockSpec(memory_space=pltpu.VMEM)
-    halo = strip is not None
-    like = lambda v: jax.ShapeDtypeStruct(v.shape, v.dtype)
     return pl.pallas_call(
-        functools.partial(exchange_kernel, halo),
-        out_shape=[like(x)] + [like(strip)] * 3 if halo else like(x),
-        in_specs=[vmem] + [pl.BlockSpec(memory_space=pltpu.HBM)] * halo,
-        out_specs=[vmem] * 4 if halo else vmem,
-        scratch_shapes=[pltpu.SemaphoreType.DMA] * 3 + [pltpu.SemaphoreType.DMA((3,))] * (2 if halo else 0),
+        exchange_kernel,
+        out_shape=jax.ShapeDtypeStruct(x.shape, x.dtype),
+        in_specs=[vmem],
+        out_specs=vmem,
+        scratch_shapes=[pltpu.SemaphoreType.DMA] * 3,
         compiler_params=comm_params(number),
         name="exchange",
-    )(*([x, strip] if halo else [x]))
+    )(x)
 
 
 def halo_kernel(strip, before, after, send_sem, recv_sem):
@@ -680,19 +743,8 @@
     pixels = height * height
     params = lambda mib: pltpu.CompilerParams(vmem_limit_bytes=mib << 20)
     sources = (send_rows, centres, conic, rho, opacity, colors)
-    outgoing = pl.pallas_call(
-        owner_kernel,
-        in_specs=[pl.BlockSpec(memory_space=pltpu.HBM)] * 6,
-        out_shape=struct(devices, SUB, LANE),
-        scratch_shapes=[pltpu.VMEM((SUB, owned), F32), pltpu.VMEM((owned // LANE, LANE), F32)]
-        + [pltpu.VMEM(v.shape, v.dtype) for v in sources]
-        + [pltpu.SemaphoreType.DMA((6,))],
-        compiler_params=params(8),
-        name="owner_gather",
-    )(*sources)
-
     lists = tile_lists.reshape(tiles, SUB, count // SUB).transpose(0, 2, 1).reshape(tiles, 1, count)
-    incoming, t_before, t_centre, t_after = exchange(outgoing, 0, target)
+    incoming, t_before, t_centre, t_after = send_owned(sources, target, 0)
     whole = lambda *shape: pl.BlockSpec(shape, lambda t: (0,) * len(shape))
     per = 2
     per_tile = lambda *shape: pl.BlockSpec((per,) + shape, lambda t: (t,) + (0,) * len(shape))

time: 94.5 us -> 88.9 us (0.941)
  Pallas kernels: 86.8 us -> 82.9 us
  local copies, waits for them, and re-layouts: 6.4 us -> 4.86 us
    pallas_call x3 -> x2, Pallas kernels: 37.3 us -> 34.1 us  [the longest x1 18.7 us: send_owned(): pl.pallas_call(send_owned_kernel, out_shape=[struct(devices, SUB, LANE)]...]
    unnamed x24 -> x18, local copies, waits for them, and re-layouts: 5.26 us -> 3.71 us
where the time goes in v6:
time: 88.9 us; the launch traced here: 88.5 us
  Pallas kernels  82.9 us (93%)
  local copies, waits for them, and re-layouts  4.86 us (5%)
    pallas_call x1, Pallas kernels, shards(): pl.pallas_call(forward_kernel, grid=(tiles // per,), in_specs=[whole(tile...  19.3 us
    pallas_call x1, Pallas kernels, send_owned(): pl.pallas_call(send_owned_kernel, out_shape=[struct(devices, SUB, LANE)]...  18.7 us
    pallas_call x1, Pallas kernels, shards(): pl.pallas_call(backward_kernel, grid=(tiles // per,), in_specs=[whole(til...  16.6 us
    pallas_call x1, Pallas kernels, exchange(): pl.pallas_call(exchange_kernel, out_shape=jax.ShapeDtypeStruct(x.shape, x...  15.5 us
    pallas_call x1, Pallas kernels, halo_strips(): pl.pallas_call(halo_kernel, out_shape=[jax.ShapeDtypeStruct(strip.shape,...  5.95 us
    unnamed x18, local copies, waits for them, and re-layouts  3.71 us
    pallas_call x1, Pallas kernels, shards(): pl.pallas_call(home_kernel, out_shape=struct(9, owned), scratch_shapes=[p...  3.52 us
    pallas_call x1, Pallas kernels, shards(): pl.pallas_call(loss_kernel, out_shape=struct(3, height, width), scratch_s...  3.35 us

profile of v6, /device:TPU:1, one launch (start us, length us, event | category | flops | bytes accessed | tf_op | source)
XLA Modules:
  0.0 88.5 jit_solution(11024627931653502512)
XLA Ops:
  0.6 0.9 reshape.10
  1.5 0.2 copy.11
  1.7 0.1 copy.12.lists
  1.8 18.7 %owner_send.1 = (f32[128,8,128]{2,1,0:T(8,128)}, f32[3,16,384]{2,1,0:T(8,128)}, f32[3,16,384]{2,1,0:T(8,128)}, f32[3,16,384]{2,1,0:T(8,128)}) custom-call(s32[1,8192]{1,0:T(1,128)} %send.1, f32[2,2048]{1,0:T(2,128)} %centres.1, f32[2,2048]{1,0:T(2,128)} %conic.1, f32[1,2048]{1,0:T(1,128)} %rho.1, f32[1,2048]{1,0:T(1,128)} %opacity.1, f32[3,2048]{1,0:T(4,128)} %refs_5_.1, ...), custom_call_target="tpu_custom_call" | custom-call | tf_op jit(solution)/shard_map/owner_send/pallas_call | solution.py:189
  20.4 0.0 copy-start
  20.5 1.0 %copy-done = f32[128,8,128]{2,1,0:T(8,128)S(1)} copy-done((f32[128,8,128]{2,1,0:T(8,128)S(1)}, f32[128,8,128]{2,1,0:T(8,128)}, u32[]{:S(2)}) %copy-start) | copy-done | bytes 524312
  21.5 19.3 %tile_forward.1 = (f32[3,16,384]{2,1,0:T(8,128)}, f32[3,16,384]{2,1,0:T(8,128)S(1)}, f32[24,3,2,8,256]{4,3,2,1,0:T(8,128)S(1)}, f32[24,2,8,256]{3,2,1,0:T(8,128)S(1)}, bf16[24,512,32]{2,1,0:T(8,128)(2,1)S(1)}) custom-call(s32[24,1,512]{2,1,0:T(1,128)S(1)} %copy.12.lists, f32[128,8,128]{2,1,0:T(8,128)S(1)} %copy-done), custom_call_target="tpu_custom_call" | custom-call | tf_op jit(solution)/shard_map/tile_forward/pallas_call | solution.py:752
  40.8 5.9 %halo.1 = (f32[3,16,384]{2,1,0:T(8,128)S(1)}, f32[3,16,384]{2,1,0:T(8,128)S(1)}) custom-call(f32[3,16,384]{2,1,0:T(8,128)S(1)} %get-tuple-element.16.strip.centre), custom_call_target="tpu_custom_call" | custom-call | tf_op jit(solution)/shard_map/halo/pallas_call | solution.py:267
  46.8 0.0 copy-start.2
  46.8 0.9 copy-done.2
  47.6 0.0 copy-start.3
  47.6 0.9 copy-done.3
  48.5 0.0 copy-start.4
  48.5 0.9 copy-done.4
  49.4 3.4 %loss_gradient.1.grad = f32[3,16,384]{2,1,0:T(8,128)S(1)} custom-call(f32[3,16,384]{2,1,0:T(8,128)S(1)} %get-tuple-element.17.before, f32[3,16,384]{2,1,0:T(8,128)S(1)} %get-tuple-element.16.strip.centre, f32[3,16,384]{2,1,0:T(8,128)S(1)} %get-tuple-element.18.after, f32[3,16,384]{2,1,0:T(8,128)S(1)} %copy-done.2, f32[3,16,384]{2,1,0:T(8,128)S(1)} %copy-done.3, ...), custom_call_target="tpu_custom_call" | custom-call | tf_op jit(solution)/shard_map/loss_gradient/pallas_call | solution.py:780
  52.8 0.0 copy-start.1
  52.8 0.0 copy-start.5
  52.8 0.0 copy-start.6
  52.8 0.0 copy-start.7
  52.8 0.0 copy-start.8
  52.8 16.6 %tile_backward.1.x = f32[128,8,128]{2,1,0:T(8,128)S(1)} custom-call(s32[24,1,512]{2,1,0:T(1,128)S(1)} %copy.12.lists, bf16[24,512,32]{2,1,0:T(8,128)(2,1)S(1)} %get-tuple-element.15.left_in, f32[3,16,384]{2,1,0:T(8,128)S(1)} %loss_gradient.1.grad, f32[24,3,2,8,256]{4,3,2,1,0:T(8,128)S(1)} %get-tuple-element.22.chunk_rend, ...), custom_call_target="tpu_custom_call" | custom-call | tf_op jit(solution)/shard_map/tile_backward/pallas_call | solution.py:788
  69.5 15.5 %exchange.1.back = f32[128,8,128]{2,1,0:T(8,128)S(1)} custom-call(f32[128,8,128]{2,1,0:T(8,128)S(1)} %tile_backward.1.x), custom_call_target="tpu_custom_call" | custom-call | tf_op jit(solution)/shard_map/exchange/pallas_call | solution.py:240
  84.9 0.0 copy-done.1
  85.0 0.0 copy-done.5
  85.0 0.0 copy-done.6
  85.0 0.0 copy-done.7
  85.0 0.0 copy-done.8
  85.0 3.5 %owner_scatter.1 = f32[9,2048]{1,0:T(8,128)} custom-call(f32[128,8,128]{2,1,0:T(8,128)S(1)} %exchange.1.back, s32[1,8192]{1,0:T(1,128)S(1)} %copy-done.1, f32[2,2048]{1,0:T(2,128)S(1)} %copy-done.5, f32[2,2048]{1,0:T(2,128)S(1)} %copy-done.6, f32[1,2048]{1,0:T(1,128)S(1)} %copy-done.7, f32[1,2048]{1,0:T(1,128)S(1)} %copy-done.8), custom_call_target="tpu_custom_call" | custom-call | tf_op jit(solution)/shard_map/owner_scatter/pallas_call | solution.py:807
Async XLA Ops:
  20.4 1.0 %copy-start = (f32[128,8,128]{2,1,0:T(8,128)S(1)}, f32[128,8,128]{2,1,0:T(8,128)}, u32[]{:S(2)}) copy-start(f32[128,8,128]{2,1,0:T(8,128)} %get-tuple-element.13.recv) | copy-start | bytes 1572868
  46.8 0.9 %copy-start.2 = (f32[3,16,384]{2,1,0:T(8,128)S(1)}, f32[3,16,384]{2,1,0:T(8,128)}, u32[]{:S(2)}) copy-start(f32[3,16,384]{2,1,0:T(8,128)} %get-tuple-element.19.t_before) | copy-start | bytes 221188
  47.6 0.9 copy-start.3
  48.5 0.9 copy-start.4
  52.8 32.2 %copy-start.1 = (s32[1,8192]{1,0:T(1,128)S(1)}, s32[1,8192]{1,0:T(1,128)}, u32[]{:S(2)}) copy-start(s32[1,8192]{1,0:T(1,128)} %send.1) | copy-start | bytes 98308
  52.8 32.2 %copy-start.5 = (f32[2,2048]{1,0:T(2,128)S(1)}, f32[2,2048]{1,0:T(2,128)}, u32[]{:S(2)}) copy-start(f32[2,2048]{1,0:T(2,128)} %centres.1) | copy-start | bytes 49156
  52.8 32.2 %copy-start.6 = (f32[2,2048]{1,0:T(2,128)S(1)}, f32[2,2048]{1,0:T(2,128)}, u32[]{:S(2)}) copy-start(f32[2,2048]{1,0:T(2,128)} %conic.1) | copy-start | bytes 49156
  52.8 32.2 %copy-start.7 = (f32[1,2048]{1,0:T(1,128)S(1)}, f32[1,2048]{1,0:T(1,128)}, u32[]{:S(2)}) copy-start(f32[1,2048]{1,0:T(1,128)} %rho.1) | copy-start | bytes 24580
  52.8 32.2 %copy-start.8 = (f32[1,2048]{1,0:T(1,128)S(1)}, f32[1,2048]{1,0:T(1,128)}, u32[]{:S(2)}) copy-start(f32[1,2048]{1,0:T(1,128)} %opacity.1) | copy-start | bytes 24580

commit v7 on v6

--- a/solution.py
+++ b/solution.py
@@ -62,6 +62,8 @@
 
 MESH = pl.DeviceIdType.MESH
 USED = 5
+RIM = 10
+RIMS = 32
 
 
 def pack_pair(eight, last, left, row):
@@ -99,8 +101,8 @@
 
 
 def send_owned_kernel(*refs):
-    sources, strip, (out, before, centre, after), x, table, ninth = refs[:6], refs[6], refs[7:11], *refs[11:14]
-    places, (local_sem, send_sem, recv_sem, halo_send, halo_recv) = refs[14:20], refs[20:25]
+    sources, strip, (out, strips), x, table, ninth = refs[:6], refs[6], refs[7:9], *refs[9:12]
+    places, (local_sem, send_sem, recv_sem, halo_send, halo_recv) = refs[12:18], refs[18:23]
     me = lax.axis_index("dev")
     n = lax.axis_size("dev")
     fetched = [pltpu.make_async_copy(a, b, local_sem.at[k]) for k, (a, b) in enumerate(zip(sources, places))]
@@ -141,8 +143,8 @@
                 device_id=(peer,), device_id_type=MESH,
             ).start()
 
-    copies = halo_copies(n, me, strip, before, after, halo_send, halo_recv)
-    copies.append(pltpu.make_async_copy(strip, centre, halo_recv.at[2]))
+    copies = halo_copies(n, me, strip, strips.at[0], strips.at[2], halo_send, halo_recv)
+    copies.append(pltpu.make_async_copy(strip, strips.at[1], halo_recv.at[2]))
     early = 5
 
     def first(group, carry):
@@ -188,9 +190,9 @@
     vmem, hbm = pl.BlockSpec(memory_space=pltpu.VMEM), pl.BlockSpec(memory_space=pltpu.HBM)
     return pl.pallas_call(
         send_owned_kernel,
-        out_shape=[struct(devices, SUB, LANE)] + [struct(*strip.shape)] * 3,
+        out_shape=[struct(devices, SUB, LANE), struct(3, *strip.shape)],
         in_specs=[hbm] * 7,
-        out_specs=[hbm] * 4,
+        out_specs=[hbm] * 2,
         scratch_shapes=[
             pltpu.VMEM((devices, SUB, LANE), F32),
             pltpu.VMEM((SUB, owned), F32),
@@ -246,33 +248,6 @@
         compiler_params=comm_params(number),
         name="exchange",
     )(x)
-
-
-def halo_kernel(strip, before, after, send_sem, recv_sem):
-    me = lax.axis_index("dev")
-    n = lax.axis_size("dev")
-    barrier = pltpu.get_barrier_semaphore()
-    for hop in (1, n - 1):
-        pl.semaphore_signal(barrier, inc=1, device_id=(lax.rem(me + hop, n),), device_id_type=MESH)
-    pl.semaphore_wait(barrier, 2)
-    copies = halo_copies(n, me, strip, before, after, send_sem, recv_sem)
-    for copy in copies:
-        copy.start()
-    for copy in copies:
-        copy.wait()
-
-
-def halo_strips(strip, number):
-    vmem = pl.BlockSpec(memory_space=pltpu.VMEM)
-    return pl.pallas_call(
-        halo_kernel,
-        out_shape=[jax.ShapeDtypeStruct(strip.shape, strip.dtype)] * 2,
-        in_specs=[vmem],
-        out_specs=[vmem] * 2,
-        scratch_shapes=[pltpu.SemaphoreType.DMA((2,))] * 2,
-        compiler_params=comm_params(number),
-        name="halo",
-    )(strip)
 
 
 def block_transpose(x):
@@ -411,7 +386,7 @@
 
 
 def forward_kernel(
-    lists, recv, image, image_too, chunk_rend, chunk_start, left_out, pieces, ninth, flat, cols, alphas, rends
+    lists, recv, image, image_too, head, tail, chunk_rend, chunk_start, left_out, pieces, ninth, flat, cols, alphas, rends
 ):
     step = pl.program_id(0)
     row = iota((SUB, LANE), 0)
@@ -454,8 +429,16 @@
             for g in range(rends.shape[1] // SUB):
                 for h in range(2):
                     block = block_transpose(rends[ch, g * SUB : (g + 1) * SUB, h * LANE : (h + 1) * LANE])
+                    span = slice(g * LANE, (g + 1) * LANE)
                     for to in (image, image_too):
-                        to[ch, h * SUB : (h + 1) * SUB, g * LANE : (g + 1) * LANE] = block
+                        to[ch, h * SUB : (h + 1) * SUB, span] = block
+                    at = RIM * ch
+                    if h == 0:
+                        head[at : at + SUB, span] = block
+                        tail[at : at + 2, span] = block[6:8, :]
+                    else:
+                        head[at + SUB : at + RIM, span] = block[0:2, :]
+                        tail[at + 2 : at + RIM, span] = block
 
 
 def taps_of():
@@ -485,31 +468,70 @@
     return total
 
 
-def loss_kernel(before, centre, after, t_before, t_centre, t_after, grad, pads, maps):
-    height = centre.shape[1]
-    mine = lax.axis_index("dev")
-    total_rows = lax.axis_size("dev") * height
-    width = centre.shape[2]
-    at = iota((2 * height, width), 0) - height // 2 + mine * height
-    inside = (at >= 0) & (at < total_rows)
+def loss_kernel(
+    centre, head, tail, target, grad, before, after, pads, maps, blurred, send_sem, recv_sem
+):
+    height, width = centre.shape[1:]
+    me = lax.axis_index("dev")
+    n = lax.axis_size("dev")
+    barrier = pltpu.get_barrier_semaphore()
+    for hop in (1, n - 1):
+        pl.semaphore_signal(barrier, inc=1, device_id=(lax.rem(me + hop, n),), device_id_type=MESH)
+    rim = RIM
+    copies = []
+    for part in range(RIMS // SUB):
+        rows = pl.ds(part * SUB, SUB)
+        for k, (hop, source, to) in enumerate(((1, tail, before), (n - 1, head, after))):
+            copies.append(
+                pltpu.make_async_remote_copy(
+                    src_ref=source.at[rows], dst_ref=to.at[rows],
+                    send_sem=send_sem.at[2 * part + k], recv_sem=recv_sem.at[2 * part + k],
+                    device_id=(lax.rem(me + hop, n),), device_id_type=MESH,
+                )
+            )
+    t_before, t_centre, t_after = target.at[0], target.at[1], target.at[2]
+    pl.semaphore_wait(barrier, 2)
+    for copy in copies:
+        copy.start()
+
+    at = iota((2 * height, width), 0) - height // 2 + me * height
+    inside = (at >= 0) & (at < n * height)
+
+    def wide_blur(k):
+        vertical = blur_rows(lambda s, c: pads[k, s : s + c, :], height // 2, 2 * height)
+        return blur_lanes(vertical)
+
+    edge = height - rim
+    for k in range(5):
+        pads[k, 0:edge, :] = jnp.zeros((edge, width), F32)
+        pads[k, 3 * height - edge :, :] = jnp.zeros((edge, width), F32)
     for ch in range(3):
-        for i, (r, t) in enumerate(((before, t_before), (centre, t_centre), (after, t_after))):
-            span = slice(i * height, (i + 1) * height)
-            rr, tt = r[ch], t[ch]
-            if i != 1:
-                keep = mine > 0 if i == 0 else mine < total_rows // height - 1
-                rr, tt = jnp.where(keep, rr, 0.0), jnp.where(keep, tt, 0.0)
-            pads[0, span, :] = rr
-            pads[1, span, :] = tt
-            pads[2, span, :] = rr * rr
-            pads[3, span, :] = tt * tt
-            pads[4, span, :] = rr * tt
-
-        def wide_blur(k):
-            vertical = blur_rows(lambda s, n: pads[k, s : s + n, :], height // 2, 2 * height)
-            return blur_lanes(vertical)
-
-        mr, mt, rr, tt, rt = (wide_blur(k) for k in range(5))
+        first = jnp.where(me > 0, t_before[ch, edge:height, :], 0.0)
+        last = jnp.where(me < n - 1, t_after[ch, 0:rim, :], 0.0)
+        for rows, tt in (
+            (slice(edge, height), first), (slice(height, 2 * height), t_centre[ch]),
+            (slice(2 * height, 2 * height + rim), last),
+        ):
+            pads[1, rows, :] = tt
+            pads[3, rows, :] = tt * tt
+        blurred[ch, 0] = wide_blur(1)
+        blurred[ch, 1] = wide_blur(3)
+
+    for ch in range(3):
+        for copy in copies[:4] if ch == 0 else copies[2 * ch + 2 : 2 * ch + 4]:
+            copy.wait_recv()
+        for rows, keep, r, t in (
+            (slice(edge, height), me > 0, before[rim * ch : rim * (ch + 1), :], t_before[ch, edge:height, :]),
+            (slice(height, 2 * height), None, centre[ch], t_centre[ch]),
+            (slice(2 * height, 2 * height + rim), me < n - 1, after[rim * ch : rim * (ch + 1), :], t_after[ch, 0:rim, :]),
+        ):
+            if keep is not None:
+                r, t = jnp.where(keep, r, 0.0), jnp.where(keep, t, 0.0)
+            pads[0, rows, :] = r
+            pads[2, rows, :] = r * r
+            pads[4, rows, :] = r * t
+        mr, rr, rt = wide_blur(0), wide_blur(2), wide_blur(4)
+        mt, tt = blurred[ch, 0], blurred[ch, 1]
         cv = rt - mr * mt
         top1 = 2.0 * mr * mt + 0.0001
         top2 = 2.0 * cv + 0.0009
@@ -525,12 +547,14 @@
             maps[k] = jnp.where(inside, value, 0.0)
 
         def back_blur(k):
-            vertical = blur_rows(lambda s, n: maps[k, s : s + n, :], height // 2, height)
+            vertical = blur_rows(lambda s, c: maps[k, s : s + c, :], height // 2, height)
             return blur_lanes(vertical)
 
         g_mr, g_rr, g_rt = (back_blur(k) for k in range(3))
         r, t = centre[ch], t_centre[ch]
         grad[ch] = 1.6 * (r - t) - 0.2 * (g_mr + 2.0 * r * g_rr + t * g_rt)
+    for copy in copies:
+        copy.wait_send()
 
 
 NT = (((1,), (1,)), ((), ()))
@@ -744,22 +768,24 @@
     params = lambda mib: pltpu.CompilerParams(vmem_limit_bytes=mib << 20)
     sources = (send_rows, centres, conic, rho, opacity, colors)
     lists = tile_lists.reshape(tiles, SUB, count // SUB).transpose(0, 2, 1).reshape(tiles, 1, count)
-    incoming, t_before, t_centre, t_after = send_owned(sources, target, 0)
+    incoming, t_strips = send_owned(sources, target, 0)
     whole = lambda *shape: pl.BlockSpec(shape, lambda t: (0,) * len(shape))
     per = 2
     per_tile = lambda *shape: pl.BlockSpec((per,) + shape, lambda t: (t,) + (0,) * len(shape))
     hi_blocks = devices * 64 // 256
-    image, image_too, chunk_rend, chunk_start, left = pl.pallas_call(
+    image, image_too, head, tail, chunk_rend, chunk_start, left = pl.pallas_call(
         forward_kernel,
         grid=(tiles // per,),
         in_specs=[whole(tiles, 1, count), whole(devices, SUB, LANE)],
         out_specs=[
-            whole(3, height, width), whole(3, height, width),
+            whole(3, height, width), whole(3, height, width), whole(RIMS, width), whole(RIMS, width),
             per_tile(3, 2, SUB, pixels), per_tile(2, SUB, pixels), per_tile(count, 32),
         ],
         out_shape=[
             struct(3, height, width),
             struct(3, height, width),
+            struct(RIMS, width),
+            struct(RIMS, width),
             struct(tiles, 3, 2, SUB, pixels),
             struct(tiles, 2, SUB, pixels),
             struct(tiles, count, 32, dtype=BF16),
@@ -776,14 +802,19 @@
         name="tile_forward",
     )(lists, incoming)
 
-    before, after = halo_strips(image_too, 1)
     pixel_grad = pl.pallas_call(
         loss_kernel,
         out_shape=struct(3, height, width),
-        scratch_shapes=[pltpu.VMEM((5, 3 * height, width), F32), pltpu.VMEM((3, 2 * height, width), F32)],
-        compiler_params=params(8),
+        scratch_shapes=[pltpu.VMEM((RIMS, width), F32)] * 2
+        + [
+            pltpu.VMEM((5, 3 * height, width), F32),
+            pltpu.VMEM((3, 2 * height, width), F32),
+            pltpu.VMEM((3, 2, 2 * height, width), F32),
+        ]
+        + [pltpu.SemaphoreType.DMA((8,))] * 2,
+        compiler_params=pltpu.CompilerParams(collective_id=1, has_side_effects=True, vmem_limit_bytes=8 << 20),
         name="loss_gradient",
-    )(before, image_too, after, t_before, t_centre, t_after)
+    )(image_too, head, tail, t_strips)
 
     slot_grads = pl.pallas_call(
         backward_kernel,

time: 88.9 us -> 86.1 us (0.969)
  local copies, waits for them, and re-layouts: 4.86 us -> 3.15 us
  Pallas kernels: 82.9 us -> 81.9 us
    pallas_call x2 -> x1, Pallas kernels: 24.6 us -> 18.7 us  [send_owned(): pl.pallas_call(send_owned_kernel, out_shape=[struct(devices, SUB, LANE),...]
    pallas_call x1, Pallas kernels: 3.35 us -> 8.77 us  [shards(): pl.pallas_call(loss_kernel, out_shape=struct(3, height, width), scratch_s...]
    unnamed x18 -> x14, local copies, waits for them, and re-layouts: 3.71 us -> 2 us
where the time goes in v7:
time: 86.1 us; the launch traced here: 85.8 us
  Pallas kernels  81.9 us (95%)
  local copies, waits for them, and re-layouts  3.15 us (4%)
    pallas_call x1, Pallas kernels, shards(): pl.pallas_call(forward_kernel, grid=(tiles // per,), in_specs=[whole(tile...  19.3 us
    pallas_call x1, Pallas kernels, send_owned(): pl.pallas_call(send_owned_kernel, out_shape=[struct(devices, SUB, LANE),...  18.7 us
    pallas_call x1, Pallas kernels, shards(): pl.pallas_call(backward_kernel, grid=(tiles // per,), in_specs=[whole(til...  16.6 us
    pallas_call x1, Pallas kernels, exchange(): pl.pallas_call(exchange_kernel, out_shape=jax.ShapeDtypeStruct(x.shape, x...  15 us
    pallas_call x1, Pallas kernels, shards(): pl.pallas_call(loss_kernel, out_shape=struct(3, height, width), scratch_s...  8.77 us
    pallas_call x1, Pallas kernels, shards(): pl.pallas_call(home_kernel, out_shape=struct(9, owned), scratch_shapes=[p...  3.52 us
    unnamed x14, local copies, waits for them, and re-layouts  2 us

profile of v7, /device:TPU:1, one launch (start us, length us, event | category | flops | bytes accessed | tf_op | source)
XLA Modules:
  0.0 85.8 jit_solution(13528246011013883079)
XLA Ops:
  0.6 0.9 %reshape.10 = s32[24,8,64]{2,1,0:T(8,128)S(1)} reshape(s32[24,512]{1,0:T(8,128)} %param.8) | data formatting | bytes 98304 | tf_op jit(solution)/shard_map/reshape | solution.py:770
  1.5 0.2 copy.11
  1.7 0.1 copy.12.lists
  1.8 18.7 %owner_send.1 = (f32[128,8,128]{2,1,0:T(8,128)}, f32[3,3,16,384]{3,2,1,0:T(8,128)}) custom-call(s32[1,8192]{1,0:T(1,128)} %send.1, f32[2,2048]{1,0:T(2,128)} %centres.1, f32[2,2048]{1,0:T(2,128)} %conic.1, f32[1,2048]{1,0:T(1,128)} %rho.1, f32[1,2048]{1,0:T(1,128)} %opacity.1, f32[3,2048]{1,0:T(4,128)} %refs_5_.1, f32[3,16,384]{2,1,0:T(8,128)} %refs_6_.1), custom_call_target="tpu_custom_call" | custom-call | tf_op jit(solution)/shard_map/owner_send/pallas_call | solution.py:191
  20.4 0.0 copy-start
  20.5 1.0 %copy-done = f32[128,8,128]{2,1,0:T(8,128)S(1)} copy-done((f32[128,8,128]{2,1,0:T(8,128)S(1)}, f32[128,8,128]{2,1,0:T(8,128)}, u32[]{:S(2)}) %copy-start) | copy-done | bytes 524312
  21.5 19.3 %tile_forward.1 = (f32[3,16,384]{2,1,0:T(8,128)}, f32[3,16,384]{2,1,0:T(8,128)S(1)}, f32[32,384]{1,0:T(8,128)S(1)}, f32[32,384]{1,0:T(8,128)S(1)}, f32[24,3,2,8,...) custom-call(s32[24,1,512]{2,1,0:T(1,128)S(1)} %copy.12.lists, ...), custom_call_target="tpu_custom_call" | custom-call | tf_op jit(solution)/shard_map/tile_forward/pallas_call | solution.py:776
  40.8 0.0 copy-start.1
  40.8 0.9 %copy-done.1 = f32[3,3,16,384]{3,2,1,0:T(8,128)S(1)} copy-done((f32[3,3,16,384]{3,2,1,0:T(8,128)S(1)}, f32[3,3,16,384]{3,2,1,0:T(8,128)}, u32[]{:S(2)}) %copy-start.1) | copy-done | bytes 221208
  41.7 8.8 %loss_gradient.1.grad = f32[3,16,384]{2,1,0:T(8,128)S(1)} custom-call(f32[3,16,384]{2,1,0:T(8,128)S(1)} %get-tuple-element.14.centre, f32[32,384]{1,0:T(8,128)S(1)} %get-tuple-element.15.head, f32[32,384]{1,0:T(8,128)S(1)} %get-tuple-element.16.tail, f32[3,3,16,384]{3,2,1,0:T(8,128)S(1)} %copy-done.1), custom_call_target="tpu_custom_call" | custom-call | tf_op jit(solution)/shard_map/loss_gradient/pallas_call | solution.py:805
  50.5 0.0 copy-start.2
  50.5 0.0 copy-start.3
  50.5 0.0 copy-start.4
  50.6 0.0 copy-start.5
  50.6 0.0 copy-start.6
  50.6 16.6 %tile_backward.1.x = f32[128,8,128]{2,1,0:T(8,128)S(1)} custom-call(s32[24,1,512]{2,1,0:T(1,128)S(1)} %copy.12.lists, bf16[24,512,32]{2,1,0:T(8,128)(2,1)S(1)} %get-tuple-element.13.left_in, f32[3,16,384]{2,1,0:T(8,128)S(1)} %loss_gradient.1.grad, f32[24,3,2,8,256]{4,3,2,1,0:T(8,128)S(1)} %get-tuple-element.18.chunk_rend, ...), custom_call_target="tpu_custom_call" | custom-call | tf_op jit(solution)/shard_map/tile_backward/pallas_call | solution.py:819
  67.2 15.0 %exchange.1.back = f32[128,8,128]{2,1,0:T(8,128)S(1)} custom-call(f32[128,8,128]{2,1,0:T(8,128)S(1)} %tile_backward.1.x), custom_call_target="tpu_custom_call" | custom-call | tf_op jit(solution)/shard_map/exchange/pallas_call | solution.py:242
  82.3 0.0 copy-done.2
  82.3 0.0 copy-done.3
  82.3 0.0 copy-done.4
  82.3 0.0 copy-done.5
  82.3 0.0 copy-done.6
  82.3 3.5 %owner_scatter.1 = f32[9,2048]{1,0:T(8,128)} custom-call(f32[128,8,128]{2,1,0:T(8,128)S(1)} %exchange.1.back, s32[1,8192]{1,0:T(1,128)S(1)} %copy-done.2, f32[2,2048]{1,0:T(2,128)S(1)} %copy-done.3, f32[2,2048]{1,0:T(2,128)S(1)} %copy-done.4, f32[1,2048]{1,0:T(1,128)S(1)} %copy-done.5, f32[1,2048]{1,0:T(1,128)S(1)} %copy-done.6), custom_call_target="tpu_custom_call" | custom-call | tf_op jit(solution)/shard_map/owner_scatter/pallas_call | solution.py:838
Async XLA Ops:
  20.4 1.0 %copy-start = (f32[128,8,128]{2,1,0:T(8,128)S(1)}, f32[128,8,128]{2,1,0:T(8,128)}, u32[]{:S(2)}) copy-start(f32[128,8,128]{2,1,0:T(8,128)} %get-tuple-element.11.recv) | copy-start | bytes 1572868
  40.8 0.9 %copy-start.1 = (f32[3,3,16,384]{3,2,1,0:T(8,128)S(1)}, f32[3,3,16,384]{3,2,1,0:T(8,128)}, u32[]{:S(2)}) copy-start(f32[3,3,16,384]{3,2,1,0:T(8,128)} %get-tuple-element.17.target) | copy-start | bytes 663556
  50.5 31.7 %copy-start.2 = (s32[1,8192]{1,0:T(1,128)S(1)}, s32[1,8192]{1,0:T(1,128)}, u32[]{:S(2)}) copy-start(s32[1,8192]{1,0:T(1,128)} %send.1) | copy-start | bytes 98308
  50.5 31.7 %copy-start.3 = (f32[2,2048]{1,0:T(2,128)S(1)}, f32[2,2048]{1,0:T(2,128)}, u32[]{:S(2)}) copy-start(f32[2,2048]{1,0:T(2,128)} %centres.1) | copy-start | bytes 49156
  50.5 31.7 %copy-start.4 = (f32[2,2048]{1,0:T(2,128)S(1)}, f32[2,2048]{1,0:T(2,128)}, u32[]{:S(2)}) copy-start(f32[2,2048]{1,0:T(2,128)} %conic.1) | copy-start | bytes 49156
  50.6 31.7 %copy-start.5 = (f32[1,2048]{1,0:T(1,128)S(1)}, f32[1,2048]{1,0:T(1,128)}, u32[]{:S(2)}) copy-start(f32[1,2048]{1,0:T(1,128)} %rho.1) | copy-start | bytes 24580
  50.6 31.7 %copy-start.6 = (f32[1,2048]{1,0:T(1,128)S(1)}, f32[1,2048]{1,0:T(1,128)}, u32[]{:S(2)}) copy-start(f32[1,2048]{1,0:T(1,128)} %opacity.1) | copy-start | bytes 24580

commit v8 on v7

--- a/solution.py
+++ b/solution.py
@@ -62,6 +62,7 @@
 
 MESH = pl.DeviceIdType.MESH
 USED = 5
+GROUP = 8
 RIM = 10
 RIMS = 32
 
@@ -207,47 +208,6 @@
         ),
         name="owner_send",
     )(*sources, strip)
-
-
-def exchange_kernel(x, out, local_sem, send_sem, recv_sem):
-    me = lax.axis_index("dev")
-    n = lax.axis_size("dev")
-    rows = pl.ds(0, USED)
-    barrier = greet_all(n, me)
-    own = pltpu.make_async_copy(x.at[me, rows], out.at[me, rows], local_sem)
-    own.start()
-    pl.semaphore_wait(barrier, n - 1)
-
-    def start(k, carry):
-        peer = lax.rem(me + k, n)
-        pltpu.make_async_remote_copy(
-            src_ref=x.at[peer, rows], dst_ref=out.at[me, rows], send_sem=send_sem, recv_sem=recv_sem,
-            device_id=(peer,), device_id_type=MESH,
-        ).start()
-        return carry
-
-    lax.fori_loop(1, n, start, 0)
-    own.wait()
-    rest = pl.ds(0, n - 1)
-    pltpu.make_async_copy(x.at[rest, rows], x.at[rest, rows], send_sem).wait()
-    pltpu.make_async_copy(out.at[rest, rows], out.at[rest, rows], recv_sem).wait()
-
-
-def comm_params(number):
-    return pltpu.CompilerParams(collective_id=number, has_side_effects=True, vmem_limit_bytes=4 << 20)
-
-
-def exchange(x, number):
-    vmem = pl.BlockSpec(memory_space=pltpu.VMEM)
-    return pl.pallas_call(
-        exchange_kernel,
-        out_shape=jax.ShapeDtypeStruct(x.shape, x.dtype),
-        in_specs=[vmem],
-        out_specs=vmem,
-        scratch_shapes=[pltpu.SemaphoreType.DMA] * 3,
-        compiler_params=comm_params(number),
-        name="exchange",
-    )(x)
 
 
 def block_transpose(x):
@@ -386,9 +346,17 @@
 
 
 def forward_kernel(
-    lists, recv, image, image_too, head, tail, chunk_rend, chunk_start, left_out, pieces, ninth, flat, cols, alphas, rends
+    lists, recv, target, image, grad, chunk_rend, chunk_start, left_out, pieces, ninth, flat, cols, alphas, rends,
+    image_too, head, tail, *loss_refs
 ):
     step = pl.program_id(0)
+    me = lax.axis_index("dev")
+    n = lax.axis_size("dev")
+
+    @pl.when(step == 0)
+    def _():
+        greet_sides(me, n)
+
     row = iota((SUB, LANE), 0)
 
     @pl.when(step == 0)
@@ -439,6 +407,7 @@
                     else:
                         head[at + SUB : at + RIM, span] = block[0:2, :]
                         tail[at + 2 : at + RIM, span] = block
+        loss_gradient(me, n, image_too, head, tail, target, grad, *loss_refs)
 
 
 def taps_of():
@@ -468,32 +437,49 @@
     return total
 
 
-def loss_kernel(
-    centre, head, tail, target, grad, before, after, pads, maps, blurred, send_sem, recv_sem
-):
-    height, width = centre.shape[1:]
-    me = lax.axis_index("dev")
-    n = lax.axis_size("dev")
-    barrier = pltpu.get_barrier_semaphore()
-    for hop in (1, n - 1):
-        pl.semaphore_signal(barrier, inc=1, device_id=(lax.rem(me + hop, n),), device_id_type=MESH)
-    rim = RIM
-    copies = []
-    for part in range(RIMS // SUB):
-        rows = pl.ds(part * SUB, SUB)
-        for k, (hop, source, to) in enumerate(((1, tail, before), (n - 1, head, after))):
-            copies.append(
+def rim_copies(me, n, head, tail, before, after, send_sem, recv_sem):
+    sides = []
+    for k, (hop, source, to) in enumerate(((1, tail, before), (n - 1, head, after))):
+        side = []
+        for part in range(RIMS // SUB):
+            rows = pl.ds(part * SUB, SUB)
+            side.append(
                 pltpu.make_async_remote_copy(
                     src_ref=source.at[rows], dst_ref=to.at[rows],
                     send_sem=send_sem.at[2 * part + k], recv_sem=recv_sem.at[2 * part + k],
                     device_id=(lax.rem(me + hop, n),), device_id_type=MESH,
                 )
             )
+        sides.append(side)
+    return sides
+
+
+def greet_sides(me, n):
+    barrier = pltpu.get_barrier_semaphore()
+    for there, hop in ((me < n - 1, 1), (me > 0, n - 1)):
+        @pl.when(there)
+        def _():
+            pl.semaphore_signal(barrier, inc=1, device_id=(lax.rem(me + hop, n),), device_id_type=MESH)
+
+
+def meet_sides(me, n):
+    sides = 2 - jnp.where(me == 0, 1, 0) - jnp.where(me == n - 1, 1, 0)
+    pl.semaphore_wait(pltpu.get_barrier_semaphore(), sides)
+
+
+def loss_gradient(
+    me, n, centre, head, tail, target, grad, before, after, pads, maps, blurred, send_sem, recv_sem
+):
+    height, width = centre.shape[1:]
+    rim = RIM
+    up, down = rim_copies(me, n, head, tail, before, after, send_sem, recv_sem)
+    meet_sides(me, n)
+    for there, side in ((me < n - 1, up), (me > 0, down)):
+        @pl.when(there)
+        def _():
+            for copy in side:
+                copy.start()
     t_before, t_centre, t_after = target.at[0], target.at[1], target.at[2]
-    pl.semaphore_wait(barrier, 2)
-    for copy in copies:
-        copy.start()
-
     at = iota((2 * height, width), 0) - height // 2 + me * height
     inside = (at >= 0) & (at < n * height)
 
@@ -518,8 +504,13 @@
         blurred[ch, 1] = wide_blur(3)
 
     for ch in range(3):
-        for copy in copies[:4] if ch == 0 else copies[2 * ch + 2 : 2 * ch + 4]:
-            copy.wait_recv()
+        parts = slice(0, 2) if ch == 0 else slice(ch + 1, ch + 2)
+        for there, side in ((me > 0, up[parts]), (me < n - 1, down[parts])):
+            @pl.when(there)
+            def _():
+                for copy in side:
+                    copy.wait_recv()
+
         for rows, keep, r, t in (
             (slice(edge, height), me > 0, before[rim * ch : rim * (ch + 1), :], t_before[ch, edge:height, :]),
             (slice(height, 2 * height), None, centre[ch], t_centre[ch]),
@@ -553,8 +544,11 @@
         g_mr, g_rr, g_rt = (back_blur(k) for k in range(3))
         r, t = centre[ch], t_centre[ch]
         grad[ch] = 1.6 * (r - t) - 0.2 * (g_mr + 2.0 * r * g_rr + t * g_rt)
-    for copy in copies:
-        copy.wait_send()
+    for there, side in ((me < n - 1, up), (me > 0, down)):
+        @pl.when(there)
+        def _():
+            for copy in side:
+                copy.wait_send()
 
 
 NT = (((1,), (1,)), ((), ()))
@@ -657,81 +651,37 @@
         yield
 
 
-def backward_kernel(lists, left_in, grad, chunk_rend, chunk_start, out, cots, halves, grads, slots):
-    step = pl.program_id(0)
-    steps = pl.num_programs(0)
-
-    @pl.when(step == 0)
-    def _():
-        for ch in range(3):
-            for g in range(cots.shape[0] // SUB):
-                for h in range(2):
-                    span = slice(h * LANE, (h + 1) * LANE)
-                    block = block_transpose(grad[ch, h * SUB : (h + 1) * SUB, g * LANE : (g + 1) * LANE])
-                    for t in range(SUB):
-                        cots[g * SUB + t, ch : ch + 1, span] = block[t : t + 1, :]
-
-    for slot in range(2):
-        tile = 2 * step + slot
-        past = jnp.maximum(tile - 1, 0)
-        take_turns(
-            BACK_TURNS,
-            f=find_moments(1 - slot, past, cots, halves, grads),
-            s=shade_tile(slot, tile, left_in, chunk_rend, chunk_start, cots, halves),
-        )
-
-    @pl.when(step == steps - 1)
-    def _():
-        for _ in find_moments(1, 2 * step + 1, cots, halves, grads):
-            pass
-        slots[...] = jnp.zeros_like(slots)
-        blocks = slots.shape[0] // (SUB + 1)
-        group = 2
-
-        def chunk(c, carry):
-            each = [c * group + k for k in range(group)]
-            idx = jnp.concatenate([jnp.maximum(lists[t], 0) for t in each], axis=1)
-            eight = jnp.concatenate([grads[t, 0:8, :] for t in each], axis=1)
-            ninth = jnp.concatenate([grads[t, 8:9, :] for t in each], axis=1)
-            slots[...] = slots[...] + scatter_block(eight, ninth, idx, blocks)
-            return carry
-
-        lax.fori_loop(0, cots.shape[0] // group, chunk, 0)
-        left = iota((SUB, LANE), 1) < 64
-        row = iota((SUB, LANE), 0)
-        for h in range(blocks):
-            for half in range(2):
-                span = slice(half * LANE, (half + 1) * LANE)
-                acc = slots[h * SUB : (h + 1) * SUB, span]
-                extra = jnp.broadcast_to(slots[blocks * SUB + h : blocks * SUB + h + 1, span], (SUB, LANE))
-                owner = 4 * h + 2 * half
-                out[owner], out[owner + 1] = pack_pair(acc, extra, left, row)
-
-
-def home_kernel(back, send, centres, conic, rho, opacity, out, total, rows):
-    lane = iota((SUB, LANE), 1)
-    left = lane < 64
+def gather_home(me, n, back, send, centres, conic, rho, opacity, out, total, rows, own, recv_sem):
+    left = iota((SUB, LANE), 1) < 64
     row = iota((SUB, LANE), 0)
-    pairs = back.shape[0] // 2
-    per = 8
+    pairs = n // 2
+    mine = me // 2
     blocks = centres.shape[1] // 256
+    used = pl.ds(0, USED)
     total[...] = jnp.zeros_like(total)
 
-    def chunk(c, carry):
-        eight, ninth = [], []
-        for k in range(per):
-            i = c * per + k
+    def chunk(g, messages):
+        arrived = back.at[pl.ds(0, messages), used]
+        pltpu.make_async_copy(arrived, arrived, recv_sem.at[g]).wait()
+        eight, ninth, idx = [], [], []
+        for k in range(GROUP):
+            i = lax.rem(mine + pairs - (g * GROUP + k), pairs)
             values, last = unpack_pair(back[2 * i], back[2 * i + 1], left, row)
             eight.append(values)
             ninth.append(last)
-        start = pl.multiple_of(c * per * LANE, per * LANE)
-        idx = send[0:1, pl.ds(start, per * LANE)]
+            idx.append(send[0:1, pl.ds(pl.multiple_of(i * LANE, LANE), LANE)])
         total[...] = total[...] + scatter_block(
-            jnp.concatenate(eight, axis=1), jnp.concatenate(ninth, axis=1), idx, blocks
+            jnp.concatenate(eight, axis=1), jnp.concatenate(ninth, axis=1), jnp.concatenate(idx, axis=1), blocks
         )
+
+    own.wait()
+    chunk(0, 2 * GROUP - 1)
+
+    def later(g, carry):
+        chunk(g, 2 * GROUP)
         return carry
 
-    lax.fori_loop(0, pairs // per, chunk, 0)
+    lax.fori_loop(1, pairs // GROUP, later, 0)
     for h in range(blocks):
         span = slice(h * 256, (h + 1) * 256)
         rows[0:8, span] = total[h * SUB : (h + 1) * SUB, :]
@@ -755,6 +705,99 @@
     out[6:9, :] = rows[6:9, :]
 
 
+def backward_kernel(
+    lists, left_in, grad, chunk_rend, chunk_start, send, centres, conic, rho, opacity, result,
+    cots, halves, grads, slots, out, back, total, rows, local_sem, send_sem, recv_sem
+):
+    me = lax.axis_index("dev")
+    n = lax.axis_size("dev")
+    barrier = pltpu.get_barrier_semaphore()
+    each = (n - 1) // (lists.shape[0] // 2)
+
+    def greet(k):
+        pl.semaphore_signal(barrier, inc=1, device_id=(lax.rem(me + k, n),), device_id_type=MESH)
+
+    step = pl.program_id(0)
+    steps = pl.num_programs(0)
+
+    steps_static = lists.shape[0] // 2
+
+    @pl.when(step == 0)
+    def _():
+        for k in range(each * steps_static + 1, n):
+            greet(k)
+        for ch in range(3):
+            for g in range(cots.shape[0] // SUB):
+                for h in range(2):
+                    span = slice(h * LANE, (h + 1) * LANE)
+                    block = block_transpose(grad[ch, h * SUB : (h + 1) * SUB, g * LANE : (g + 1) * LANE])
+                    for t in range(SUB):
+                        cots[g * SUB + t, ch : ch + 1, span] = block[t : t + 1, :]
+
+    for k in range(each):
+        greet(step * each + k + 1)
+    for slot in range(2):
+        tile = 2 * step + slot
+        past = jnp.maximum(tile - 1, 0)
+        take_turns(
+            BACK_TURNS,
+            f=find_moments(1 - slot, past, cots, halves, grads),
+            s=shade_tile(slot, tile, left_in, chunk_rend, chunk_start, cots, halves),
+        )
+
+    @pl.when(step == steps - 1)
+    def _():
+        for _ in find_moments(1, 2 * step + 1, cots, halves, grads):
+            pass
+        slots[...] = jnp.zeros_like(slots)
+        blocks = slots.shape[0] // (SUB + 1)
+        group = 2
+
+        def chunk(c, carry):
+            each = [c * group + k for k in range(group)]
+            idx = jnp.concatenate([jnp.maximum(lists[t], 0) for t in each], axis=1)
+            eight = jnp.concatenate([grads[t, 0:8, :] for t in each], axis=1)
+            ninth = jnp.concatenate([grads[t, 8:9, :] for t in each], axis=1)
+            slots[...] = slots[...] + scatter_block(eight, ninth, idx, blocks)
+            return carry
+
+        lax.fori_loop(0, cots.shape[0] // group, chunk, 0)
+        left = iota((SUB, LANE), 1) < 64
+        row = iota((SUB, LANE), 0)
+        for h in range(blocks):
+            for half in range(2):
+                span = slice(half * LANE, (half + 1) * LANE)
+                acc = slots[h * SUB : (h + 1) * SUB, span]
+                extra = jnp.broadcast_to(slots[blocks * SUB + h : blocks * SUB + h + 1, span], (SUB, LANE))
+                owner = 4 * h + 2 * half
+                out[owner], out[owner + 1] = pack_pair(acc, extra, left, row)
+        pl.semaphore_wait(barrier, n - 1)
+        used = pl.ds(0, USED)
+        own = pltpu.make_async_copy(out.at[me, used], back.at[me, used], local_sem)
+        own.start()
+        pairs = n // 2
+        mine = me // 2
+
+        def ship_to(peer, k):
+            pltpu.make_async_remote_copy(
+                src_ref=out.at[peer, used], dst_ref=back.at[me, used],
+                send_sem=send_sem, recv_sem=recv_sem.at[k // GROUP],
+                device_id=(peer,), device_id_type=MESH,
+            ).start()
+
+        ship_to(me + 1 - 2 * lax.rem(me, 2), 0)
+
+        def ship(k, carry):
+            for core in range(2):
+                ship_to(2 * lax.rem(mine + k, pairs) + core, k)
+            return carry
+
+        lax.fori_loop(1, pairs, ship, 0)
+        gather_home(me, n, back, send, centres, conic, rho, opacity, result, total, rows, own, recv_sem)
+        sent = out.at[pl.ds(0, n - 1), used]
+        pltpu.make_async_copy(sent, sent, send_sem).wait()
+
+
 def struct(*shape, dtype=F32):
     return jax.ShapeDtypeStruct(shape, dtype)
 
@@ -773,19 +816,17 @@
     per = 2
     per_tile = lambda *shape: pl.BlockSpec((per,) + shape, lambda t: (t,) + (0,) * len(shape))
     hi_blocks = devices * 64 // 256
-    image, image_too, head, tail, chunk_rend, chunk_start, left = pl.pallas_call(
+    image, pixel_grad, chunk_rend, chunk_start, left = pl.pallas_call(
         forward_kernel,
         grid=(tiles // per,),
-        in_specs=[whole(tiles, 1, count), whole(devices, SUB, LANE)],
+        in_specs=[whole(tiles, 1, count), whole(devices, SUB, LANE), whole(3, 3, height, width)],
         out_specs=[
-            whole(3, height, width), whole(3, height, width), whole(RIMS, width), whole(RIMS, width),
+            whole(3, height, width), whole(3, height, width),
             per_tile(3, 2, SUB, pixels), per_tile(2, SUB, pixels), per_tile(count, 32),
         ],
         out_shape=[
             struct(3, height, width),
             struct(3, height, width),
-            struct(RIMS, width),
-            struct(RIMS, width),
             struct(tiles, 3, 2, SUB, pixels),
             struct(tiles, 2, SUB, pixels),
             struct(tiles, count, 32, dtype=BF16),
@@ -797,54 +838,45 @@
             pltpu.VMEM((per, count, LANE), F32),
             pltpu.VMEM((per, count, pixels), F32),
             pltpu.VMEM((3, tiles, pixels), F32),
-        ],
-        compiler_params=params(16),
-        name="tile_forward",
-    )(lists, incoming)
-
-    pixel_grad = pl.pallas_call(
-        loss_kernel,
-        out_shape=struct(3, height, width),
-        scratch_shapes=[pltpu.VMEM((RIMS, width), F32)] * 2
+            pltpu.VMEM((3, height, width), F32),
+        ]
+        + [pltpu.VMEM((RIMS, width), F32)] * 4
         + [
             pltpu.VMEM((5, 3 * height, width), F32),
             pltpu.VMEM((3, 2 * height, width), F32),
             pltpu.VMEM((3, 2, 2 * height, width), F32),
         ]
         + [pltpu.SemaphoreType.DMA((8,))] * 2,
-        compiler_params=pltpu.CompilerParams(collective_id=1, has_side_effects=True, vmem_limit_bytes=8 << 20),
-        name="loss_gradient",
-    )(image_too, head, tail, t_strips)
-
-    slot_grads = pl.pallas_call(
+        compiler_params=pltpu.CompilerParams(collective_id=1, has_side_effects=True, vmem_limit_bytes=20 << 20),
+        name="tile_forward",
+    )(lists, incoming, t_strips)
+
+    grads = pl.pallas_call(
         backward_kernel,
         grid=(tiles // per,),
         in_specs=[
             whole(tiles, 1, count), per_tile(count, 32), whole(3, height, width),
             per_tile(3, 2, SUB, pixels), per_tile(2, SUB, pixels),
-        ],
-        out_specs=whole(devices, SUB, LANE),
-        out_shape=struct(devices, SUB, LANE),
+        ]
+        + [whole(*v.shape) for v in sources[:5]],
+        out_specs=whole(9, owned),
+        out_shape=struct(9, owned),
         scratch_shapes=[
             pltpu.VMEM((tiles, 3, pixels), F32),
             pltpu.VMEM((per, count, 3 * pixels), BF16),
             pltpu.VMEM((tiles, 16, count), F32),
             pltpu.VMEM((hi_blocks * (SUB + 1), 256), F32),
-        ],
-        compiler_params=params(20),
-        name="tile_backward",
-    )(lists, left, pixel_grad, chunk_rend, chunk_start)
-    returned = exchange(slot_grads, 2)
-    grads = pl.pallas_call(
-        home_kernel,
-        out_shape=struct(9, owned),
-        scratch_shapes=[
+            pltpu.VMEM((devices, SUB, LANE), F32),
+            pltpu.VMEM((devices, SUB, LANE), F32),
             pltpu.VMEM((owned // 256 * (SUB + 1), 256), F32),
             pltpu.VMEM((16, owned), F32),
+            pltpu.SemaphoreType.DMA,
+            pltpu.SemaphoreType.DMA,
+            pltpu.SemaphoreType.DMA((devices // 2 // GROUP,)),
         ],
-        compiler_params=params(16),
-        name="owner_scatter",
-    )(returned, send_rows, centres, conic, rho, opacity)
+        compiler_params=pltpu.CompilerParams(collective_id=2, has_side_effects=True, vmem_limit_bytes=24 << 20),
+        name="tile_backward",
+    )(lists, left, pixel_grad, chunk_rend, chunk_start, *sources[:5])
     return image, grads
 
 

time: 86.1 us -> 80.3 us (0.933)
  Pallas kernels: 81.9 us -> 71.1 us
  local copies, waits for them, and re-layouts: 3.15 us -> 7.99 us
    pallas_call x3 -> x0, Pallas kernels: 27.3 us -> none  [the longest x1 15 us: exchange(): pl.pallas_call(exchange_kernel, out_shape=jax.ShapeDtypeStruct(x.shape, x...]
    pallas_call x1, Pallas kernels: 16.6 us -> 28.8 us  [shards(): pl.pallas_call(backward_kernel, grid=(tiles // per,), in_specs=[whole(til...]
    unnamed x14 -> x16, local copies, waits for them, and re-layouts: 2 us -> 6.84 us
    pallas_call x1, Pallas kernels: 19.3 us -> 23.7 us  [shards(): pl.pallas_call(forward_kernel, grid=(tiles // per,), in_specs=[whole(tile...]
where the time goes in v8:
time: 80.3 us; the launch traced here: 79.8 us
  Pallas kernels  71.1 us (89%)
  local copies, waits for them, and re-layouts  7.99 us (10%)
    pallas_call x1, Pallas kernels, shards(): pl.pallas_call(backward_kernel, grid=(tiles // per,), in_specs=[whole(til...  28.8 us
    pallas_call x1, Pallas kernels, shards(): pl.pallas_call(forward_kernel, grid=(tiles // per,), in_specs=[whole(tile...  23.7 us
    pallas_call x1, Pallas kernels, send_owned(): pl.pallas_call(send_owned_kernel, out_shape=[struct(devices, SUB, LANE),...  18.7 us
    unnamed x16, local copies, waits for them, and re-layouts  6.84 us

profile of v8, /device:TPU:1, one launch (start us, length us, event | category | flops | bytes accessed | tf_op | source)
XLA Modules:
  0.0 79.8 jit_solution(14920864573776684249)
XLA Ops:
  0.6 0.9 %reshape.10 = s32[24,8,64]{2,1,0:T(8,128)S(1)} reshape(s32[24,512]{1,0:T(8,128)} %param.8) | data formatting | bytes 98304 | tf_op jit(solution)/shard_map/reshape | solution.py:813
  1.5 0.2 copy.11
  1.7 0.1 copy.12.lists
  1.8 18.7 %owner_send.1 = (f32[128,8,128]{2,1,0:T(8,128)}, f32[3,3,16,384]{3,2,1,0:T(8,128)}) custom-call(s32[1,8192]{1,0:T(1,128)} %send.1, f32[2,2048]{1,0:T(2,128)} %centres.1, f32[2,2048]{1,0:T(2,128)} %conic.1, f32[1,2048]{1,0:T(1,128)} %rho.1, f32[1,2048]{1,0:T(1,128)} %opacity.1, f32[3,2048]{1,0:T(4,128)} %refs_5_.1, f32[3,16,384]{2,1,0:T(8,128)} %refs_6_.1), custom_call_target="tpu_custom_call" | custom-call | tf_op jit(solution)/shard_map/owner_send/pallas_call | solution.py:192
  20.4 0.0 copy-start
  20.5 1.0 %copy-done = f32[128,8,128]{2,1,0:T(8,128)S(1)} copy-done((f32[128,8,128]{2,1,0:T(8,128)S(1)}, f32[128,8,128]{2,1,0:T(8,128)}, u32[]{:S(2)}) %copy-start) | copy-done | bytes 524312
  21.5 0.0 copy-start.1
  21.5 0.9 %copy-done.1 = f32[3,3,16,384]{3,2,1,0:T(8,128)S(1)} copy-done((f32[3,3,16,384]{3,2,1,0:T(8,128)S(1)}, f32[3,3,16,384]{3,2,1,0:T(8,128)}, u32[]{:S(2)}) %copy-start.1) | copy-done | bytes 221208
  22.4 23.7 %tile_forward.1 = (f32[3,16,384]{2,1,0:T(8,128)S(1)}, f32[3,16,384]{2,1,0:T(8,128)S(1)}, f32[24,3,2,8,256]{4,3,2,1,0:T(8,128)S(1)}, f32[24,2,8,256]{3,2,1,0:T(8,128)S(1)}, bf16[24,512,32]{2,1,0:T(8,128)(2,1)S(1)}) custom-call(s32[24,1,512]{2,1,0:T(1,128)S(1)} %copy.12.lists, f32[128,8,128]{2,1,0:T(8,128)S(1)} %copy-done, f32[3,3,16,384]{3,2,1,0:T(8,128)S(1)} %copy-done.1), custom_call_target="tpu_custom_call" | custom-call | tf_op jit(solution)/shard_map/tile_forward/pallas_call | solution.py:819
  46.1 0.0 copy-start.2
  46.1 0.7 copy-done.2
  46.9 0.0 copy-start.3
  46.9 0.7 copy-done.3
  47.6 0.0 copy-start.4
  47.6 0.7 copy-done.4
  48.3 0.0 copy-start.5
  48.3 0.7 copy-done.5
  49.0 0.0 copy-start.6
  49.0 0.7 copy-done.6
  49.7 28.8 %tile_backward.1 = f32[9,2048]{1,0:T(8,128)S(1)} custom-call(s32[24,1,512]{2,1,0:T(1,128)S(1)} %copy.12.lists, bf16[24,512,32]{2,1,0:T(8,128)(2,1)S(1)} %get-tuple-element.12.left_in, f32[3,16,384]{2,1,0:T(8,128)S(1)} %get-tuple-element.13.grad, f32[24,3,2,8,256]{4,3,2,1,0:T(8,128)S(1)} %get-tuple-element.14.chunk_rend, ...), custom_call_target="tpu_custom_call" | custom-call | tf_op jit(solution)/shard_map/tile_backward/pallas_call | solution.py:854
  78.5 0.6 copy.16
  79.1 0.7 copy.17
Async XLA Ops:
  20.4 1.0 %copy-start = (f32[128,8,128]{2,1,0:T(8,128)S(1)}, f32[128,8,128]{2,1,0:T(8,128)}, u32[]{:S(2)}) copy-start(f32[128,8,128]{2,1,0:T(8,128)} %get-tuple-element.9.recv) | copy-start | bytes 1572868
  21.5 0.9 %copy-start.1 = (f32[3,3,16,384]{3,2,1,0:T(8,128)S(1)}, f32[3,3,16,384]{3,2,1,0:T(8,128)}, u32[]{:S(2)}) copy-start(f32[3,3,16,384]{3,2,1,0:T(8,128)} %get-tuple-element.10.target) | copy-start | bytes 663556
  46.1 0.8 copy-start.2
  46.9 0.7 copy-start.3
  47.6 0.7 copy-start.4
  48.3 0.7 copy-start.5
  49.0 0.7 copy-start.6

commit v9 on v8

--- a/solution.py
+++ b/solution.py
@@ -102,8 +102,8 @@
 
 
 def send_owned_kernel(*refs):
-    sources, strip, (out, strips), x, table, ninth = refs[:6], refs[6], refs[7:9], *refs[9:12]
-    places, (local_sem, send_sem, recv_sem, halo_send, halo_recv) = refs[12:18], refs[18:23]
+    sources, strip, (out, strips, lists), x, table, ninth = refs[:7], refs[7], refs[8:11], *refs[11:14]
+    places, sorted_lists, (local_sem, send_sem, recv_sem, halo_send, halo_recv) = refs[14:21], refs[21], refs[22:27]
     me = lax.axis_index("dev")
     n = lax.axis_size("dev")
     fetched = [pltpu.make_async_copy(a, b, local_sem.at[k]) for k, (a, b) in enumerate(zip(sources, places))]
@@ -112,7 +112,7 @@
     barrier = greet_all(n, me)
     for copy in fetched:
         copy.wait()
-    send, centres, conic, rho, opacity, colors = places
+    send, centres, conic, rho, opacity, colors, raw_lists = places
     rows = coefficient_rows(
         centres[0:1, :], centres[1:2, :], conic[0:1, :], conic[1:2, :], rho[...], opacity[...]
     )
@@ -157,7 +157,7 @@
     for copy in copies:
         copy.start()
     partner = me + 1 - 2 * lax.rem(me, 2)
-    own = pltpu.make_async_copy(x.at[me, used], out.at[me, used], local_sem.at[6])
+    own = pltpu.make_async_copy(x.at[me, used], out.at[me, used], local_sem.at[7])
     own.start()
     pltpu.make_async_remote_copy(
         src_ref=x.at[partner, used], dst_ref=out.at[me, used], send_sem=send_sem, recv_sem=recv_sem,
@@ -178,12 +178,28 @@
 
     lax.fori_loop(early, pairs // step, both, 0)
     lax.fori_loop(pairs - step, pairs, ship_one, 0)
+    lane = iota((SUB, LANE), 1)
+    place = lax.bitwise_and(lane, 7)
+    count = raw_lists.shape[1]
+    for q in range(count // LANE):
+        source = lax.bitwise_and(place, 1) * 64 + (LANE // SUB) * q + lax.shift_right_logical(lane, 3)
+        half = lax.shift_right_logical(place, 1)
+        for g in range(raw_lists.shape[0] // SUB):
+            mixed = jnp.zeros((SUB, LANE), jnp.int32)
+            for b in range(count // LANE):
+                block = raw_lists[g * SUB : (g + 1) * SUB, b * LANE : (b + 1) * LANE]
+                mixed = jnp.where(half == b, lane_pick(block, source), mixed)
+            for t in range(SUB):
+                sorted_lists[g * SUB + t, :, q * LANE : (q + 1) * LANE] = mixed[t : t + 1, :]
     own.wait()
     rest = pl.ds(0, n - 1)
     pltpu.make_async_copy(x.at[rest, used], x.at[rest, used], send_sem).wait()
     pltpu.make_async_copy(out.at[rest, used], out.at[rest, used], recv_sem).wait()
+    keep = pltpu.make_async_copy(sorted_lists, lists, local_sem.at[8])
+    keep.start()
     for copy in copies:
         copy.wait()
+    keep.wait()
 
 
 def send_owned(sources, strip, number):
@@ -191,16 +207,21 @@
     vmem, hbm = pl.BlockSpec(memory_space=pltpu.VMEM), pl.BlockSpec(memory_space=pltpu.HBM)
     return pl.pallas_call(
         send_owned_kernel,
-        out_shape=[struct(devices, SUB, LANE), struct(3, *strip.shape)],
-        in_specs=[hbm] * 7,
-        out_specs=[hbm] * 2,
+        out_shape=[
+            struct(devices, SUB, LANE),
+            struct(3, *strip.shape),
+            struct(sources[6].shape[0], 1, sources[6].shape[1], dtype=jnp.int32),
+        ],
+        in_specs=[hbm] * 8,
+        out_specs=[hbm] * 3,
         scratch_shapes=[
             pltpu.VMEM((devices, SUB, LANE), F32),
             pltpu.VMEM((SUB, owned), F32),
             pltpu.VMEM((owned // LANE, LANE), F32),
         ]
         + [pltpu.VMEM(v.shape, v.dtype) for v in sources]
-        + [pltpu.SemaphoreType.DMA((7,))]
+        + [pltpu.VMEM((sources[6].shape[0], 1, sources[6].shape[1]), jnp.int32)]
+        + [pltpu.SemaphoreType.DMA((9,))]
         + [pltpu.SemaphoreType.DMA] * 2
         + [pltpu.SemaphoreType.DMA((3,))] * 2,
         compiler_params=pltpu.CompilerParams(
@@ -810,8 +831,7 @@
     pixels = height * height
     params = lambda mib: pltpu.CompilerParams(vmem_limit_bytes=mib << 20)
     sources = (send_rows, centres, conic, rho, opacity, colors)
-    lists = tile_lists.reshape(tiles, SUB, count // SUB).transpose(0, 2, 1).reshape(tiles, 1, count)
-    incoming, t_strips = send_owned(sources, target, 0)
+    incoming, t_strips, lists = send_owned(sources + (tile_lists,), target, 0)
     whole = lambda *shape: pl.BlockSpec(shape, lambda t: (0,) * len(shape))
     per = 2
     per_tile = lambda *shape: pl.BlockSpec((per,) + shape, lambda t: (t,) + (0,) * len(shape))
@@ -847,7 +867,7 @@
             pltpu.VMEM((3, 2, 2 * height, width), F32),
         ]
         + [pltpu.SemaphoreType.DMA((8,))] * 2,
-        compiler_params=pltpu.CompilerParams(collective_id=1, has_side_effects=True, vmem_limit_bytes=20 << 20),
+        compiler_params=pltpu.CompilerParams(collective_id=1, has_side_effects=True, vmem_limit_bytes=60 * 1024 * 1024),
         name="tile_forward",
     )(lists, incoming, t_strips)
 
@@ -874,7 +894,7 @@
             pltpu.SemaphoreType.DMA,
             pltpu.SemaphoreType.DMA((devices // 2 // GROUP,)),
         ],
-        compiler_params=pltpu.CompilerParams(collective_id=2, has_side_effects=True, vmem_limit_bytes=24 << 20),
+        compiler_params=pltpu.CompilerParams(collective_id=2, has_side_effects=True, vmem_limit_bytes=60 * 1024 * 1024),
         name="tile_backward",
     )(lists, left, pixel_grad, chunk_rend, chunk_start, *sources[:5])
     return image, grads

time: 80.3 us -> 79.5 us (0.990)
  local copies, waits for them, and re-layouts: 7.99 us -> 2.21 us
  Pallas kernels: 71.1 us -> 76.3 us
    unnamed x16 -> x4, local copies, waits for them, and re-layouts: 6.84 us -> 2.21 us
    pallas_call x1, Pallas kernels: 23.7 us -> 26.1 us  [shards(): pl.pallas_call(forward_kernel, grid=(tiles // per,), in_specs=[whole(tile...]
    pallas_call x1, Pallas kernels: 28.8 us -> 30.9 us  [shards(): pl.pallas_call(backward_kernel, grid=(tiles // per,), in_specs=[whole(til...]
    reshape x3 -> x0, local copies, waits for them, and re-layouts: 1.15 us -> none  [shards(): tile_lists.reshape(tiles, SUB, count // SUB).transpose(0, 2, 1)]
where the time goes in v9:
time: 79.5 us; the launch traced here: 79.2 us
  Pallas kernels  76.3 us (96%)
  local copies, waits for them, and re-layouts  2.21 us (3%)
    pallas_call x1, Pallas kernels, shards(): pl.pallas_call(backward_kernel, grid=(tiles // per,), in_specs=[whole(til...  30.9 us
    pallas_call x1, Pallas kernels, shards(): pl.pallas_call(forward_kernel, grid=(tiles // per,), in_specs=[whole(tile...  26.1 us
    pallas_call x1, Pallas kernels, send_owned(): pl.pallas_call(send_owned_kernel, out_shape=[struct(devices, SUB, LANE),...  19.3 us
    unnamed x4, local copies, waits for them, and re-layouts  2.21 us

profile of v9, /device:TPU:1, one launch (start us, length us, event | category | flops | bytes accessed | tf_op | source)
XLA Modules:
  0.0 79.2 jit_solution(7954202470425936076)
XLA Ops:
  0.6 19.3 %owner_send.1 = (f32[128,8,128]{2,1,0:T(8,128)}, f32[3,3,16,384]{3,2,1,0:T(8,128)}, s32[24,1,512]{2,1,0:T(1,128)}) custom-call(s32[1,8192]{1,0:T(1,128)} %send.1, f32[2,2048]{1,0:T(2,128)} %centres.1, f32[2,2048]{1,0:T(2,128)} %conic.1, f32[1,2048]{1,0:T(1,128)} %rho.1, f32[1,2048]{1,0:T(1,128)} %opacity.1, f32[3,2048]{1,0:T(4,128)} %refs_5_.1, ...), custom_call_target="tpu_custom_call" | custom-call | tf_op jit(solution)/shard_map/owner_send/pallas_call | solution.py:208
  19.9 26.1 %tile_forward.1 = (f32[3,16,384]{2,1,0:T(8,128)}, f32[3,16,384]{2,1,0:T(8,128)}, f32[24,3,2,8,256]{4,3,2,1,0:T(8,128)}, f32[24,2,8,256]{3,2,1,0:T(8,128)}, bf16[24,512,32]{2,1,0:T(8,128)(2,1)}) custom-call(s32[24,1,512]{2,1,0:T(1,128)} %get-tuple-element.10.lists, f32[128,8,128]{2,1,0:T(8,128)} %get-tuple-element.11.recv, ...), custom_call_target="tpu_custom_call" | custom-call | tf_op jit(solution)/shard_map/tile_forward/pallas_call | solution.py:839
  46.0 0.0 copy-start
  46.0 30.9 %tile_backward.1 = f32[9,2048]{1,0:T(8,128)} custom-call(s32[24,1,512]{2,1,0:T(1,128)} %get-tuple-element.10.lists, bf16[24,512,32]{2,1,0:T(8,128)(2,1)} %get-tuple-element.14.left_in, f32[3,16,384]{2,1,0:T(8,128)} %get-tuple-element.15.grad, f32[24,3,2,8,256]{4,3,2,1,0:T(8,128)} %get-tuple-element.16.chunk_rend, ...), custom_call_target="tpu_custom_call" | custom-call | tf_op jit(solution)/shard_map/tile_backward/pallas_call | solution.py:874
  77.0 0.0 copy-done
  77.0 0.6 copy.12
  77.6 1.6 %copy.13 = f32[9,2048]{1,0:T(8,128)} copy(f32[9,2048]{1,0:T(8,128)} %tile_backward.1) | data formatting | bytes 147456
Async XLA Ops:
  46.0 30.9 %copy-start = (f32[3,16,384]{2,1,0:T(8,128)S(1)}, f32[3,16,384]{2,1,0:T(8,128)}, u32[]{:S(2)}) copy-start(f32[3,16,384]{2,1,0:T(8,128)} %get-tuple-element.20) | copy-start | bytes 221188

commit v10 on v9

--- a/solution.py
+++ b/solution.py
@@ -101,11 +101,10 @@
     ]
 
 
-def send_owned_kernel(*refs):
-    sources, strip, (out, strips, lists), x, table, ninth = refs[:7], refs[7], refs[8:11], *refs[11:14]
-    places, sorted_lists, (local_sem, send_sem, recv_sem, halo_send, halo_recv) = refs[14:21], refs[21], refs[22:27]
-    me = lax.axis_index("dev")
-    n = lax.axis_size("dev")
+def send_owned(
+    me, n, sources, strip, out, strips, x, table, ninth, places, sorted_lists,
+    local_sem, send_sem, recv_sem, halo_send, halo_recv
+):
     fetched = [pltpu.make_async_copy(a, b, local_sem.at[k]) for k, (a, b) in enumerate(zip(sources, places))]
     for copy in fetched:
         copy.start()
@@ -195,40 +194,8 @@
     rest = pl.ds(0, n - 1)
     pltpu.make_async_copy(x.at[rest, used], x.at[rest, used], send_sem).wait()
     pltpu.make_async_copy(out.at[rest, used], out.at[rest, used], recv_sem).wait()
-    keep = pltpu.make_async_copy(sorted_lists, lists, local_sem.at[8])
-    keep.start()
     for copy in copies:
         copy.wait()
-    keep.wait()
-
-
-def send_owned(sources, strip, number):
-    devices, owned = lax.axis_size("dev"), sources[1].shape[1]
-    vmem, hbm = pl.BlockSpec(memory_space=pltpu.VMEM), pl.BlockSpec(memory_space=pltpu.HBM)
-    return pl.pallas_call(
-        send_owned_kernel,
-        out_shape=[
-            struct(devices, SUB, LANE),
-            struct(3, *strip.shape),
-            struct(sources[6].shape[0], 1, sources[6].shape[1], dtype=jnp.int32),
-        ],
-        in_specs=[hbm] * 8,
-        out_specs=[hbm] * 3,
-        scratch_shapes=[
-            pltpu.VMEM((devices, SUB, LANE), F32),
-            pltpu.VMEM((SUB, owned), F32),
-            pltpu.VMEM((owned // LANE, LANE), F32),
-        ]
-        + [pltpu.VMEM(v.shape, v.dtype) for v in sources]
-        + [pltpu.VMEM((sources[6].shape[0], 1, sources[6].shape[1]), jnp.int32)]
-        + [pltpu.SemaphoreType.DMA((9,))]
-        + [pltpu.SemaphoreType.DMA] * 2
-        + [pltpu.SemaphoreType.DMA((3,))] * 2,
-        compiler_params=pltpu.CompilerParams(
-            collective_id=number, has_side_effects=True, vmem_limit_bytes=60 * 1024 * 1024
-        ),
-        name="owner_send",
-    )(*sources, strip)
 
 
 def block_transpose(x):
@@ -366,17 +333,19 @@
         rends[ch, pl.ds(tile, 1), :] = sub_sum(sums[0][ch] + sums[1][ch])[0:1, :]
 
 
-def forward_kernel(
-    lists, recv, target, image, grad, chunk_rend, chunk_start, left_out, pieces, ninth, flat, cols, alphas, rends,
-    image_too, head, tail, *loss_refs
-):
+def forward_kernel(*refs):
+    sources, target, image, grad, chunk_rend, chunk_start, left_out, lists_out = refs[:7], *refs[7:14]
+    pieces, ninth, flat, cols, alphas, rends, image_too, head, tail, *loss_refs = refs[14:30]
+    recv, lists, strips, *send_refs = refs[30:]
     step = pl.program_id(0)
     me = lax.axis_index("dev")
     n = lax.axis_size("dev")
 
     @pl.when(step == 0)
     def _():
-        greet_sides(me, n)
+        x, table, own_ninth, *more = send_refs
+        send_owned(me, n, sources, target, recv, strips, x, table, own_ninth, more[:7], lists, *more[7:])
+        lists_out[...] = lists[...]
 
     row = iota((SUB, LANE), 0)
 
@@ -428,7 +397,7 @@
                     else:
                         head[at + SUB : at + RIM, span] = block[0:2, :]
                         tail[at + 2 : at + RIM, span] = block
-        loss_gradient(me, n, image_too, head, tail, target, grad, *loss_refs)
+        loss_gradient(me, n, image_too, head, tail, strips, grad, *loss_refs)
 
 
 def taps_of():
@@ -475,26 +444,12 @@
     return sides
 
 
-def greet_sides(me, n):
-    barrier = pltpu.get_barrier_semaphore()
-    for there, hop in ((me < n - 1, 1), (me > 0, n - 1)):
-        @pl.when(there)
-        def _():
-            pl.semaphore_signal(barrier, inc=1, device_id=(lax.rem(me + hop, n),), device_id_type=MESH)
-
-
-def meet_sides(me, n):
-    sides = 2 - jnp.where(me == 0, 1, 0) - jnp.where(me == n - 1, 1, 0)
-    pl.semaphore_wait(pltpu.get_barrier_semaphore(), sides)
-
-
 def loss_gradient(
     me, n, centre, head, tail, target, grad, before, after, pads, maps, blurred, send_sem, recv_sem
 ):
     height, width = centre.shape[1:]
     rim = RIM
     up, down = rim_copies(me, n, head, tail, before, after, send_sem, recv_sem)
-    meet_sides(me, n)
     for there, side in ((me < n - 1, up), (me > 0, down)):
         @pl.when(there)
         def _():
@@ -830,19 +785,18 @@
     height, width = target.shape[1], target.shape[2]
     pixels = height * height
     params = lambda mib: pltpu.CompilerParams(vmem_limit_bytes=mib << 20)
-    sources = (send_rows, centres, conic, rho, opacity, colors)
-    incoming, t_strips, lists = send_owned(sources + (tile_lists,), target, 0)
+    sources = (send_rows, centres, conic, rho, opacity, colors, tile_lists)
     whole = lambda *shape: pl.BlockSpec(shape, lambda t: (0,) * len(shape))
     per = 2
     per_tile = lambda *shape: pl.BlockSpec((per,) + shape, lambda t: (t,) + (0,) * len(shape))
     hi_blocks = devices * 64 // 256
-    image, pixel_grad, chunk_rend, chunk_start, left = pl.pallas_call(
+    image, pixel_grad, chunk_rend, chunk_start, left, lists = pl.pallas_call(
         forward_kernel,
         grid=(tiles // per,),
-        in_specs=[whole(tiles, 1, count), whole(devices, SUB, LANE), whole(3, 3, height, width)],
+        in_specs=[pl.BlockSpec(memory_space=pltpu.HBM)] * 8,
         out_specs=[
             whole(3, height, width), whole(3, height, width),
-            per_tile(3, 2, SUB, pixels), per_tile(2, SUB, pixels), per_tile(count, 32),
+            per_tile(3, 2, SUB, pixels), per_tile(2, SUB, pixels), per_tile(count, 32), whole(tiles, 1, count),
         ],
         out_shape=[
             struct(3, height, width),
@@ -850,6 +804,7 @@
             struct(tiles, 3, 2, SUB, pixels),
             struct(tiles, 2, SUB, pixels),
             struct(tiles, count, 32, dtype=BF16),
+            struct(tiles, 1, count, dtype=jnp.int32),
         ],
         scratch_shapes=[
             pltpu.VMEM((hi_blocks * SUB, 256), F32),
@@ -866,10 +821,22 @@
             pltpu.VMEM((3, 2 * height, width), F32),
             pltpu.VMEM((3, 2, 2 * height, width), F32),
         ]
-        + [pltpu.SemaphoreType.DMA((8,))] * 2,
-        compiler_params=pltpu.CompilerParams(collective_id=1, has_side_effects=True, vmem_limit_bytes=60 * 1024 * 1024),
+        + [pltpu.SemaphoreType.DMA((8,))] * 2
+        + [
+            pltpu.VMEM((devices, SUB, LANE), F32),
+            pltpu.VMEM((tiles, 1, count), jnp.int32),
+            pltpu.VMEM((3, 3, height, width), F32),
+            pltpu.VMEM((devices, SUB, LANE), F32),
+            pltpu.VMEM((SUB, owned), F32),
+            pltpu.VMEM((owned // LANE, LANE), F32),
+        ]
+        + [pltpu.VMEM(v.shape, v.dtype) for v in sources]
+        + [pltpu.SemaphoreType.DMA((8,))]
+        + [pltpu.SemaphoreType.DMA] * 2
+        + [pltpu.SemaphoreType.DMA((3,))] * 2,
+        compiler_params=pltpu.CompilerParams(collective_id=0, has_side_effects=True, vmem_limit_bytes=60 * 1024 * 1024),
         name="tile_forward",
-    )(lists, incoming, t_strips)
+    )(*sources, target)
 
     grads = pl.pallas_call(
         backward_kernel,
@@ -894,7 +861,7 @@
             pltpu.SemaphoreType.DMA,
             pltpu.SemaphoreType.DMA((devices // 2 // GROUP,)),
         ],
-        compiler_params=pltpu.CompilerParams(collective_id=2, has_side_effects=True, vmem_limit_bytes=60 * 1024 * 1024),
+        compiler_params=pltpu.CompilerParams(collective_id=1, has_side_effects=True, vmem_limit_bytes=60 * 1024 * 1024),
         name="tile_backward",
     )(lists, left, pixel_grad, chunk_rend, chunk_start, *sources[:5])
     return image, grads

time: 79.5 us -> 77.8 us (0.979)
  Pallas kernels: 76.3 us -> 74.6 us
    pallas_call x2 -> x1, Pallas kernels: 45.4 us -> 43.6 us  [shards(): pl.pallas_call(forward_kernel, grid=(tiles // per,), in_specs=[pl.BlockSp...]
where the time goes in v10:
time: 77.8 us; the launch traced here: 77.4 us
  Pallas kernels  74.6 us (96%)
  local copies, waits for them, and re-layouts  2.21 us (3%)
    pallas_call x1, Pallas kernels, shards(): pl.pallas_call(forward_kernel, grid=(tiles // per,), in_specs=[pl.BlockSp...  43.6 us
    pallas_call x1, Pallas kernels, shards(): pl.pallas_call(backward_kernel, grid=(tiles // per,), in_specs=[whole(til...  30.9 us
    unnamed x4, local copies, waits for them, and re-layouts  2.21 us

profile of v10, /device:TPU:1, one launch (start us, length us, event | category | flops | bytes accessed | tf_op | source)
XLA Modules:
  0.0 77.4 jit_solution(3502518688630041116)
XLA Ops:
  0.6 43.6 %tile_forward.1 = (f32[3,16,384]{2,1,0:T(8,128)}, f32[3,16,384]{2,1,0:T(8,128)}, f32[24,3,2,8,256]{4,3,2,1,0:T(8,128)}, f32[24,2,8,256]{3,2,1,0:T(8,128)}, bf16[...) custom-call(s32[1,8192]{1,0:T(1,128)} %send.1, f32[2,2048]{1,0:T(2,128)} %centres.1, f32[2,2048]{1,0:T(2,128)} %conic.1, ...), custom_call_target="tpu_custom_call" | custom-call | tf_op jit(solution)/shard_map/tile_forward/pallas_call | solution.py:793
  44.3 0.0 copy-start
  44.3 30.9 %tile_backward.1 = f32[9,2048]{1,0:T(8,128)} custom-call(s32[24,1,512]{2,1,0:T(1,128)} %get-tuple-element.9.lists, bf16[24,512,32]{2,1,0:T(8,128)(2,1)} %get-tuple-element.10.left_in, f32[3,16,384]{2,1,0:T(8,128)} %get-tuple-element.11.grad, f32[24,3,2,8,256]{4,3,2,1,0:T(8,128)} %get-tuple-element.12.chunk_rend, ...), custom_call_target="tpu_custom_call" | custom-call | tf_op jit(solution)/shard_map/tile_backward/pallas_call | solution.py:841
  75.2 0.0 copy-done
  75.2 0.6 copy.12
  75.9 1.6 %copy.13 = f32[9,2048]{1,0:T(8,128)} copy(f32[9,2048]{1,0:T(8,128)} %tile_backward.1) | data formatting | bytes 147456
Async XLA Ops:
  44.3 30.9 %copy-start = (f32[3,16,384]{2,1,0:T(8,128)S(1)}, f32[3,16,384]{2,1,0:T(8,128)}, u32[]{:S(2)}) copy-start(f32[3,16,384]{2,1,0:T(8,128)} %get-tuple-element.16) | copy-start | bytes 221188

commit v11 on v10

--- a/solution.py
+++ b/solution.py
@@ -333,71 +333,66 @@
         rends[ch, pl.ds(tile, 1), :] = sub_sum(sums[0][ch] + sums[1][ch])[0:1, :]
 
 
-def forward_kernel(*refs):
-    sources, target, image, grad, chunk_rend, chunk_start, left_out, lists_out = refs[:7], *refs[7:14]
-    pieces, ninth, flat, cols, alphas, rends, image_too, head, tail, *loss_refs = refs[14:30]
-    recv, lists, strips, *send_refs = refs[30:]
-    step = pl.program_id(0)
+def step_kernel(*refs):
+    sources, target, image, result = refs[:7], *refs[7:10]
+    pieces, ninth, flat, cols, alphas, rends, image_too, head, tail, *loss_refs = refs[10:26]
+    recv, lists, strips, *send_refs = refs[26:44]
+    grad, chunk_rend, chunk_start, left_out, *back_refs = refs[44:]
     me = lax.axis_index("dev")
     n = lax.axis_size("dev")
-
-    @pl.when(step == 0)
-    def _():
-        x, table, own_ninth, *more = send_refs
-        send_owned(me, n, sources, target, recv, strips, x, table, own_ninth, more[:7], lists, *more[7:])
-        lists_out[...] = lists[...]
-
+    x, table, own_ninth, *more = send_refs
+    send_owned(me, n, sources, target, recv, strips, x, table, own_ninth, more[:7], lists, *more[7:])
     row = iota((SUB, LANE), 0)
-
-    @pl.when(step == 0)
-    def _():
-        blocks = pieces.shape[0] // SUB
-        left = iota((SUB, LANE), 1) < 64
-
-        def block(h, carry):
-            lasts = []
-            for half in range(2):
-                owner = 4 * h + 2 * half
-                eight, last = unpack_pair(recv[owner], recv[owner + 1], left, row)
-                pieces[pl.ds(pl.multiple_of(h * SUB, SUB), SUB), half * LANE : (half + 1) * LANE] = eight
-                lasts.append(last)
-            ninth[pl.ds(h, 1), :] = jnp.concatenate(lasts, axis=1)
-            return carry
-
-        lax.fori_loop(0, blocks, block, 0)
-        for rows, source in ((slice(0, blocks * SUB), pieces), (slice(blocks * SUB, None), ninth)):
-            for k, part in enumerate(split2(source[...])):
-                flat[rows, k * 256 : (k + 1) * 256] = part.astype(BF16)
-        for _ in gather_columns(lists[0], flat, cols, 0):
-            pass
-
+    blocks = pieces.shape[0] // SUB
+    left = iota((SUB, LANE), 1) < 64
+
+    def block(h, carry):
+        lasts = []
+        for half in range(2):
+            owner = 4 * h + 2 * half
+            eight, last = unpack_pair(recv[owner], recv[owner + 1], left, row)
+            pieces[pl.ds(pl.multiple_of(h * SUB, SUB), SUB), half * LANE : (half + 1) * LANE] = eight
+            lasts.append(last)
+        ninth[pl.ds(h, 1), :] = jnp.concatenate(lasts, axis=1)
+        return carry
+
+    lax.fori_loop(0, blocks, block, 0)
+    for rows, source in ((slice(0, blocks * SUB), pieces), (slice(blocks * SUB, None), ninth)):
+        for k, part in enumerate(split2(source[...])):
+            flat[rows, k * 256 : (k + 1) * 256] = part.astype(BF16)
+    for _ in gather_columns(lists[0], flat, cols, 0):
+        pass
     basis = stack_rows((basis_rows(256) + [None, None]) * 3, 32).astype(BF16)
-    for slot in range(2):
-        tile = 2 * step + slot
-        later = jnp.minimum(tile + 1, lists.shape[0] - 1)
-        take_turns(
-            TURNS,
-            g=gather_columns(lists[later], flat, cols, 1 - slot),
-            d=draw_tile(slot, tile, basis, chunk_rend, chunk_start, left_out, cols, alphas, rends),
-        )
-
-    @pl.when(step == pl.num_programs(0) - 1)
-    def _():
-        for ch in range(3):
-            for g in range(rends.shape[1] // SUB):
-                for h in range(2):
-                    block = block_transpose(rends[ch, g * SUB : (g + 1) * SUB, h * LANE : (h + 1) * LANE])
-                    span = slice(g * LANE, (g + 1) * LANE)
-                    for to in (image, image_too):
-                        to[ch, h * SUB : (h + 1) * SUB, span] = block
-                    at = RIM * ch
-                    if h == 0:
-                        head[at : at + SUB, span] = block
-                        tail[at : at + 2, span] = block[6:8, :]
-                    else:
-                        head[at + SUB : at + RIM, span] = block[0:2, :]
-                        tail[at + 2 : at + RIM, span] = block
-        loss_gradient(me, n, image_too, head, tail, strips, grad, *loss_refs)
+
+    def forward(step, carry):
+        views = [ref.at[pl.ds(2 * step, 2)] for ref in (chunk_rend, chunk_start, left_out)]
+        for slot in range(2):
+            tile = 2 * step + slot
+            later = jnp.minimum(tile + 1, lists.shape[0] - 1)
+            take_turns(
+                TURNS,
+                g=gather_columns(lists[later], flat, cols, 1 - slot),
+                d=draw_tile(slot, tile, basis, *views, cols, alphas, rends),
+            )
+        return carry
+
+    lax.fori_loop(0, lists.shape[0] // 2, forward, 0)
+    for ch in range(3):
+        for g in range(rends.shape[1] // SUB):
+            for h in range(2):
+                block = block_transpose(rends[ch, g * SUB : (g + 1) * SUB, h * LANE : (h + 1) * LANE])
+                span = slice(g * LANE, (g + 1) * LANE)
+                for to in (image, image_too):
+                    to[ch, h * SUB : (h + 1) * SUB, span] = block
+                at = RIM * ch
+                if h == 0:
+                    head[at : at + SUB, span] = block
+                    tail[at : at + 2, span] = block[6:8, :]
+                else:
+                    head[at + SUB : at + RIM, span] = block[0:2, :]
+                    tail[at + 2 : at + RIM, span] = block
+    loss_gradient(me, n, image_too, head, tail, strips, grad, *loss_refs)
+    shade_all(me, n, lists, left_out, grad, chunk_rend, chunk_start, *more[:5], result, *back_refs)
 
 
 def taps_of():
@@ -681,97 +676,79 @@
     out[6:9, :] = rows[6:9, :]
 
 
-def backward_kernel(
-    lists, left_in, grad, chunk_rend, chunk_start, send, centres, conic, rho, opacity, result,
+def shade_all(
+    me, n, lists, left_in, grad, chunk_rend, chunk_start, send, centres, conic, rho, opacity, result,
     cots, halves, grads, slots, out, back, total, rows, local_sem, send_sem, recv_sem
 ):
-    me = lax.axis_index("dev")
-    n = lax.axis_size("dev")
-    barrier = pltpu.get_barrier_semaphore()
-    each = (n - 1) // (lists.shape[0] // 2)
-
-    def greet(k):
-        pl.semaphore_signal(barrier, inc=1, device_id=(lax.rem(me + k, n),), device_id_type=MESH)
-
-    step = pl.program_id(0)
-    steps = pl.num_programs(0)
-
-    steps_static = lists.shape[0] // 2
-
-    @pl.when(step == 0)
-    def _():
-        for k in range(each * steps_static + 1, n):
-            greet(k)
-        for ch in range(3):
-            for g in range(cots.shape[0] // SUB):
-                for h in range(2):
-                    span = slice(h * LANE, (h + 1) * LANE)
-                    block = block_transpose(grad[ch, h * SUB : (h + 1) * SUB, g * LANE : (g + 1) * LANE])
-                    for t in range(SUB):
-                        cots[g * SUB + t, ch : ch + 1, span] = block[t : t + 1, :]
-
-    for k in range(each):
-        greet(step * each + k + 1)
-    for slot in range(2):
-        tile = 2 * step + slot
-        past = jnp.maximum(tile - 1, 0)
-        take_turns(
-            BACK_TURNS,
-            f=find_moments(1 - slot, past, cots, halves, grads),
-            s=shade_tile(slot, tile, left_in, chunk_rend, chunk_start, cots, halves),
-        )
-
-    @pl.when(step == steps - 1)
-    def _():
-        for _ in find_moments(1, 2 * step + 1, cots, halves, grads):
-            pass
-        slots[...] = jnp.zeros_like(slots)
-        blocks = slots.shape[0] // (SUB + 1)
-        group = 2
-
-        def chunk(c, carry):
-            each = [c * group + k for k in range(group)]
-            idx = jnp.concatenate([jnp.maximum(lists[t], 0) for t in each], axis=1)
-            eight = jnp.concatenate([grads[t, 0:8, :] for t in each], axis=1)
-            ninth = jnp.concatenate([grads[t, 8:9, :] for t in each], axis=1)
-            slots[...] = slots[...] + scatter_block(eight, ninth, idx, blocks)
-            return carry
-
-        lax.fori_loop(0, cots.shape[0] // group, chunk, 0)
-        left = iota((SUB, LANE), 1) < 64
-        row = iota((SUB, LANE), 0)
-        for h in range(blocks):
-            for half in range(2):
-                span = slice(half * LANE, (half + 1) * LANE)
-                acc = slots[h * SUB : (h + 1) * SUB, span]
-                extra = jnp.broadcast_to(slots[blocks * SUB + h : blocks * SUB + h + 1, span], (SUB, LANE))
-                owner = 4 * h + 2 * half
-                out[owner], out[owner + 1] = pack_pair(acc, extra, left, row)
-        pl.semaphore_wait(barrier, n - 1)
-        used = pl.ds(0, USED)
-        own = pltpu.make_async_copy(out.at[me, used], back.at[me, used], local_sem)
-        own.start()
-        pairs = n // 2
-        mine = me // 2
-
-        def ship_to(peer, k):
-            pltpu.make_async_remote_copy(
-                src_ref=out.at[peer, used], dst_ref=back.at[me, used],
-                send_sem=send_sem, recv_sem=recv_sem.at[k // GROUP],
-                device_id=(peer,), device_id_type=MESH,
-            ).start()
-
-        ship_to(me + 1 - 2 * lax.rem(me, 2), 0)
-
-        def ship(k, carry):
-            for core in range(2):
-                ship_to(2 * lax.rem(mine + k, pairs) + core, k)
-            return carry
-
-        lax.fori_loop(1, pairs, ship, 0)
-        gather_home(me, n, back, send, centres, conic, rho, opacity, result, total, rows, own, recv_sem)
-        sent = out.at[pl.ds(0, n - 1), used]
-        pltpu.make_async_copy(sent, sent, send_sem).wait()
+    for ch in range(3):
+        for g in range(cots.shape[0] // SUB):
+            for h in range(2):
+                span = slice(h * LANE, (h + 1) * LANE)
+                block = block_transpose(grad[ch, h * SUB : (h + 1) * SUB, g * LANE : (g + 1) * LANE])
+                for t in range(SUB):
+                    cots[g * SUB + t, ch : ch + 1, span] = block[t : t + 1, :]
+
+    def backward(step, carry):
+        views = [ref.at[pl.ds(2 * step, 2)] for ref in (left_in, chunk_rend, chunk_start)]
+        for slot in range(2):
+            tile = 2 * step + slot
+            past = jnp.maximum(tile - 1, 0)
+            take_turns(
+                BACK_TURNS,
+                f=find_moments(1 - slot, past, cots, halves, grads),
+                s=shade_tile(slot, tile, *views, cots, halves),
+            )
+        return carry
+
+    lax.fori_loop(0, cots.shape[0] // 2, backward, 0)
+    for _ in find_moments(1, cots.shape[0] - 1, cots, halves, grads):
+        pass
+    slots[...] = jnp.zeros_like(slots)
+    blocks = slots.shape[0] // (SUB + 1)
+    group = 6
+
+    def chunk(c, carry):
+        each = [c * group + k for k in range(group)]
+        idx = jnp.concatenate([jnp.maximum(lists[t], 0) for t in each], axis=1)
+        eight = jnp.concatenate([grads[t, 0:8, :] for t in each], axis=1)
+        ninth = jnp.concatenate([grads[t, 8:9, :] for t in each], axis=1)
+        slots[...] = slots[...] + scatter_block(eight, ninth, idx, blocks)
+        return carry
+
+    lax.fori_loop(0, cots.shape[0] // group, chunk, 0)
+    left = iota((SUB, LANE), 1) < 64
+    row = iota((SUB, LANE), 0)
+    for h in range(blocks):
+        for half in range(2):
+            span = slice(half * LANE, (half + 1) * LANE)
+            acc = slots[h * SUB : (h + 1) * SUB, span]
+            extra = jnp.broadcast_to(slots[blocks * SUB + h : blocks * SUB + h + 1, span], (SUB, LANE))
+            owner = 4 * h + 2 * half
+            out[owner], out[owner + 1] = pack_pair(acc, extra, left, row)
+    used = pl.ds(0, USED)
+    own = pltpu.make_async_copy(out.at[me, used], back.at[me, used], local_sem)
+    own.start()
+    pairs = n // 2
+    mine = me // 2
+
+    def ship_to(peer, k):
+        pltpu.make_async_remote_copy(
+            src_ref=out.at[peer, used], dst_ref=back.at[me, used],
+            send_sem=send_sem, recv_sem=recv_sem.at[k // GROUP],
+            device_id=(peer,), device_id_type=MESH,
+        ).start()
+
+    ship_to(me + 1 - 2 * lax.rem(me, 2), 0)
+
+    def ship(k, carry):
+        for core in range(2):
+            ship_to(2 * lax.rem(mine + k, pairs) + core, k)
+        return carry
+
+    lax.fori_loop(1, pairs, ship, 0)
+    gather_home(me, n, back, send, centres, conic, rho, opacity, result, total, rows, own, recv_sem)
+    sent = out.at[pl.ds(0, n - 1), used]
+    pltpu.make_async_copy(sent, sent, send_sem).wait()
 
 
 def struct(*shape, dtype=F32):
@@ -786,26 +763,14 @@
     pixels = height * height
     params = lambda mib: pltpu.CompilerParams(vmem_limit_bytes=mib << 20)
     sources = (send_rows, centres, conic, rho, opacity, colors, tile_lists)
-    whole = lambda *shape: pl.BlockSpec(shape, lambda t: (0,) * len(shape))
     per = 2
-    per_tile = lambda *shape: pl.BlockSpec((per,) + shape, lambda t: (t,) + (0,) * len(shape))
     hi_blocks = devices * 64 // 256
-    image, pixel_grad, chunk_rend, chunk_start, left, lists = pl.pallas_call(
-        forward_kernel,
-        grid=(tiles // per,),
-        in_specs=[pl.BlockSpec(memory_space=pltpu.HBM)] * 8,
-        out_specs=[
-            whole(3, height, width), whole(3, height, width),
-            per_tile(3, 2, SUB, pixels), per_tile(2, SUB, pixels), per_tile(count, 32), whole(tiles, 1, count),
-        ],
-        out_shape=[
-            struct(3, height, width),
-            struct(3, height, width),
-            struct(tiles, 3, 2, SUB, pixels),
-            struct(tiles, 2, SUB, pixels),
-            struct(tiles, count, 32, dtype=BF16),
-            struct(tiles, 1, count, dtype=jnp.int32),
-        ],
+    vmem, hbm = pl.BlockSpec(memory_space=pltpu.VMEM), pl.BlockSpec(memory_space=pltpu.HBM)
+    image, grads = pl.pallas_call(
+        step_kernel,
+        in_specs=[hbm] * 8,
+        out_specs=[vmem] * 2,
+        out_shape=[struct(3, height, width), struct(9, owned)],
         scratch_shapes=[
             pltpu.VMEM((hi_blocks * SUB, 256), F32),
             pltpu.VMEM((hi_blocks, 256), F32),
@@ -833,22 +798,14 @@
         + [pltpu.VMEM(v.shape, v.dtype) for v in sources]
         + [pltpu.SemaphoreType.DMA((8,))]
         + [pltpu.SemaphoreType.DMA] * 2
-        + [pltpu.SemaphoreType.DMA((3,))] * 2,
-        compiler_params=pltpu.CompilerParams(collective_id=0, has_side_effects=True, vmem_limit_bytes=60 * 1024 * 1024),
-        name="tile_forward",
-    )(*sources, target)
-
-    grads = pl.pallas_call(
-        backward_kernel,
-        grid=(tiles // per,),
-        in_specs=[
-            whole(tiles, 1, count), per_tile(count, 32), whole(3, height, width),
-            per_tile(3, 2, SUB, pixels), per_tile(2, SUB, pixels),
+        + [pltpu.SemaphoreType.DMA((3,))] * 2
+        + [
+            pltpu.VMEM((3, height, width), F32),
+            pltpu.VMEM((tiles, 3, 2, SUB, pixels), F32),
+            pltpu.VMEM((tiles, 2, SUB, pixels), F32),
+            pltpu.VMEM((tiles, count, 32), BF16),
         ]
-        + [whole(*v.shape) for v in sources[:5]],
-        out_specs=whole(9, owned),
-        out_shape=struct(9, owned),
-        scratch_shapes=[
+        + [
             pltpu.VMEM((tiles, 3, pixels), F32),
             pltpu.VMEM((per, count, 3 * pixels), BF16),
             pltpu.VMEM((tiles, 16, count), F32),
@@ -861,9 +818,9 @@
             pltpu.SemaphoreType.DMA,
             pltpu.SemaphoreType.DMA((devices // 2 // GROUP,)),
         ],
-        compiler_params=pltpu.CompilerParams(collective_id=1, has_side_effects=True, vmem_limit_bytes=60 * 1024 * 1024),
-        name="tile_backward",
-    )(lists, left, pixel_grad, chunk_rend, chunk_start, *sources[:5])
+        compiler_params=pltpu.CompilerParams(collective_id=0, has_side_effects=True, vmem_limit_bytes=60 * 1024 * 1024),
+        name="training_step",
+    )(*sources, target)
     return image, grads
 
 

time: 77.8 us -> 71.7 us (0.922)
  Pallas kernels: 74.6 us -> 68.8 us
    pallas_call x2 -> x1, Pallas kernels: 74.6 us -> 68.8 us  [shards(): pl.pallas_call(step_kernel, in_specs=[hbm] * 8, out_specs=[vmem] * 2, out...]
where the time goes in v11:
time: 71.7 us; the launch traced here: 71.6 us
  Pallas kernels  68.8 us (96%)
  local copies, waits for them, and re-layouts  2.22 us (3%)
    pallas_call x1, Pallas kernels, shards(): pl.pallas_call(step_kernel, in_specs=[hbm] * 8, out_specs=[vmem] * 2, out...  68.8 us
    unnamed x4, local copies, waits for them, and re-layouts  2.22 us

profile of v11, /device:TPU:1, one launch (start us, length us, event | category | flops | bytes accessed | tf_op | source)
XLA Modules:
  0.0 71.6 jit_solution(1223742906899678258)
XLA Ops:
  0.6 68.8 %training_step.1 = (f32[3,16,384]{2,1,0:T(8,128)}, f32[9,2048]{1,0:T(8,128)}) custom-call(s32[1,8192]{1,0:T(1,128)} %refs_0_.1, f32[2,2048]{1,0:T(2,128)} %refs_1_.1, f32[2,2048]{1,0:T(2,128)} %refs_2_.1, f32[1,2048]{1,0:T(1,128)} %refs_3_.1, f32[1,2048]{1,0:T(1,128)} %refs_4_.1, f32[3,2048]{1,0:T(4,128)} %refs_5_.1, s32[24,512]{1,0:T(8,128)} %refs_6_.1, ...), custom_call_target="tpu_custom_call" | custom-call | tf_op jit(solution)/shard_map/training_step/pallas_call | solution.py:769
  69.4 0.0 copy-start
  69.4 1.6 %copy.12 = f32[3,16,384]{2,1,0:T(8,128)} copy(f32[3,16,384]{2,1,0:T(8,128)} %get-tuple-element.4) | data formatting | bytes 147456
  71.0 0.0 copy-done
  71.0 0.7 copy.13
Async XLA Ops:
  69.4 1.6 %copy-start = (f32[9,2048]{1,0:T(8,128)S(1)}, f32[9,2048]{1,0:T(8,128)}, u32[]{:S(2)}) copy-start(f32[9,2048]{1,0:T(8,128)} %get-tuple-element.5) | copy-start | bytes 221188
